TPU v7x, 128 devices: a whole 4x4x4 slice. The times are simulated.
128 devices in a mesh: group: 2 (over x_lo), lane: 64 (over x_hi, y, z, core).
Axes of the slice: x: 4 (x_hi: 2, x_lo: 2; x = x_hi * 2 + x_lo), y: 4, z: 4, core: 2. Of those that a mesh axis runs over, the one named last changes fastest.
Arguments:
- queries: bfloat16 [8, 768], replicated, may hold values from -6 to 6
- hyper_weight: bfloat16 [768, 589824], P(None, ('group', 'lane')), may hold values from -0.0078125 to 0.0078125
- hyper_bias: bfloat16 [768, 768], P(None, ('group', 'lane')), may hold values from -0.21875 to 0.21875
- documents: bfloat16 [65536, 768], P(('group', 'lane')), may hold values from -6 to 6
- teacher: bfloat16 [65536, 8], P(('group', 'lane')), may hold values from 8 to 24
Outputs:
- doc_grad: bfloat16 [65536, 768], P(('group', 'lane'))
- weight_grad: bfloat16 [768, 589824], P(None, ('group', 'lane'))
- bias_grad: bfloat16 [768, 768], P(None, ('group', 'lane'))
All inputs are finite; a program needn't handle non-finite values.
Results may differ from a plain program's by a relative error of at most 0.024.
The roundings to bfloat16 on the way count: a program that leaves them out, or rounds other values in their place, can miss the bound.
Values may be sent and summed in bfloat16 or wider, within the bound.
No kernel may reach another device: no remote copies, remote signals or barrier semaphores. Data moves between devices by JAX's collectives and lax.ppermute only.
A program may use at most 192 MiB of HBM per device.

v0:
```python
import jax
import jax.numpy as jnp
from jax import lax
from jax.experimental import pallas as pl
from jax.experimental.pallas import tpu as pltpu
from jax.sharding import Mesh
from jax.sharding import PartitionSpec as P


AXES = ("xl", "xh", "y", "z", "c")
PLANE = ("xl", "xh", "y")
RING = ("z", "c")
D = 768
Q = 8
ROWS = 6
CHIPS = 16
CHUNK = 48
DOCS = 512
WIRE = 304
TALL = 128
SCALE = D ** (-0.5)
F32 = jnp.float32
BF16 = jnp.bfloat16
TN = (((0,), (0,)), ((), ()))
NT = (((1,), (1,)), ((), ()))
NN = (((1,), (0,)), ((), ()))


def iota(shape, dim):
    return lax.broadcasted_iota(jnp.int32, shape, dim)


def one_hot(cond):
    return jnp.where(cond, 1.0, 0.0).astype(BF16)


def mm(a, b, dims=NN):
    return lax.dot_general(a, b, dims, preferred_element_type=F32)


def gen_kernel(q_ref, w_ref, hb_ref, t_ref, out_ref, qrep, acc):
    step = pl.program_id(0)
    row = iota((64, Q), 0)
    col = iota((64, Q), 1)
    sub = iota((64, D), 0) % 8

    @pl.when(step == 0)
    def _():
        rep = mm(one_hot(row // 8 == col), q_ref[...])
        qrep[...] = rep.astype(BF16)
        acc[...] = jnp.zeros_like(acc)
        placed = jnp.where(sub == 6, rep, 0.0).astype(BF16)
        acc[:, 0:ROWS] = mm(placed, hb_ref[...], NT)
        acc[:, 0:DOCS] += mm(one_hot(row == col * 8 + 7), t_ref[...])

    q = qrep[...].astype(F32)
    for n in range(2):
        placed = jnp.where(sub == step * 2 + n, q, 0.0).astype(BF16)
        acc[...] += mm(placed, w_ref[:, n * D : (n + 1) * D])

    @pl.when(step == ROWS // 2 - 1)
    def _():
        out_ref[...] = acc[...].astype(BF16)


def generate(queries, weight, bias_t, teacher_t):
    return pl.pallas_call(
        gen_kernel,
        grid=(ROWS // 2,),
        in_specs=[
            pl.BlockSpec((Q, D), lambda i: (0, 0)),
            pl.BlockSpec((D, 2 * D), lambda i: (0, i)),
            pl.BlockSpec((ROWS, D), lambda i: (0, 0)),
            pl.BlockSpec((Q, DOCS), lambda i: (0, 0)),
        ],
        out_specs=pl.BlockSpec((64, D), lambda i: (0, 0)),
        out_shape=jax.ShapeDtypeStruct((64, D), BF16),
        scratch_shapes=[pltpu.VMEM((64, D), BF16), pltpu.VMEM((64, D), F32)],
        compiler_params=pltpu.CompilerParams(dimension_semantics=("arbitrary",)),
        cost_estimate=pl.CostEstimate(flops=2 * 64 * D * D * 6, bytes_accessed=D * D * 12, transcendentals=0),
        name="generate",
    )(queries, weight, bias_t, teacher_t)


def assemble_kernel(src_ref, r_ref, out_ref, tgt_ref):
    r = r_ref[...]
    a, b = iota((CHUNK, 64), 0), iota((CHUNK, 64), 1)
    rows = mm(one_hot((a // 6 == b // 8) & (a % 6 == b % 8)), r).astype(BF16)
    row, lane = iota((64, 128), 0), iota((64, 128), 1)
    l, m = iota((128, 128), 0), iota((128, 128), 1)
    spread = mm(r[:, 0:128], one_hot((m % 6 == l) & (l < 6) & (m < CHUNK)))
    spread = jnp.where((lane // 6 == row // 8) & (row % 8 == 6), spread, 0.0)
    bias = jnp.sum(spread, axis=0, keepdims=True)
    bias = jnp.where(iota((16, 128), 0) == 0, bias, 0.0).astype(BF16)
    for chip in range(CHIPS):
        for rb in range(3):
            for cb in range(6):
                out_ref[chip, (rb * 6 + cb) * 16 : (rb * 6 + cb + 1) * 16, :] = rows[
                    rb * 16 : (rb + 1) * 16, cb * 128 : (cb + 1) * 128
                ]
        out_ref[chip, 288:304, :] = bias
    row8, col8 = iota((64, 8), 0), iota((64, 8), 1)
    pick = jnp.zeros((64, 8), F32)
    for k in range(8):
        pick = jnp.where((col8 == k) & (row8 == src_ref[k] * 8 + 7), 1.0, pick)
    tgt_ref[...] = mm(r[:, 0:DOCS], pick.astype(BF16), TN)


def assemble(src, received):
    return pl.pallas_call(
        assemble_kernel,
        in_specs=[pl.BlockSpec(memory_space=pltpu.SMEM), pl.BlockSpec(memory_space=pltpu.VMEM)],
        out_specs=[pl.BlockSpec(memory_space=pltpu.VMEM)] * 2,
        out_shape=[
            jax.ShapeDtypeStruct((CHIPS, WIRE, 128), BF16),
            jax.ShapeDtypeStruct((DOCS, 8), F32),
        ],
        name="assemble",
    )(src, received)


def main_kernel(tgt_ref, g_ref, *refs):
    docs, outs = refs[:10], refs[10:18]
    lg_ref, dbuf, bbuf, pbuf, layer, bacc, even, odd, in_sem, out_sem = refs[18:]
    half = DOCS // 2

    def block(n, size=DOCS):
        return pl.ds(n * size, size)

    for n in range(4):
        pltpu.make_async_copy(docs[n], dbuf.at[block(n, half)], in_sem.at[n // 2]).start()
    for n in range(2, 8):
        pltpu.make_async_copy(docs[n + 2], dbuf.at[block(n)], in_sem.at[n]).start()

    for chip in range(CHIPS):
        for rb in range(3):
            for cb in range(6):
                layer[
                    chip * CHUNK + rb * 16 : chip * CHUNK + (rb + 1) * 16, cb * 128 : (cb + 1) * 128
                ] = g_ref[chip, (rb * 6 + cb) * 16 : (rb * 6 + cb + 1) * 16, :]
    bacc[...] = jnp.zeros_like(bacc)
    chip_row = iota((CHIPS, 128), 0)
    pieces = jnp.zeros((CHIPS, 128), F32)
    for chip in range(CHIPS):
        piece = g_ref[chip, 288:304, :].astype(F32)[0:1, :]
        pieces = jnp.where(chip_row == chip, piece, pieces)
    l, j = iota((128, D), 0), iota((128, D), 1)
    spread = mm(pieces.astype(BF16), one_hot((j % CHUNK == l) & (l < CHUNK)))
    own = iota((CHIPS, D), 1) // CHUNK == iota((CHIPS, D), 0)
    bias = jnp.sum(jnp.where(own, spread, 0.0), axis=0, keepdims=True)

    steps = 8 * DOCS // half
    slots = (even, odd)

    def product(n):
        if n % 2 == 0:
            landed = dbuf.at[block(n // 2)]
            pltpu.make_async_copy(landed, landed, in_sem.at[n // 2]).wait()
        slots[n % 2][...] = mm(dbuf[block(n, half)], layer[...]) + bias

    def errors_of(n):
        preact = slots[n % 2][...]
        tgt = tgt_ref[block(n % 2, half)]
        tgt = jnp.sum(jnp.where(iota((half, 8), 1) == n // 2, tgt, 0.0), axis=1, keepdims=True)
        scores = jnp.sum(jnp.maximum(preact, 0.0), axis=1, keepdims=True) * SCALE
        back = jnp.where(preact > 0, (scores - tgt) * SCALE, 0.0).astype(BF16)
        bbuf[block(n, half)] = back
        bacc[...] += jnp.sum(back.astype(F32).reshape(-1, 8, D), axis=0)

    product(0)
    for n in range(steps):
        if n + 1 < steps:
            product(n + 1)
        errors_of(n)

    for n in range(4):
        rows = block(n, 2 * DOCS)
        pbuf[rows] = mm(bbuf[rows], layer[...], NT).astype(BF16)
        for k in (2 * n, 2 * n + 1):
            pltpu.make_async_copy(pbuf.at[block(k)], outs[k], out_sem.at[k]).start()

    grad = mm(dbuf[...], bbuf[...], TN).astype(BF16)
    for chip in range(CHIPS):
        for rb in range(3):
            rows = slice(chip * CHUNK + rb * 16, chip * CHUNK + (rb + 1) * 16)
            for cb in range(6):
                lg_ref[chip, (rb * 6 + cb) * 16 : (rb * 6 + cb + 1) * 16, :] = grad[
                    rows, cb * 128 : (cb + 1) * 128
                ]
    total = jnp.sum(bacc[...], axis=0, keepdims=True)
    high = total.astype(BF16)
    low = (total - high.astype(F32)).astype(BF16)
    j, l = iota((D, 128), 0), iota((D, 128), 1)
    fold = one_hot((j % CHUNK == l) & (l < CHUNK))
    high = mm(jnp.where(own, high.astype(F32), 0.0).astype(BF16), fold)
    low = mm(jnp.where(own, low.astype(F32), 0.0).astype(BF16), fold)
    sub = iota((16, 128), 0)
    for chip in range(CHIPS):
        tile = jnp.where(sub == 0, high[chip : chip + 1], jnp.where(sub == 1, low[chip : chip + 1], 0.0))
        lg_ref[chip, 288:304, :] = tile.astype(BF16)
    for n in range(8):
        pltpu.make_async_copy(pbuf.at[block(n)], outs[n], out_sem.at[n]).wait()


def gradients(tgt, gathered, docs):
    hbm = pl.BlockSpec(memory_space=pl.ANY)
    vmem = pl.BlockSpec(memory_space=pltpu.VMEM)
    return pl.pallas_call(
        main_kernel,
        in_specs=[vmem, vmem] + [hbm] * 10,
        out_specs=[hbm] * 8 + [vmem],
        out_shape=[jax.ShapeDtypeStruct((DOCS, D), BF16)] * 8
        + [jax.ShapeDtypeStruct((CHIPS, WIRE, 128), BF16)],
        scratch_shapes=[pltpu.VMEM((8 * DOCS, D), BF16)] * 3
        + [
            pltpu.VMEM((D, D), BF16),
            pltpu.VMEM((8, D), F32),
            pltpu.VMEM((DOCS // 2, D), F32),
            pltpu.VMEM((DOCS // 2, D), F32),
            pltpu.SemaphoreType.DMA((8,)),
            pltpu.SemaphoreType.DMA((8,)),
        ],
        compiler_params=pltpu.CompilerParams(vmem_limit_bytes=60 << 20),
        cost_estimate=pl.CostEstimate(
            flops=6 * 8 * DOCS * D * D, bytes_accessed=32 * DOCS * D, transcendentals=0
        ),
        name="gradients",
    )(tgt, gathered, *docs)


def reduce_kernel(y_ref, out_ref):
    total = y_ref[0].astype(F32)
    for chip in range(1, CHIPS):
        total = total + y_ref[chip].astype(F32)
    rows = jnp.concatenate(
        [
            jnp.concatenate(
                [total[(rb * 6 + cb) * 16 : (rb * 6 + cb + 1) * 16] for cb in range(6)], axis=1
            )
            for rb in range(3)
        ],
        axis=0,
    ).astype(BF16)
    a, b = iota((64, CHUNK), 0), iota((64, CHUNK), 1)
    pieces = mm(one_hot((b // 6 == a // 8) & (b % 6 == a % 8)), rows)
    bias = jnp.sum(total[288:304], axis=0, keepdims=True).astype(BF16).astype(F32)
    row, lane = iota((64, 128), 0), iota((64, 128), 1)
    mine = jnp.where((lane // 6 == row // 8) & (row % 8 == 6) & (lane < CHUNK), bias, 0.0)
    m, l = iota((128, 128), 0), iota((128, 128), 1)
    bias = mm(mine.astype(BF16), one_hot((m % 6 == l) & (l < 6) & (m < CHUNK)))
    out_ref[:, 0:128] = (pieces[:, 0:128] + bias).astype(BF16)
    out_ref[:, 128:] = pieces[:, 128:].astype(BF16)


def reduced(arrived):
    return pl.pallas_call(
        reduce_kernel,
        out_shape=jax.ShapeDtypeStruct((64, D), BF16),
        name="reduced",
    )(arrived)


def weight_kernel(q_ref, r_ref, out_ref, bias_ref):
    row, col = iota((64, Q), 0), iota((64, Q), 1)
    rep = mm(one_hot(row // 8 == col), q_ref[...])
    sub = iota((64, TALL), 0) % 8
    for n in range(ROWS):
        placed = jnp.where(sub == n, rep, 0.0).astype(BF16)
        out_ref[:, n * D : (n + 1) * D] = mm(placed, r_ref[...], TN).astype(BF16)
    placed = jnp.where(sub == 6, rep, 0.0).astype(BF16)
    bias_ref[...] = mm(r_ref[:, 0:128], placed, TN)[0:ROWS].astype(BF16)


def weight_gradients(queries, received):
    return pl.pallas_call(
        weight_kernel,
        grid=(D // TALL,),
        in_specs=[
            pl.BlockSpec((Q, TALL), lambda i: (0, i)),
            pl.BlockSpec((64, D), lambda i: (0, 0)),
        ],
        out_specs=[
            pl.BlockSpec((TALL, ROWS * D), lambda i: (i, 0)),
            pl.BlockSpec((ROWS, TALL), lambda i: (0, i)),
        ],
        out_shape=[
            jax.ShapeDtypeStruct((D, ROWS * D), BF16),
            jax.ShapeDtypeStruct((ROWS, D), BF16),
        ],
        compiler_params=pltpu.CompilerParams(dimension_semantics=("arbitrary",)),
        cost_estimate=pl.CostEstimate(
            flops=2 * 64 * D * D * 6, bytes_accessed=D * D * 12, transcendentals=0
        ),
        name="weight_gradients",
    )(queries, received)


def up(a):
    return lax.ppermute(a, "z", [(i, (i + 1) % 4) for i in range(4)])


def down(a):
    return lax.ppermute(a, "z", [(i, (i + 3) % 4) for i in range(4)])


def swap(a):
    return lax.ppermute(a, "c", [(0, 1), (1, 0)])


def exchange(a, axes):
    return lax.all_to_all(a, axes, split_axis=0, concat_axis=0, tiled=True)


def add(*arrays):
    return sum(a.astype(F32) for a in arrays).astype(BF16)


def step(queries, hyper_weight, hyper_bias, documents, teacher):
    half = DOCS // 2
    z, c = lax.axis_index("z"), lax.axis_index("c")
    generated = generate(queries, hyper_weight, hyper_bias.T, teacher.T)
    documents, generated = lax.optimization_barrier((documents, generated))
    below = up(documents)
    above = down(documents)
    far = (up(below[:half]), down(above[half:]))
    docs = [far[0], far[1], swap(far[0]), swap(far[1])]
    for mine in (below, above, documents):
        docs += [mine, swap(mine)]
    pieces = exchange(generated, RING)
    src = jnp.stack(
        [((z + dz) % 4) * 2 + core for dz in (2, 3, 1, 0) for core in (c, 1 - c)]
    ).astype(jnp.int32)
    chunk, targets = assemble(src, pieces)
    gathered = exchange(chunk, PLANE)
    *parts, layer_grad = gradients(targets, gathered, docs)
    arrived = exchange(layer_grad, PLANE)
    pieces = exchange(reduced(arrived), RING)
    far, below, above, own = parts[0::2]
    for_far, for_below, for_above, for_own = (swap(a) for a in parts[1::2])
    from_below = up(add(far[:half], for_far[:half]))
    from_above = down(add(far[half:], for_far[half:]))
    to_above = jnp.concatenate(
        [add(above[:half], for_above[:half], from_below), add(above[half:], for_above[half:])]
    )
    to_below = jnp.concatenate(
        [add(below[:half], for_below[:half]), add(below[half:], for_below[half:], from_above)]
    )
    from_below = up(to_above)
    from_above = down(to_below)
    doc_grad = add(own, for_own, from_below, from_above)
    doc_grad, pieces = lax.optimization_barrier((doc_grad, pieces))
    weight_grad, bias_grad = weight_gradients(queries, pieces)
    return doc_grad, weight_grad, bias_grad.T


def solution(mesh):
    torus = Mesh(mesh.devices.reshape(2, 2, 4, 4, 2), AXES)
    in_specs = (P(), P(None, AXES), P(None, AXES), P(AXES, None), P(AXES, None))
    out_specs = (P(AXES, None), P(None, AXES), P(None, AXES))
    return jax.shard_map(step, mesh=torus, in_specs=in_specs, out_specs=out_specs, check_vma=False)
```

profile of v0, /device:TPU:24, one launch (start us, length us, event | category | flops | bytes accessed | tf_op | source)
XLA Modules:
  0.0 135.0 jit_solution(2861086403029514161)
XLA Ops:
  0.6 5.4 %generate.1 = bf16[64,768]{1,0:T(8,128)(2,1)} custom-call(bf16[8,768]{1,0:T(8,128)(2,1)} %q_ref.3, bf16[768,4608]{1,0:T(8,128)(2,1)} %w_ref.1, bf16[6,768]{1,0:T(8,128)(2,1)} %bitcast.19, bf16[8,512]{1,0:T(8,128)(2,1)} %bitcast.20), custom_call_target="tpu_custom_call" | custom-call | flops 452984832 | bytes 7077888 | tf_op jit(solution)/shard_map/generate/pallas_call | solution.py:67
  6.0 4.0 %collective-permute-start.2 = (bf16[512,768]{1,0:T(8,128)(2,1)}, bf16[512,768]{1,0:T(8,128)(2,1)S(1)}, u32[]{:S(2)}, u32[]{:S(2)}) collective-permute-start(bf16[512,768]{1,0:T(8,128)(2,1)} %refs_8_), channel_id=1, source_target_pairs={{0,6},{2,0},{4,2},{6,4},{1,7},{3,1},{5,3},{7,5},{8,14},{10,8},{12,... | collective-permute-start | bytes 2359304 | tf_op jit(solution)/shard_map/ppermute | solution.py:303
  10.1 0.0 collective-permute-start
  10.1 4.5 %all-to-all-start = ((bf16[8,8,768]{2,1,0:T(8,128)(2,1)}), bf16[8,8,768]{2,1,0:T(8,128)(2,1)S(1)}, u32[]{:S(2)}, u32[]{:S(2)}) async-start(bf16[8,8,768]{2,1,0:T(8,128)(2,1)} %bitcast.15), calls=%async_computation | async-start | bytes 196608 | tf_op jit(solution)/shard_map/all_to_all | solution.py:311
  14.6 0.6 stack.35.src_ref
  15.2 16.3 %all-to-all-done = bf16[8,8,768]{2,1,0:T(8,128)(2,1)S(1)} async-done(((bf16[8,8,768]{2,1,0:T(8,128)(2,1)}), bf16[8,8,768]{2,1,0:T(8,128)(2,1)S(1)}, u32[]{:S(2)}, u32[]{:S(2)}) %all-to-all-start) | async-done | bytes 98336 | tf_op jit(solution)/shard_map/all_to_all | solution.py:311
  31.5 0.6 copy-done.4
  32.2 2.3 %assemble.1 = (bf16[16,304,128]{2,1,0:T(8,128)(2,1)}, f32[512,8]{1,0:T(8,128)}) custom-call(s32[8]{0:T(128)} %stack.35.src_ref, bf16[64,768]{1,0:T(8,128)(2,1)} %bitcast.16), custom_call_target="tpu_custom_call" | custom-call | tf_op jit(solution)/shard_map/assemble/pallas_call | solution.py:110
  34.4 7.2 %all-to-all-start.1 = ((bf16[16,304,128]{2,1,0:T(8,128)(2,1)}), bf16[16,304,128]{2,1,0:T(8,128)(2,1)S(1)}, u32[]{:S(2)}, u32[]{:S(2)}) async-start(bf16[16,304,128]{2,1,0:T(8,128)(2,1)} %get-tuple-element.22), calls=%async_computation.1 | async-start | bytes 2490368 | tf_op jit(solution)/shard_map/all_to_all | solution.py:311
  41.6 0.0 collective-permute-start.8
  41.6 0.0 collective-permute-done.2.refs_6_
  41.6 0.0 copy-start.5
  41.7 0.3 collective-permute-start.3
  42.0 0.0 collective-permute-done.refs_4_
  42.1 1.8 %collective-permute-start.1 = (bf16[256,768]{1,0:T(8,128)(2,1)S(1)}, bf16[256,768]{1,0:T(8,128)(2,1)}, u32[]{:S(2)}, u32[]{:S(2)}) collective-permute-start(bf16[256,768]{1,0:T(8,128)(2,1)S(1)} %slice.56), channel_id=1, source_target_pairs={{0,2},{2,4},{4,6},{6,0},{1,3},{3,5},{5,7},{7,1},{8,10},{10,12},{12... | collective-permute-start | bytes 1179656 | tf_op jit(solution)/shard_map/ppermute | solution.py:299
  43.9 0.0 collective-permute-start.7
  43.9 0.5 collective-permute-start.6
  44.4 8.9 %collective-permute-done.3.refs_1_ = bf16[256,768]{1,0:T(8,128)(2,1)S(1)} collective-permute-done((bf16[256,768]{1,0:T(8,128)(2,1)S(1)}, bf16[256,768]{1,0:T(8,128)(2,1)S(1)}, u32[]{:S(2)}, u32[]{:S(2)}) %collective-permute-start.3) | collective-permute-done | bytes 393248 | tf_op jit(solution)/shard_map/ppermute | solution.py:303
  53.2 0.0 collective-permute-start.5
  53.2 1.5 %collective-permute-done.1.refs_0_ = bf16[256,768]{1,0:T(8,128)(2,1)} collective-permute-done((bf16[256,768]{1,0:T(8,128)(2,1)S(1)}, bf16[256,768]{1,0:T(8,128)(2,1)}, u32[]{:S(2)}, u32[]{:S(2)}) %collective-permute-start.1) | collective-permute-done | bytes 393248 | tf_op jit(solution)/shard_map/ppermute | solution.py:299
  54.7 0.0 collective-permute-start.4
  54.7 0.0 collective-permute-done.8.refs_9_
  54.7 3.8 %all-to-all-done.1.g_ref = bf16[16,304,128]{2,1,0:T(8,128)(2,1)S(1)} async-done(((bf16[16,304,128]{2,1,0:T(8,128)(2,1)}), bf16[16,304,128]{2,1,0:T(8,128)(2,1)S(1)}, u32[]{:S(2)}, u32[]{:S(2)}) %all-to-all-start.1) | async-done | bytes 1245216 | tf_op jit(solution)/shard_map/all_to_all | solution.py:311
  58.5 0.0 collective-permute-done.5.refs_3_
  58.6 0.0 collective-permute-done.7.refs_7_
  58.6 0.0 collective-permute-done.4.refs_2_
  58.6 0.0 collective-permute-done.6.refs_5_
  58.6 0.0 copy-done.5
  58.6 0.0 copy-done.6
  58.6 0.0 copy-done.8
  58.6 1.0 copy-done.1
  59.6 21.0 %gradients.1 = (bf16[512,768]{1,0:T(8,128)(2,1)}, bf16[512,768]{1,0:T(8,128)(2,1)}, bf16[512,768]{1,0:T(8,128)(2,1)}, bf16[512,768]{1,0:T(8,128)(2,1)}, bf16[512...) custom-call(f32[512,8]{1,0:T(8,128)} %get-tuple-element.21.tgt_ref, ...), custom_call_target="tpu_custom_call" | custom-call | flops 14495514624 | bytes 12582912 | tf_op jit(solution)/shard_map/gradients/pallas_call | solution.py:208
  80.6 0.1 collective-permute-start.11
  80.7 0.5 collective-permute-start.10
  81.2 2.0 %collective-permute-done.11 = bf16[512,768]{1,0:T(8,128)(2,1)S(1)} collective-permute-done((bf16[512,768]{1,0:T(8,128)(2,1)}, bf16[512,768]{1,0:T(8,128)(2,1)S(1)}, u32[]{:S(2)}, u32[]{:S(2)}) %collective-permute-start.11) | collective-permute-done | bytes 786464 | tf_op jit(solution)/shard_map/ppermute | solution.py:307
  83.1 2.0 %add_convert_fusion.6 = (bf16[256,768]{1,0:T(8,128)(2,1)}, bf16[256,768]{1,0:T(8,128)(2,1)S(1)}) fusion(bf16[512,768]{1,0:T(8,128)(2,1)S(1)} %collective-permute-done.11, bf16[512,768]{1,0:T(8,128)(2,1)} %get-tuple-element.28), kind=kLoop, calls=%fused_computation.8 | loop fusion | flops 1572864 | bytes 2359296 | tf_op jit(solution)/shard_map/convert_element_type | solution.py:315
  85.2 0.0 collective-permute-start.12
  85.2 0.1 collective-permute-start.14
  85.3 6.0 %all-to-all-start.2 = ((bf16[16,304,128]{2,1,0:T(8,128)(2,1)}), bf16[16,304,128]{2,1,0:T(8,128)(2,1)S(1)}, u32[]{:S(2)}, u32[]{:S(2)}) async-start(bf16[16,304,128]{2,1,0:T(8,128)(2,1)} %get-tuple-element.32), calls=%async_computation.2 | async-start | bytes 2490368 | tf_op jit(solution)/shard_map/all_to_all | solution.py:311
  91.3 0.0 collective-permute-start.9
  91.4 3.0 %collective-permute-start.15 = (bf16[256,768]{1,0:T(8,128)(2,1)S(1)}, bf16[256,768]{1,0:T(8,128)(2,1)S(1)}, u32[]{:S(2)}, u32[]{:S(2)}) collective-permute-start(bf16[256,768]{1,0:T(8,128)(2,1)S(1)} %get-tuple-element.40), channel_id=1, source_target_pairs={{0,6},{2,0},{4,2},{6,4},{1,7},{3,1},{5,3},{7,5},{8,14},{10,8},{12,... | collective-permute-start | bytes 1179656 | tf_op jit(solution)/shard_map/ppermute | solution.py:303
  94.4 0.0 collective-permute-done.10
  94.4 3.5 %collective-permute-done.12 = bf16[256,768]{1,0:T(8,128)(2,1)} collective-permute-done((bf16[256,768]{1,0:T(8,128)(2,1)}, bf16[256,768]{1,0:T(8,128)(2,1)}, u32[]{:S(2)}, u32[]{:S(2)}) %collective-permute-start.12) | collective-permute-done | bytes 393248 | tf_op jit(solution)/shard_map/ppermute | solution.py:299
  97.9 0.0 copy-done.3
  97.9 1.5 %add_convert_fusion.5 = (bf16[256,768]{1,0:T(8,128)(2,1)S(1)}, bf16[256,768]{1,0:T(8,128)(2,1)S(1)}) fusion(bf16[256,768]{1,0:T(8,128)(2,1)} %collective-permute-done.12, bf16[512,768]{1,0:T(8,128)(2,1)} %collective-permute-done.10, bf16[512,768]{1,0:T(8,128)(2,1)S(1)} %copy-done.3), kind=kLoop, calls=%fused_computation.7 | loop fusion | flops 1966080 | bytes 2752512 | tf_op jit(solution)/shard_map/convert_element_type | solution.py:315
  99.4 0.1 pad_maximum_fusion
  99.5 0.1 collective-permute-start.13
  99.6 0.0 collective-permute-done.14
  99.6 3.8 %collective-permute-done.15 = bf16[256,768]{1,0:T(8,128)(2,1)S(1)} collective-permute-done((bf16[256,768]{1,0:T(8,128)(2,1)S(1)}, bf16[256,768]{1,0:T(8,128)(2,1)S(1)}, u32[]{:S(2)}, u32[]{:S(2)}) %collective-permute-start.15) | collective-permute-done | bytes 393248 | tf_op jit(solution)/shard_map/ppermute | solution.py:303
  103.4 0.0 copy-done.2
  103.4 0.2 add_convert_fusion.3
  103.6 0.1 pad_maximum_fusion.1
  103.7 3.8 %collective-permute-start.16 = (bf16[512,768]{1,0:T(8,128)(2,1)S(1)}, bf16[512,768]{1,0:T(8,128)(2,1)}, u32[]{:S(2)}, u32[]{:S(2)}) collective-permute-start(bf16[512,768]{1,0:T(8,128)(2,1)S(1)} %pad_maximum_fusion.1), channel_id=1, source_target_pairs={{0,6},{2,0},{4,2},{6,4},{1,7},{3,1},{5,3},{7,5},{8,14},{10,8},{12,... | collective-permute-start | bytes 2359304 | tf_op jit(solution)/shard_map/ppermute | solution.py:303
  107.4 1.3 all-to-all-done.2.y_ref
  108.7 1.0 copy-done
  109.8 2.2 %reduced.1 = bf16[64,768]{1,0:T(8,128)(2,1)} custom-call(bf16[16,304,128]{2,1,0:T(8,128)(2,1)} %copy-done), custom_call_target="tpu_custom_call" | custom-call | tf_op jit(solution)/shard_map/reduced/pallas_call | solution.py:256
  112.0 4.7 %all-to-all-start.3 = ((bf16[8,8,768]{2,1,0:T(8,128)(2,1)}), bf16[8,8,768]{2,1,0:T(8,128)(2,1)S(1)}, u32[]{:S(2)}, u32[]{:S(2)}) async-start(bf16[8,8,768]{2,1,0:T(8,128)(2,1)} %bitcast.17), calls=%async_computation.3 | async-start | bytes 196608 | tf_op jit(solution)/shard_map/all_to_all | solution.py:311
  116.7 0.0 collective-permute-done.9
  116.7 2.9 %collective-permute-done.13 = bf16[512,768]{1,0:T(8,128)(2,1)} collective-permute-done((bf16[512,768]{1,0:T(8,128)(2,1)S(1)}, bf16[512,768]{1,0:T(8,128)(2,1)}, u32[]{:S(2)}, u32[]{:S(2)}) %collective-permute-start.13) | collective-permute-done | bytes 786464 | tf_op jit(solution)/shard_map/ppermute | solution.py:299
  119.6 5.2 %collective-permute-done.16 = bf16[512,768]{1,0:T(8,128)(2,1)} collective-permute-done((bf16[512,768]{1,0:T(8,128)(2,1)S(1)}, bf16[512,768]{1,0:T(8,128)(2,1)}, u32[]{:S(2)}, u32[]{:S(2)}) %collective-permute-start.16) | collective-permute-done | bytes 786464 | tf_op jit(solution)/shard_map/ppermute | solution.py:303
  124.8 3.1 %add_convert_fusion = bf16[512,768]{1,0:T(8,128)(2,1)} fusion(bf16[512,768]{1,0:T(8,128)(2,1)} %collective-permute-done.16, bf16[512,768]{1,0:T(8,128)(2,1)} %collective-permute-done.13, bf16[512,768]{1,0:T(8,128)(2,1)} %collective-permute-done.9, bf16[512,768]{1,0:T(8,128)(2,1)} %get-tuple-element.24), kind=kLoop, calls=%fused_computation | loop fusion | flops 3145728 | bytes 3932160 | tf_op jit(solution)/shard_map/convert_element_type | solution.py:315
  127.9 0.0 all-to-all-done.3
  127.9 0.6 copy-done.7
  128.5 6.5 %weight_gradients.1 = (bf16[768,4608]{1,0:T(8,128)(2,1)}, bf16[6,768]{1,0:T(8,128)(2,1)}) custom-call(bf16[8,768]{1,0:T(8,128)(2,1)} %q_ref.3, bf16[64,768]{1,0:T(8,128)(2,1)} %bitcast.18), custom_call_target="tpu_custom_call" | custom-call | flops 452984832 | bytes 7077888 | tf_op jit(solution)/shard_map/weight_gradients/pallas_call | solution.py:275
  (10 shorter events, 0.1 us)
Async XLA Ops:
  6.0 35.6 %collective-permute-start.2 = (bf16[512,768]{1,0:T(8,128)(2,1)}, bf16[512,768]{1,0:T(8,128)(2,1)S(1)}, u32[]{:S(2)}, u32[]{:S(2)}) collective-permute-start(bf16[512,768]{1,0:T(8,128)(2,1)} %refs_8_), channel_id=1, source_target_pairs={{0,6},{2,0},{4,2},{6,4},{1,7},{3,1},{5,3},{7,5},{8,14},{10,8},{12,... | collective-permute-start | bytes 2359304 | tf_op jit(solution)/shard_map/ppermute | solution.py:303
  10.1 32.0 %collective-permute-start = (bf16[512,768]{1,0:T(8,128)(2,1)}, bf16[512,768]{1,0:T(8,128)(2,1)S(1)}, u32[]{:S(2)}, u32[]{:S(2)}) collective-permute-start(bf16[512,768]{1,0:T(8,128)(2,1)} %refs_8_), channel_id=1, source_target_pairs={{0,2},{2,4},{4,6},{6,0},{1,3},{3,5},{5,7},{7,1},{8,10},{10,12},{12... | collective-permute-start | bytes 2359304 | tf_op jit(solution)/shard_map/ppermute | solution.py:299
  10.1 21.5 %all-to-all-start = ((bf16[8,8,768]{2,1,0:T(8,128)(2,1)}), bf16[8,8,768]{2,1,0:T(8,128)(2,1)S(1)}, u32[]{:S(2)}, u32[]{:S(2)}) async-start(bf16[8,8,768]{2,1,0:T(8,128)(2,1)} %bitcast.15), calls=%async_computation | async-start | bytes 196608 | tf_op jit(solution)/shard_map/all_to_all | solution.py:311
  31.5 0.6 copy-start.4
  34.4 24.1 %all-to-all-start.1 = ((bf16[16,304,128]{2,1,0:T(8,128)(2,1)}), bf16[16,304,128]{2,1,0:T(8,128)(2,1)S(1)}, u32[]{:S(2)}, u32[]{:S(2)}) async-start(bf16[16,304,128]{2,1,0:T(8,128)(2,1)} %get-tuple-element.22), calls=%async_computation.1 | async-start | bytes 2490368 | tf_op jit(solution)/shard_map/all_to_all | solution.py:311
  41.6 13.1 %collective-permute-start.8 = (bf16[512,768]{1,0:T(8,128)(2,1)}, bf16[512,768]{1,0:T(8,128)(2,1)}, u32[]{:S(2)}, u32[]{:S(2)}) collective-permute-start(bf16[512,768]{1,0:T(8,128)(2,1)} %refs_8_), channel_id=1, source_target_pairs={{0,1},{1,0},{2,3},{3,2},{4,5},{5,4},{6,7},{7,6},{8,9},{9,8},{10,11... | collective-permute-start | bytes 2359304 | tf_op jit(solution)/shard_map/ppermute | solution.py:307
  41.6 17.0 %copy-start.5 = (bf16[512,768]{1,0:T(8,128)(2,1)}, bf16[512,768]{1,0:T(8,128)(2,1)S(1)}, u32[]{:S(2)}) copy-start(bf16[512,768]{1,0:T(8,128)(2,1)S(1)} %collective-permute-done.2.refs_6_) | copy-start | bytes 2359300
  41.7 11.6 %collective-permute-start.3 = (bf16[256,768]{1,0:T(8,128)(2,1)S(1)}, bf16[256,768]{1,0:T(8,128)(2,1)S(1)}, u32[]{:S(2)}, u32[]{:S(2)}) collective-permute-start(bf16[256,768]{1,0:T(8,128)(2,1)S(1)} %slice.57), channel_id=1, source_target_pairs={{0,6},{2,0},{4,2},{6,4},{1,7},{3,1},{5,3},{7,5},{8,14},{10,8},{12,... | collective-permute-start | bytes 1179656 | tf_op jit(solution)/shard_map/ppermute | solution.py:303
  42.0 16.6 %copy-start.6 = (bf16[512,768]{1,0:T(8,128)(2,1)}, bf16[512,768]{1,0:T(8,128)(2,1)S(1)}, u32[]{:S(2)}) copy-start(bf16[512,768]{1,0:T(8,128)(2,1)S(1)} %collective-permute-done.refs_4_) | copy-start | bytes 2359300
  42.1 12.6 %collective-permute-start.1 = (bf16[256,768]{1,0:T(8,128)(2,1)S(1)}, bf16[256,768]{1,0:T(8,128)(2,1)}, u32[]{:S(2)}, u32[]{:S(2)}) collective-permute-start(bf16[256,768]{1,0:T(8,128)(2,1)S(1)} %slice.56), channel_id=1, source_target_pairs={{0,2},{2,4},{4,6},{6,0},{1,3},{3,5},{5,7},{7,1},{8,10},{10,12},{12... | collective-permute-start | bytes 1179656 | tf_op jit(solution)/shard_map/ppermute | solution.py:299
  43.9 14.7 %collective-permute-start.7 = (bf16[512,768]{1,0:T(8,128)(2,1)S(1)}, bf16[512,768]{1,0:T(8,128)(2,1)}, u32[]{:S(2)}, u32[]{:S(2)}) collective-permute-start(bf16[512,768]{1,0:T(8,128)(2,1)S(1)} %collective-permute-done.2.refs_6_), channel_id=1, source_target_pairs={{0,1},{1,0},{2,3},{3,2},{4,5},{5,4},{6,7},{7,6},{8,9},{9,8},{10,11... | collective-permute-start | bytes 2359304 | tf_op jit(solution)/shard_map/ppermute | solution.py:307
  43.9 14.7 %collective-permute-start.6 = (bf16[512,768]{1,0:T(8,128)(2,1)S(1)}, bf16[512,768]{1,0:T(8,128)(2,1)}, u32[]{:S(2)}, u32[]{:S(2)}) collective-permute-start(bf16[512,768]{1,0:T(8,128)(2,1)S(1)} %collective-permute-done.refs_4_), channel_id=1, source_target_pairs={{0,1},{1,0},{2,3},{3,2},{4,5},{5,4},{6,7},{7,6},{8,9},{9,8},{10,11... | collective-permute-start | bytes 2359304 | tf_op jit(solution)/shard_map/ppermute | solution.py:307
  53.2 5.4 %copy-start.8 = (bf16[256,768]{1,0:T(8,128)(2,1)}, bf16[256,768]{1,0:T(8,128)(2,1)S(1)}, u32[]{:S(2)}) copy-start(bf16[256,768]{1,0:T(8,128)(2,1)S(1)} %collective-permute-done.3.refs_1_) | copy-start | bytes 1179652
  53.2 5.3 %collective-permute-start.5 = (bf16[256,768]{1,0:T(8,128)(2,1)S(1)}, bf16[256,768]{1,0:T(8,128)(2,1)}, u32[]{:S(2)}, u32[]{:S(2)}) collective-permute-start(bf16[256,768]{1,0:T(8,128)(2,1)S(1)} %collective-permute-done.3.refs_1_), channel_id=1, source_target_pairs={{0,1},{1,0},{2,3},{3,2},{4,5},{5,4},{6,7},{7,6},{8,9},{9,8},{10,11... | collective-permute-start | bytes 1179656 | tf_op jit(solution)/shard_map/ppermute | solution.py:307
  54.7 3.9 %collective-permute-start.4 = (bf16[256,768]{1,0:T(8,128)(2,1)}, bf16[256,768]{1,0:T(8,128)(2,1)}, u32[]{:S(2)}, u32[]{:S(2)}) collective-permute-start(bf16[256,768]{1,0:T(8,128)(2,1)} %collective-permute-done.1.refs_0_), channel_id=1, source_target_pairs={{0,1},{1,0},{2,3},{3,2},{4,5},{5,4},{6,7},{7,6},{8,9},{9,8},{10,11... | collective-permute-start | bytes 1179656 | tf_op jit(solution)/shard_map/ppermute | solution.py:307
  58.5 1.0 copy-start.1
  80.6 2.6 %collective-permute-start.11 = (bf16[512,768]{1,0:T(8,128)(2,1)}, bf16[512,768]{1,0:T(8,128)(2,1)S(1)}, u32[]{:S(2)}, u32[]{:S(2)}) collective-permute-start(bf16[512,768]{1,0:T(8,128)(2,1)} %get-tuple-element.29), channel_id=1, source_target_pairs={{0,1},{1,0},{2,3},{3,2},{4,5},{5,4},{6,7},{7,6},{8,9},{9,8},{10,11... | collective-permute-start | bytes 2359304 | tf_op jit(solution)/shard_map/ppermute | solution.py:307
  80.7 13.7 %collective-permute-start.10 = (bf16[512,768]{1,0:T(8,128)(2,1)}, bf16[512,768]{1,0:T(8,128)(2,1)}, u32[]{:S(2)}, u32[]{:S(2)}) collective-permute-start(bf16[512,768]{1,0:T(8,128)(2,1)} %get-tuple-element.27), channel_id=1, source_target_pairs={{0,1},{1,0},{2,3},{3,2},{4,5},{5,4},{6,7},{7,6},{8,9},{9,8},{10,11... | collective-permute-start | bytes 2359304 | tf_op jit(solution)/shard_map/ppermute | solution.py:307
  85.2 12.7 %copy-start.3 = (bf16[512,768]{1,0:T(8,128)(2,1)S(1)}, bf16[512,768]{1,0:T(8,128)(2,1)}, u32[]{:S(2)}) copy-start(bf16[512,768]{1,0:T(8,128)(2,1)} %get-tuple-element.26) | copy-start | bytes 2359300
  85.2 12.7 %collective-permute-start.12 = (bf16[256,768]{1,0:T(8,128)(2,1)}, bf16[256,768]{1,0:T(8,128)(2,1)}, u32[]{:S(2)}, u32[]{:S(2)}) collective-permute-start(bf16[256,768]{1,0:T(8,128)(2,1)} %get-tuple-element.39), channel_id=1, source_target_pairs={{0,2},{2,4},{4,6},{6,0},{1,3},{3,5},{5,7},{7,1},{8,10},{10,12},{12... | collective-permute-start | bytes 1179656 | tf_op jit(solution)/shard_map/ppermute | solution.py:299
  85.2 14.4 %collective-permute-start.14 = (bf16[512,768]{1,0:T(8,128)(2,1)}, bf16[512,768]{1,0:T(8,128)(2,1)S(1)}, u32[]{:S(2)}, u32[]{:S(2)}) collective-permute-start(bf16[512,768]{1,0:T(8,128)(2,1)} %get-tuple-element.31), channel_id=1, source_target_pairs={{0,1},{1,0},{2,3},{3,2},{4,5},{5,4},{6,7},{7,6},{8,9},{9,8},{10,11... | collective-permute-start | bytes 2359304 | tf_op jit(solution)/shard_map/ppermute | solution.py:307
  85.3 23.4 %all-to-all-start.2 = ((bf16[16,304,128]{2,1,0:T(8,128)(2,1)}), bf16[16,304,128]{2,1,0:T(8,128)(2,1)S(1)}, u32[]{:S(2)}, u32[]{:S(2)}) async-start(bf16[16,304,128]{2,1,0:T(8,128)(2,1)} %get-tuple-element.32), calls=%async_computation.2 | async-start | bytes 2490368 | tf_op jit(solution)/shard_map/all_to_all | solution.py:311
  91.3 25.4 %collective-permute-start.9 = (bf16[512,768]{1,0:T(8,128)(2,1)}, bf16[512,768]{1,0:T(8,128)(2,1)}, u32[]{:S(2)}, u32[]{:S(2)}) collective-permute-start(bf16[512,768]{1,0:T(8,128)(2,1)} %get-tuple-element.25), channel_id=1, source_target_pairs={{0,1},{1,0},{2,3},{3,2},{4,5},{5,4},{6,7},{7,6},{8,9},{9,8},{10,11... | collective-permute-start | bytes 2359304 | tf_op jit(solution)/shard_map/ppermute | solution.py:307
  91.4 12.0 %collective-permute-start.15 = (bf16[256,768]{1,0:T(8,128)(2,1)S(1)}, bf16[256,768]{1,0:T(8,128)(2,1)S(1)}, u32[]{:S(2)}, u32[]{:S(2)}) collective-permute-start(bf16[256,768]{1,0:T(8,128)(2,1)S(1)} %get-tuple-element.40), channel_id=1, source_target_pairs={{0,6},{2,0},{4,2},{6,4},{1,7},{3,1},{5,3},{7,5},{8,14},{10,8},{12,... | collective-permute-start | bytes 1179656 | tf_op jit(solution)/shard_map/ppermute | solution.py:303
  97.9 5.5 %copy-start.2 = (bf16[512,768]{1,0:T(8,128)(2,1)S(1)}, bf16[512,768]{1,0:T(8,128)(2,1)}, u32[]{:S(2)}) copy-start(bf16[512,768]{1,0:T(8,128)(2,1)} %get-tuple-element.30) | copy-start | bytes 2359300
  99.5 20.1 %collective-permute-start.13 = (bf16[512,768]{1,0:T(8,128)(2,1)S(1)}, bf16[512,768]{1,0:T(8,128)(2,1)}, u32[]{:S(2)}, u32[]{:S(2)}) collective-permute-start(bf16[512,768]{1,0:T(8,128)(2,1)S(1)} %pad_maximum_fusion), channel_id=1, source_target_pairs={{0,2},{2,4},{4,6},{6,0},{1,3},{3,5},{5,7},{7,1},{8,10},{10,12},{12... | collective-permute-start | bytes 2359304 | tf_op jit(solution)/shard_map/ppermute | solution.py:299
  103.7 21.1 %collective-permute-start.16 = (bf16[512,768]{1,0:T(8,128)(2,1)S(1)}, bf16[512,768]{1,0:T(8,128)(2,1)}, u32[]{:S(2)}, u32[]{:S(2)}) collective-permute-start(bf16[512,768]{1,0:T(8,128)(2,1)S(1)} %pad_maximum_fusion.1), channel_id=1, source_target_pairs={{0,6},{2,0},{4,2},{6,4},{1,7},{3,1},{5,3},{7,5},{8,14},{10,8},{12,... | collective-permute-start | bytes 2359304 | tf_op jit(solution)/shard_map/ppermute | solution.py:303
  108.7 1.0 copy-start
  112.0 15.9 %all-to-all-start.3 = ((bf16[8,8,768]{2,1,0:T(8,128)(2,1)}), bf16[8,8,768]{2,1,0:T(8,128)(2,1)S(1)}, u32[]{:S(2)}, u32[]{:S(2)}) async-start(bf16[8,8,768]{2,1,0:T(8,128)(2,1)} %bitcast.17), calls=%async_computation.3 | async-start | bytes 196608 | tf_op jit(solution)/shard_map/all_to_all | solution.py:311
  127.9 0.6 copy-start.7
where the time goes:
time: 136 us; the launch traced here: 135 us
  waiting for transfers between devices  49.1 us (36%)
  Pallas kernels  37.4 us (28%)
  starting transfers between devices  36.7 us (27%)
  other arithmetic  7.03 us (5%)
  local copies, waits for them, and re-layouts  3.97 us (3%)
    all_to_all x4, starting transfers between devices, exchange(): return lax.all_to_all(a, axes, split_axis=0, concat_axis=0, tiled=True)  22.4 us
    all_to_all x4, waiting for transfers between devices, exchange(): return lax.all_to_all(a, axes, split_axis=0, concat_axis=0, tiled=True)  21.5 us
    pallas_call x1, Pallas kernels, gradients(): pl.pallas_call(main_kernel, in_specs=[vmem, vmem] + [hbm] * 10, out_specs...  21 us
    ppermute x4, waiting for transfers between devices, down(): return lax.ppermute(a, 'z', [(i, (i + 3) % 4) for i in range(4)])  17.8 us
    ppermute x4, starting transfers between devices, down(): return lax.ppermute(a, 'z', [(i, (i + 3) % 4) for i in range(4)])  11.2 us
    ppermute x4, waiting for transfers between devices, up(): return lax.ppermute(a, 'z', [(i, (i + 1) % 4) for i in range(4)])  7.78 us
    convert_element_type x4, other arithmetic, add(): return sum((a.astype(F32) for a in arrays)).astype(BF16)  6.92 us
    pallas_call x1, Pallas kernels, weight_gradients(): pl.pallas_call(weight_kernel, grid=(D // TALL,), in_specs=[pl.BlockSpec((...  6.53 us
  transfers between devices with their start and end apart: 21, of which 10 were waited for; matrix products, arithmetic and copies ran while one was open for 6% of the time, Pallas kernels for 3%

commit v1 on v0

--- a/solution.py
+++ b/solution.py
@@ -1,3 +1,5 @@
+import functools
+
 import jax
 import jax.numpy as jnp
 from jax import lax
@@ -38,46 +40,45 @@
     return lax.dot_general(a, b, dims, preferred_element_type=F32)
 
 
-def gen_kernel(q_ref, w_ref, hb_ref, t_ref, out_ref, qrep, acc):
-    step = pl.program_id(0)
-    row = iota((64, Q), 0)
-    col = iota((64, Q), 1)
+def gen_kernel(q_ref, w_ref, hb_ref, t_ref, out_ref, wbuf, sem):
+    def columns(n):
+        cols = pl.ds(n * D, D)
+        return pltpu.make_async_copy(w_ref.at[:, cols], wbuf.at[:, cols], sem.at[n])
+
+    for n in range(ROWS):
+        columns(n).start()
+    row, col = iota((64, Q), 0), iota((64, Q), 1)
     sub = iota((64, D), 0) % 8
-
-    @pl.when(step == 0)
-    def _():
-        rep = mm(one_hot(row // 8 == col), q_ref[...])
-        qrep[...] = rep.astype(BF16)
-        acc[...] = jnp.zeros_like(acc)
-        placed = jnp.where(sub == 6, rep, 0.0).astype(BF16)
-        acc[:, 0:ROWS] = mm(placed, hb_ref[...], NT)
-        acc[:, 0:DOCS] += mm(one_hot(row == col * 8 + 7), t_ref[...])
-
-    q = qrep[...].astype(F32)
-    for n in range(2):
-        placed = jnp.where(sub == step * 2 + n, q, 0.0).astype(BF16)
-        acc[...] += mm(placed, w_ref[:, n * D : (n + 1) * D])
-
-    @pl.when(step == ROWS // 2 - 1)
-    def _():
-        out_ref[...] = acc[...].astype(BF16)
+    rep = mm(one_hot(row // 8 == col), q_ref[...])
+    placed = jnp.where(sub == 6, rep, 0.0).astype(BF16)
+    bias = mm(placed, hb_ref[...], NT)
+    targets = mm(one_hot(row == col * 8 + 7), t_ref[...])
+    total = jnp.zeros((64, D), F32)
+    for n in range(ROWS):
+        placed = jnp.where(sub == n, rep, 0.0).astype(BF16)
+        columns(n).wait()
+        total = total + mm(placed, wbuf[:, n * D : (n + 1) * D])
+    out_ref[:, DOCS:] = total[:, DOCS:].astype(BF16)
+    total = total[:, 0:DOCS] + targets
+    out_ref[:, 128:DOCS] = total[:, 128:].astype(BF16)
+    m, l = iota((8, 128), 0), iota((8, 128), 1)
+    bias = jnp.concatenate([bias, jnp.zeros((64, 2), F32)], axis=1).astype(BF16)
+    bias = mm(bias, one_hot(m == l))
+    out_ref[:, 0:128] = (total[:, 0:128] + bias).astype(BF16)
 
 
 def generate(queries, weight, bias_t, teacher_t):
+    vmem = pl.BlockSpec(memory_space=pltpu.VMEM)
     return pl.pallas_call(
         gen_kernel,
-        grid=(ROWS // 2,),
-        in_specs=[
-            pl.BlockSpec((Q, D), lambda i: (0, 0)),
-            pl.BlockSpec((D, 2 * D), lambda i: (0, i)),
-            pl.BlockSpec((ROWS, D), lambda i: (0, 0)),
-            pl.BlockSpec((Q, DOCS), lambda i: (0, 0)),
-        ],
-        out_specs=pl.BlockSpec((64, D), lambda i: (0, 0)),
+        in_specs=[vmem, pl.BlockSpec(memory_space=pl.ANY), vmem, vmem],
+        out_specs=vmem,
         out_shape=jax.ShapeDtypeStruct((64, D), BF16),
-        scratch_shapes=[pltpu.VMEM((64, D), BF16), pltpu.VMEM((64, D), F32)],
-        compiler_params=pltpu.CompilerParams(dimension_semantics=("arbitrary",)),
-        cost_estimate=pl.CostEstimate(flops=2 * 64 * D * D * 6, bytes_accessed=D * D * 12, transcendentals=0),
+        scratch_shapes=[pltpu.VMEM((D, ROWS * D), BF16), pltpu.SemaphoreType.DMA((ROWS,))],
+        compiler_params=pltpu.CompilerParams(vmem_limit_bytes=60 << 20),
+        cost_estimate=pl.CostEstimate(
+            flops=2 * 64 * D * D * 6, bytes_accessed=D * D * 12, transcendentals=0
+        ),
         name="generate",
     )(queries, weight, bias_t, teacher_t)
 
@@ -115,22 +116,23 @@
             jax.ShapeDtypeStruct((CHIPS, WIRE, 128), BF16),
             jax.ShapeDtypeStruct((DOCS, 8), F32),
         ],
+        compiler_params=pltpu.CompilerParams(vmem_limit_bytes=8 << 20),
         name="assemble",
     )(src, received)
 
 
 def main_kernel(tgt_ref, g_ref, *refs):
-    docs, outs = refs[:10], refs[10:18]
-    lg_ref, dbuf, bbuf, pbuf, layer, bacc, even, odd, in_sem, out_sem = refs[18:]
+    docs, outs = refs[:14], refs[14:22]
+    lg_ref, dbuf, bbuf, pbuf, layer, bacc, even, odd, in_sem, out_sem = refs[22:]
     half = DOCS // 2
 
     def block(n, size=DOCS):
         return pl.ds(n * size, size)
 
-    for n in range(4):
+    for n in range(12):
         pltpu.make_async_copy(docs[n], dbuf.at[block(n, half)], in_sem.at[n // 2]).start()
-    for n in range(2, 8):
-        pltpu.make_async_copy(docs[n + 2], dbuf.at[block(n)], in_sem.at[n]).start()
+    for n in range(6, 8):
+        pltpu.make_async_copy(docs[n + 6], dbuf.at[block(n)], in_sem.at[n]).start()
 
     for chip in range(CHIPS):
         for rb in range(3):
@@ -207,7 +209,7 @@
     vmem = pl.BlockSpec(memory_space=pltpu.VMEM)
     return pl.pallas_call(
         main_kernel,
-        in_specs=[vmem, vmem] + [hbm] * 10,
+        in_specs=[vmem, vmem] + [hbm] * 14,
         out_specs=[hbm] * 8 + [vmem],
         out_shape=[jax.ShapeDtypeStruct((DOCS, D), BF16)] * 8
         + [jax.ShapeDtypeStruct((CHIPS, WIRE, 128), BF16)],
@@ -256,38 +258,45 @@
     return pl.pallas_call(
         reduce_kernel,
         out_shape=jax.ShapeDtypeStruct((64, D), BF16),
+        compiler_params=pltpu.CompilerParams(vmem_limit_bytes=8 << 20),
         name="reduced",
     )(arrived)
 
 
-def weight_kernel(q_ref, r_ref, out_ref, bias_ref):
+def weight_kernel(q_ref, r_ref, out_ref, bias_ref, obuf, sem):
+    def rows_of(n):
+        rows = pl.ds(n * TALL, TALL)
+        return pltpu.make_async_copy(obuf.at[rows], out_ref.at[rows], sem.at[n])
+
     row, col = iota((64, Q), 0), iota((64, Q), 1)
+    sub = iota((64, D), 0) % 8
     rep = mm(one_hot(row // 8 == col), q_ref[...])
-    sub = iota((64, TALL), 0) % 8
-    for n in range(ROWS):
-        placed = jnp.where(sub == n, rep, 0.0).astype(BF16)
-        out_ref[:, n * D : (n + 1) * D] = mm(placed, r_ref[...], TN).astype(BF16)
-    placed = jnp.where(sub == 6, rep, 0.0).astype(BF16)
-    bias_ref[...] = mm(r_ref[:, 0:128], placed, TN)[0:ROWS].astype(BF16)
+    placed = [jnp.where(sub == n, rep, 0.0).astype(BF16) for n in range(7)]
+    for k in range(D // TALL):
+        rows = slice(k * TALL, (k + 1) * TALL)
+        for n in range(ROWS):
+            obuf[rows, n * D : (n + 1) * D] = mm(placed[n][:, rows], r_ref[...], TN).astype(BF16)
+        rows_of(k).start()
+    bias_ref[...] = mm(r_ref[:, 0:128], placed[6], TN)[0:ROWS].astype(BF16)
+    for k in range(D // TALL):
+        rows_of(k).wait()
 
 
 def weight_gradients(queries, received):
+    vmem = pl.BlockSpec(memory_space=pltpu.VMEM)
     return pl.pallas_call(
         weight_kernel,
-        grid=(D // TALL,),
-        in_specs=[
-            pl.BlockSpec((Q, TALL), lambda i: (0, i)),
-            pl.BlockSpec((64, D), lambda i: (0, 0)),
-        ],
-        out_specs=[
-            pl.BlockSpec((TALL, ROWS * D), lambda i: (i, 0)),
-            pl.BlockSpec((ROWS, TALL), lambda i: (0, i)),
-        ],
+        in_specs=[vmem, vmem],
+        out_specs=[pl.BlockSpec(memory_space=pl.ANY), vmem],
         out_shape=[
             jax.ShapeDtypeStruct((D, ROWS * D), BF16),
             jax.ShapeDtypeStruct((ROWS, D), BF16),
         ],
-        compiler_params=pltpu.CompilerParams(dimension_semantics=("arbitrary",)),
+        scratch_shapes=[
+            pltpu.VMEM((D, ROWS * D), BF16),
+            pltpu.SemaphoreType.DMA((D // TALL,)),
+        ],
+        compiler_params=pltpu.CompilerParams(vmem_limit_bytes=16 << 20),
         cost_estimate=pl.CostEstimate(
             flops=2 * 64 * D * D * 6, bytes_accessed=D * D * 12, transcendentals=0
         ),
@@ -295,6 +304,55 @@
     )(queries, received)
 
 
+def sums_kernel(sizes, *refs):
+    outs = refs[sum(sizes) :]
+    at = 0
+    for out, size in zip(outs, sizes):
+        total = refs[at][...].astype(F32)
+        for term in refs[at + 1 : at + size]:
+            total = total + term[...].astype(F32)
+        out[...] = total.astype(BF16)
+        at += size
+
+
+def sums(*groups):
+    def half_of(h):
+        return pl.BlockSpec((DOCS // 4, D), lambda i: (2 * h + i, 0))
+
+    terms = [term for group in groups for term in group]
+    return pl.pallas_call(
+        functools.partial(sums_kernel, [len(group) for group in groups]),
+        grid=(2,),
+        in_specs=[half_of(h) for _, h in terms],
+        out_specs=[half_of(0) for _ in groups],
+        out_shape=[jax.ShapeDtypeStruct((DOCS // 2, D), BF16) for _ in groups],
+        compiler_params=pltpu.CompilerParams(vmem_limit_bytes=12 << 20),
+        cost_estimate=pl.CostEstimate(
+            flops=len(terms) * DOCS * D, bytes_accessed=len(terms) * DOCS * D, transcendentals=0
+        ),
+    )(*(array for array, _ in terms))
+
+
+def final_kernel(mine_ref, other_ref, ul_ref, dl_ref, uh_ref, dh_ref, out_ref):
+    half = DOCS // 2
+    for rows, a, b in ((slice(0, half), ul_ref, dl_ref), (slice(half, DOCS), uh_ref, dh_ref)):
+        total = mine_ref[rows].astype(F32) + other_ref[rows].astype(F32)
+        total = total + a[...].astype(F32) + b[...].astype(F32)
+        out_ref[rows] = total.astype(BF16)
+
+
+def document_sum(*parts):
+    return pl.pallas_call(
+        final_kernel,
+        out_shape=jax.ShapeDtypeStruct((DOCS, D), BF16),
+        compiler_params=pltpu.CompilerParams(vmem_limit_bytes=12 << 20),
+        cost_estimate=pl.CostEstimate(
+            flops=4 * DOCS * D, bytes_accessed=10 * DOCS * D, transcendentals=0
+        ),
+        name="document_sum",
+    )(*parts)
+
+
 def up(a):
     return lax.ppermute(a, "z", [(i, (i + 1) % 4) for i in range(4)])
 
@@ -309,10 +367,6 @@
 
 def exchange(a, axes):
     return lax.all_to_all(a, axes, split_axis=0, concat_axis=0, tiled=True)
-
-
-def add(*arrays):
-    return sum(a.astype(F32) for a in arrays).astype(BF16)
 
 
 def step(queries, hyper_weight, hyper_bias, documents, teacher):
@@ -320,12 +374,16 @@
     z, c = lax.axis_index("z"), lax.axis_index("c")
     generated = generate(queries, hyper_weight, hyper_bias.T, teacher.T)
     documents, generated = lax.optimization_barrier((documents, generated))
-    below = up(documents)
-    above = down(documents)
-    far = (up(below[:half]), down(above[half:]))
-    docs = [far[0], far[1], swap(far[0]), swap(far[1])]
-    for mine in (below, above, documents):
-        docs += [mine, swap(mine)]
+    low, high = documents[:half], documents[half:]
+    below_low = up(low)
+    above_high = down(high)
+    below_high = up(high)
+    above_low = down(low)
+    far = (up(below_low), down(above_high))
+    docs = []
+    for pair in (far, (below_low, below_high), (above_low, above_high)):
+        docs += [*pair, swap(pair[0]), swap(pair[1])]
+    docs += [documents, swap(documents)]
     pieces = exchange(generated, RING)
     src = jnp.stack(
         [((z + dz) % 4) * 2 + core for dz in (2, 3, 1, 0) for core in (c, 1 - c)]
@@ -337,18 +395,15 @@
     pieces = exchange(reduced(arrived), RING)
     far, below, above, own = parts[0::2]
     for_far, for_below, for_above, for_own = (swap(a) for a in parts[1::2])
-    from_below = up(add(far[:half], for_far[:half]))
-    from_above = down(add(far[half:], for_far[half:]))
-    to_above = jnp.concatenate(
-        [add(above[:half], for_above[:half], from_below), add(above[half:], for_above[half:])]
+    first = sums([(far, 0), (for_far, 0)], [(far, 1), (for_far, 1)])
+    far_low, far_high = up(first[0]), down(first[1])
+    second = sums([(above, 1), (for_above, 1)], [(below, 0), (for_below, 0)])
+    up_high, down_low = up(second[0]), down(second[1])
+    third = sums(
+        [(above, 0), (for_above, 0), (far_low, 0)], [(below, 1), (for_below, 1), (far_high, 0)]
     )
-    to_below = jnp.concatenate(
-        [add(below[:half], for_below[:half]), add(below[half:], for_below[half:], from_above)]
-    )
-    from_below = up(to_above)
-    from_above = down(to_below)
-    doc_grad = add(own, for_own, from_below, from_above)
-    doc_grad, pieces = lax.optimization_barrier((doc_grad, pieces))
+    up_low, down_high = up(third[0]), down(third[1])
+    doc_grad = document_sum(own, for_own, up_low, down_low, up_high, down_high)
     weight_grad, bias_grad = weight_gradients(queries, pieces)
     return doc_grad, weight_grad, bias_grad.T
 

time: 136 us -> 117 us (0.86)
  waiting for transfers between devices: 49.1 us -> 23.5 us
  blocking collectives: 0 us -> 12.5 us
  other arithmetic: 7.03 us -> 0 us
  starting transfers between devices: 36.7 us -> 38.8 us
    all_to_all x4 -> x3, waiting for transfers between devices: 21.5 us -> 0.54 us  [exchange(): return lax.all_to_all(a, axes, split_axis=0, concat_axis=0, tiled=True)]
    all_to_all x0 -> x1, blocking collectives: none -> 12.5 us  [exchange(): return lax.all_to_all(a, axes, split_axis=0, concat_axis=0, tiled=True)]
    convert_element_type x4 -> x0, other arithmetic: 6.92 us -> none  [add(): return sum((a.astype(F32) for a in arrays)).astype(BF16)]
    ppermute x4 -> x6, waiting for transfers between devices: 17.8 us -> 12.7 us  [down(): return lax.ppermute(a, 'z', [(i, (i + 3) % 4) for i in range(4)])]
    all_to_all x4 -> x3, starting transfers between devices: 22.4 us -> 19.8 us  [exchange(): return lax.all_to_all(a, axes, split_axis=0, concat_axis=0, tiled=True)]
    ppermute x4 -> x6, waiting for transfers between devices: 7.78 us -> 10.2 us  [up(): return lax.ppermute(a, 'z', [(i, (i + 1) % 4) for i in range(4)])]
    ppermute x4 -> x6, starting transfers between devices: 1.9 us -> 4.16 us  [up(): return lax.ppermute(a, 'z', [(i, (i + 1) % 4) for i in range(4)])]
    ppermute x9 -> x11, waiting for transfers between devices: 2.01 us -> 0.03 us  [swap(): return lax.ppermute(a, 'c', [(0, 1), (1, 0)])]
  transfers between devices with their start and end apart: 21 -> 26, of which waited for: 10 -> 5; matrix products, arithmetic and copies ran while one was open for 6% -> 0% of each run, Pallas kernels for 3% -> 7%
where the time goes in v1:
time: 117 us; the launch traced here: 116 us
  starting transfers between devices  38.8 us (33%)
  Pallas kernels  36.7 us (31%)
  waiting for transfers between devices  23.5 us (20%)
  blocking collectives  12.5 us (11%)
  local copies, waits for them, and re-layouts  3.8 us (3%)
    pallas_call x1, Pallas kernels, gradients(): pl.pallas_call(main_kernel, in_specs=[vmem, vmem] + [hbm] * 14, out_specs...  21 us
    all_to_all x3, starting transfers between devices, exchange(): return lax.all_to_all(a, axes, split_axis=0, concat_axis=0, tiled=True)  19.8 us
    ppermute x6, waiting for transfers between devices, down(): return lax.ppermute(a, 'z', [(i, (i + 3) % 4) for i in range(4)])  12.7 us
    ppermute x6, starting transfers between devices, down(): return lax.ppermute(a, 'z', [(i, (i + 3) % 4) for i in range(4)])  12.6 us
    all_to_all x1, blocking collectives, exchange(): return lax.all_to_all(a, axes, split_axis=0, concat_axis=0, tiled=True)  12.5 us
    ppermute x6, waiting for transfers between devices, up(): return lax.ppermute(a, 'z', [(i, (i + 1) % 4) for i in range(4)])  10.2 us
    pallas_call x1, Pallas kernels, generate(): pl.pallas_call(gen_kernel, in_specs=[vmem, pl.BlockSpec(memory_space=pl.A...  4.94 us
    pallas_call x1, Pallas kernels, weight_gradients(): pl.pallas_call(weight_kernel, in_specs=[vmem, vmem], out_specs=[pl.BlockS...  4.23 us
  transfers between devices with their start and end apart: 26, of which 5 were waited for; matrix products, arithmetic and copies ran while one was open for 0% of the time, Pallas kernels for 7%

profile of v1, /device:TPU:24, one launch (start us, length us, event | category | flops | bytes accessed | tf_op | source)
XLA Modules:
  0.0 116.2 jit_solution(16481152419473828030)
XLA Ops:
  0.6 0.0 copy-start.7
  0.6 4.9 %generate.1 = bf16[64,768]{1,0:T(8,128)(2,1)} custom-call(bf16[8,768]{1,0:T(8,128)(2,1)} %q_ref.3, bf16[768,4608]{1,0:T(8,128)(2,1)} %w_ref.1, bf16[6,768]{1,0:T(8,128)(2,1)} %bitcast.19, bf16[8,512]{1,0:T(8,128)(2,1)} %bitcast.20), custom_call_target="tpu_custom_call" | custom-call | flops 452984832 | bytes 7077888 | tf_op jit(solution)/shard_map/generate/pallas_call | solution.py:72
  5.6 5.3 %all-to-all-start = ((bf16[8,8,768]{2,1,0:T(8,128)(2,1)}), bf16[8,8,768]{2,1,0:T(8,128)(2,1)S(1)}, u32[]{:S(2)}, u32[]{:S(2)}) async-start(bf16[8,8,768]{2,1,0:T(8,128)(2,1)} %bitcast.18), calls=%async_computation | async-start | bytes 196608 | tf_op jit(solution)/shard_map/all_to_all | solution.py:369
  10.9 0.1 fusion
  11.0 2.1 %collective-permute-start.6 = (bf16[256,768]{1,0:T(8,128)(2,1)S(1)}, bf16[256,768]{1,0:T(8,128)(2,1)S(1)}, u32[]{:S(2)}, u32[]{:S(2)}) collective-permute-start(bf16[256,768]{1,0:T(8,128)(2,1)S(1)} %get-tuple-element.45), channel_id=1, source_target_pairs={{0,2},{2,4},{4,6},{6,0},{1,3},{3,5},{5,7},{7,1},{8,10},{10,12},{12... | collective-permute-start | bytes 1179656 | tf_op jit(solution)/shard_map/ppermute | solution.py:357
  13.1 1.3 %collective-permute-start.2 = (bf16[256,768]{1,0:T(8,128)(2,1)S(1)}, bf16[256,768]{1,0:T(8,128)(2,1)}, u32[]{:S(2)}, u32[]{:S(2)}) collective-permute-start(bf16[256,768]{1,0:T(8,128)(2,1)S(1)} %get-tuple-element.45), channel_id=1, source_target_pairs={{0,6},{2,0},{4,2},{6,4},{1,7},{3,1},{5,3},{7,5},{8,14},{10,8},{12,... | collective-permute-start | bytes 1179656 | tf_op jit(solution)/shard_map/ppermute | solution.py:361
  14.4 1.9 %collective-permute-start.9 = (bf16[256,768]{1,0:T(8,128)(2,1)S(1)}, bf16[256,768]{1,0:T(8,128)(2,1)}, u32[]{:S(2)}, u32[]{:S(2)}) collective-permute-start(bf16[256,768]{1,0:T(8,128)(2,1)S(1)} %get-tuple-element.46), channel_id=1, source_target_pairs={{0,6},{2,0},{4,2},{6,4},{1,7},{3,1},{5,3},{7,5},{8,14},{10,8},{12,... | collective-permute-start | bytes 1179656 | tf_op jit(solution)/shard_map/ppermute | solution.py:361
  16.3 0.1 collective-permute-start
  16.4 0.1 stack.35.src_ref
  16.5 0.5 all-to-all-done
  17.0 1.8 %assemble.1 = (bf16[16,304,128]{2,1,0:T(8,128)(2,1)}, f32[512,8]{1,0:T(8,128)S(1)}) custom-call(s32[8]{0:T(128)S(1)} %stack.35.src_ref, bf16[64,768]{1,0:T(8,128)(2,1)S(1)} %bitcast.15), custom_call_target="tpu_custom_call" | custom-call | tf_op jit(solution)/shard_map/assemble/pallas_call | solution.py:111
  18.8 0.7 copy-done.5
  19.5 7.2 %all-to-all-start.1 = ((bf16[16,304,128]{2,1,0:T(8,128)(2,1)}), bf16[16,304,128]{2,1,0:T(8,128)(2,1)S(1)}, u32[]{:S(2)}, u32[]{:S(2)}) async-start(bf16[16,304,128]{2,1,0:T(8,128)(2,1)} %get-tuple-element.26), calls=%async_computation.1 | async-start | bytes 2490368 | tf_op jit(solution)/shard_map/all_to_all | solution.py:369
  26.7 0.0 collective-permute-start.12
  26.7 0.0 collective-permute-done.6.refs_5_
  26.7 0.5 collective-permute-start.8
  27.2 0.0 collective-permute-done.2.refs_9_
  27.2 0.1 collective-permute-start.11
  27.3 5.1 %collective-permute-done.9.refs_8_ = bf16[256,768]{1,0:T(8,128)(2,1)} collective-permute-done((bf16[256,768]{1,0:T(8,128)(2,1)S(1)}, bf16[256,768]{1,0:T(8,128)(2,1)}, u32[]{:S(2)}, u32[]{:S(2)}) %collective-permute-start.9) | collective-permute-done | bytes 393248 | tf_op jit(solution)/shard_map/ppermute | solution.py:361
  32.4 2.8 %collective-permute-start.3 = (bf16[256,768]{1,0:T(8,128)(2,1)}, bf16[256,768]{1,0:T(8,128)(2,1)S(1)}, u32[]{:S(2)}, u32[]{:S(2)}) collective-permute-start(bf16[256,768]{1,0:T(8,128)(2,1)} %collective-permute-done.2.refs_9_), channel_id=1, source_target_pairs={{0,6},{2,0},{4,2},{6,4},{1,7},{3,1},{5,3},{7,5},{8,14},{10,8},{12,... | collective-permute-start | bytes 1179656 | tf_op jit(solution)/shard_map/ppermute | solution.py:361
  35.3 0.0 collective-permute-done.refs_4_
  35.3 0.0 collective-permute-start.1
  35.3 0.0 collective-permute-done.8.refs_7_
  35.3 0.1 collective-permute-start.7
  35.4 0.0 collective-permute-done.11.refs_11_
  35.4 0.5 collective-permute-start.10
  35.9 7.5 %collective-permute-done.3.refs_1_ = bf16[256,768]{1,0:T(8,128)(2,1)S(1)} collective-permute-done((bf16[256,768]{1,0:T(8,128)(2,1)}, bf16[256,768]{1,0:T(8,128)(2,1)S(1)}, u32[]{:S(2)}, u32[]{:S(2)}) %collective-permute-start.3) | collective-permute-done | bytes 393248 | tf_op jit(solution)/shard_map/ppermute | solution.py:361
  43.4 0.0 collective-permute-start.5
  43.4 3.3 %collective-permute-done.1.refs_0_ = bf16[256,768]{1,0:T(8,128)(2,1)S(1)} collective-permute-done((bf16[256,768]{1,0:T(8,128)(2,1)}, bf16[256,768]{1,0:T(8,128)(2,1)S(1)}, u32[]{:S(2)}, u32[]{:S(2)}) %collective-permute-start.1) | collective-permute-done | bytes 393248 | tf_op jit(solution)/shard_map/ppermute | solution.py:357
  46.7 0.0 collective-permute-start.4
  46.7 0.0 collective-permute-done.10.refs_10_
  46.7 0.0 collective-permute-done.7.refs_6_
  46.8 0.0 copy-start.8
  46.8 0.0 collective-permute-done.5.refs_3_
  46.8 0.7 copy-done.15
  47.5 0.2 copy-done.14
  47.7 0.3 copy-done.8
  47.9 0.8 copy-done.16
  48.7 1.0 copy-done.6
  49.7 21.0 %gradients.1 = (bf16[512,768]{1,0:T(8,128)(2,1)}, bf16[512,768]{1,0:T(8,128)(2,1)}, bf16[512,768]{1,0:T(8,128)(2,1)}, bf16[512,768]{1,0:T(8,128)(2,1)}, bf16[512...) custom-call(f32[512,8]{1,0:T(8,128)} %copy-done.5, ...), custom_call_target="tpu_custom_call" | custom-call | flops 14495514624 | bytes 12582912 | tf_op jit(solution)/shard_map/gradients/pallas_call | solution.py:210
  70.8 0.5 collective-permute-start.15
  71.3 7.3 %all-to-all-start.2 = ((bf16[16,304,128]{2,1,0:T(8,128)(2,1)}), bf16[16,304,128]{2,1,0:T(8,128)(2,1)S(1)}, u32[]{:S(2)}, u32[]{:S(2)}) async-start(bf16[16,304,128]{2,1,0:T(8,128)(2,1)} %get-tuple-element.42), calls=%async_computation.2 | async-start | bytes 2490368 | tf_op jit(solution)/shard_map/all_to_all | solution.py:369
  78.6 0.5 collective-permute-start.17
  79.1 0.0 collective-permute-done.15.refs_1_.refs_3_
  79.1 0.2 shard_map.76
  79.4 0.1 collective-permute-start.16
  79.4 3.2 %collective-permute-start.18 = (bf16[256,768]{1,0:T(8,128)(2,1)S(1)}, bf16[256,768]{1,0:T(8,128)(2,1)S(1)}, u32[]{:S(2)}, u32[]{:S(2)}) collective-permute-start(bf16[256,768]{1,0:T(8,128)(2,1)S(1)} %get-tuple-element.37), channel_id=1, source_target_pairs={{0,6},{2,0},{4,2},{6,4},{1,7},{3,1},{5,3},{7,5},{8,14},{10,8},{12,... | collective-permute-start | bytes 1179656 | tf_op jit(solution)/shard_map/ppermute | solution.py:361
  82.7 0.0 collective-permute-start.13
  82.7 0.0 collective-permute-done.14.refs_1_
  82.7 0.0 collective-permute-done.17.refs_4_.refs_3_
  82.7 1.0 shard_map.78
  83.7 0.1 collective-permute-start.20
  83.8 1.9 %collective-permute-start.21 = (bf16[256,768]{1,0:T(8,128)(2,1)}, bf16[256,768]{1,0:T(8,128)(2,1)S(1)}, u32[]{:S(2)}, u32[]{:S(2)}) collective-permute-start(bf16[256,768]{1,0:T(8,128)(2,1)} %get-tuple-element.40), channel_id=1, source_target_pairs={{0,2},{2,4},{4,6},{6,0},{1,3},{3,5},{5,7},{7,1},{8,10},{10,12},{12... | collective-permute-start | bytes 1179656 | tf_op jit(solution)/shard_map/ppermute | solution.py:357
  85.7 6.9 %collective-permute-done.16.refs_2_ = bf16[256,768]{1,0:T(8,128)(2,1)S(1)} collective-permute-done((bf16[256,768]{1,0:T(8,128)(2,1)S(1)}, bf16[256,768]{1,0:T(8,128)(2,1)S(1)}, u32[]{:S(2)}, u32[]{:S(2)}) %collective-permute-start.16) | collective-permute-done | bytes 393248 | tf_op jit(solution)/shard_map/ppermute | solution.py:357
  92.6 1.0 shard_map.77
  93.6 3.3 %collective-permute-start.22 = (bf16[256,768]{1,0:T(8,128)(2,1)}, bf16[256,768]{1,0:T(8,128)(2,1)}, u32[]{:S(2)}, u32[]{:S(2)}) collective-permute-start(bf16[256,768]{1,0:T(8,128)(2,1)} %get-tuple-element.41), channel_id=1, source_target_pairs={{0,6},{2,0},{4,2},{6,4},{1,7},{3,1},{5,3},{7,5},{8,14},{10,8},{12,... | collective-permute-start | bytes 1179656 | tf_op jit(solution)/shard_map/ppermute | solution.py:361
  96.9 0.0 all-to-all-done.2.y_ref
  96.9 0.3 reduced.1
  97.2 12.5 %all_to_all.32 = bf16[8,8,768]{2,1,0:T(8,128)(2,1)S(1)} all-to-all(bf16[8,8,768]{2,1,0:T(8,128)(2,1)S(1)} %bitcast.16), channel_id=1, replica_groups=mesh['xl'=2,'xh'=2,'y'=4,'z'=4,'c'=2] {'z','c'}, dimensions={0} | all-to-all | bytes 196608 | tf_op jit(solution)/shard_map/all_to_all | solution.py:369
  109.7 4.2 %weight_gradients.1 = (bf16[768,4608]{1,0:T(8,128)(2,1)}, bf16[6,768]{1,0:T(8,128)(2,1)}) custom-call(bf16[8,768]{1,0:T(8,128)(2,1)S(1)} %copy-done.4, bf16[64,768]{1,0:T(8,128)(2,1)S(1)} %bitcast.17), custom_call_target="tpu_custom_call" | custom-call | flops 452984832 | bytes 7077888 | tf_op jit(solution)/shard_map/weight_gradients/pallas_call | solution.py:287
  113.9 0.0 collective-permute-done.20.dl_ref
  113.9 0.0 collective-permute-done.21.uh_ref
  113.9 0.0 collective-permute-done.22.dh_ref
  114.0 2.3 %document_sum.1 = bf16[512,768]{1,0:T(8,128)(2,1)} custom-call(bf16[512,768]{1,0:T(8,128)(2,1)S(1)} %copy-done.3, bf16[512,768]{1,0:T(8,128)(2,1)S(1)} %collective-permute-done.13.other_ref, bf16[256,768]{1,0:T(8,128)(2,1)S(1)} %collective-permute-done.19.ul_ref, bf16[256,768]{1,0:T(8,128)(2,1)S(1)} %collective-permute-done.20.dl_ref, ...), custom_call_target="tpu_custom_call" | custom-call | flops 1572864 | bytes 3932160 | tf_op jit(solution)/shard_map/document_sum/pallas_call | solution.py:345
  (34 shorter events, 0.1 us)
Async XLA Ops:
  0.6 10.3 %copy-start.7 = (bf16[512,768]{1,0:T(8,128)(2,1)S(1)}, bf16[512,768]{1,0:T(8,128)(2,1)}, u32[]{:S(2)}) copy-start(bf16[512,768]{1,0:T(8,128)(2,1)} %refs_12_) | copy-start | bytes 2359300
  5.6 11.4 %all-to-all-start = ((bf16[8,8,768]{2,1,0:T(8,128)(2,1)}), bf16[8,8,768]{2,1,0:T(8,128)(2,1)S(1)}, u32[]{:S(2)}, u32[]{:S(2)}) async-start(bf16[8,8,768]{2,1,0:T(8,128)(2,1)} %bitcast.18), calls=%async_computation | async-start | bytes 196608 | tf_op jit(solution)/shard_map/all_to_all | solution.py:369
  11.0 15.7 %collective-permute-start.6 = (bf16[256,768]{1,0:T(8,128)(2,1)S(1)}, bf16[256,768]{1,0:T(8,128)(2,1)S(1)}, u32[]{:S(2)}, u32[]{:S(2)}) collective-permute-start(bf16[256,768]{1,0:T(8,128)(2,1)S(1)} %get-tuple-element.45), channel_id=1, source_target_pairs={{0,2},{2,4},{4,6},{6,0},{1,3},{3,5},{5,7},{7,1},{8,10},{10,12},{12... | collective-permute-start | bytes 1179656 | tf_op jit(solution)/shard_map/ppermute | solution.py:357
  13.1 14.2 %collective-permute-start.2 = (bf16[256,768]{1,0:T(8,128)(2,1)S(1)}, bf16[256,768]{1,0:T(8,128)(2,1)}, u32[]{:S(2)}, u32[]{:S(2)}) collective-permute-start(bf16[256,768]{1,0:T(8,128)(2,1)S(1)} %get-tuple-element.45), channel_id=1, source_target_pairs={{0,6},{2,0},{4,2},{6,4},{1,7},{3,1},{5,3},{7,5},{8,14},{10,8},{12,... | collective-permute-start | bytes 1179656 | tf_op jit(solution)/shard_map/ppermute | solution.py:361
  14.4 18.1 %collective-permute-start.9 = (bf16[256,768]{1,0:T(8,128)(2,1)S(1)}, bf16[256,768]{1,0:T(8,128)(2,1)}, u32[]{:S(2)}, u32[]{:S(2)}) collective-permute-start(bf16[256,768]{1,0:T(8,128)(2,1)S(1)} %get-tuple-element.46), channel_id=1, source_target_pairs={{0,6},{2,0},{4,2},{6,4},{1,7},{3,1},{5,3},{7,5},{8,14},{10,8},{12,... | collective-permute-start | bytes 1179656 | tf_op jit(solution)/shard_map/ppermute | solution.py:361
  16.3 19.0 %collective-permute-start = (bf16[256,768]{1,0:T(8,128)(2,1)S(1)}, bf16[256,768]{1,0:T(8,128)(2,1)}, u32[]{:S(2)}, u32[]{:S(2)}) collective-permute-start(bf16[256,768]{1,0:T(8,128)(2,1)S(1)} %get-tuple-element.46), channel_id=1, source_target_pairs={{0,2},{2,4},{4,6},{6,0},{1,3},{3,5},{5,7},{7,1},{8,10},{10,12},{12... | collective-permute-start | bytes 1179656 | tf_op jit(solution)/shard_map/ppermute | solution.py:357
  18.8 0.7 copy-start.5
  19.5 29.2 %all-to-all-start.1 = ((bf16[16,304,128]{2,1,0:T(8,128)(2,1)}), bf16[16,304,128]{2,1,0:T(8,128)(2,1)S(1)}, u32[]{:S(2)}, u32[]{:S(2)}) async-start(bf16[16,304,128]{2,1,0:T(8,128)(2,1)} %get-tuple-element.26), calls=%async_computation.1 | async-start | bytes 2490368 | tf_op jit(solution)/shard_map/all_to_all | solution.py:369
  26.7 20.1 %collective-permute-start.12 = (bf16[512,768]{1,0:T(8,128)(2,1)S(1)}, bf16[512,768]{1,0:T(8,128)(2,1)S(1)}, u32[]{:S(2)}, u32[]{:S(2)}) collective-permute-start(bf16[512,768]{1,0:T(8,128)(2,1)S(1)} %copy-done.7), channel_id=1, source_target_pairs={{0,1},{1,0},{2,3},{3,2},{4,5},{5,4},{6,7},{7,6},{8,9},{9,8},{10,11... | collective-permute-start | bytes 2359304 | tf_op jit(solution)/shard_map/ppermute | solution.py:365
  26.7 22.0 %copy-start.9 = (bf16[256,768]{1,0:T(8,128)(2,1)}, bf16[256,768]{1,0:T(8,128)(2,1)S(1)}, u32[]{:S(2)}) copy-start(bf16[256,768]{1,0:T(8,128)(2,1)S(1)} %collective-permute-done.6.refs_5_) | copy-start | bytes 1179652
  26.7 8.5 %collective-permute-start.8 = (bf16[256,768]{1,0:T(8,128)(2,1)S(1)}, bf16[256,768]{1,0:T(8,128)(2,1)S(1)}, u32[]{:S(2)}, u32[]{:S(2)}) collective-permute-start(bf16[256,768]{1,0:T(8,128)(2,1)S(1)} %collective-permute-done.6.refs_5_), channel_id=1, source_target_pairs={{0,1},{1,0},{2,3},{3,2},{4,5},{5,4},{6,7},{7,6},{8,9},{9,8},{10,11... | collective-permute-start | bytes 1179656 | tf_op jit(solution)/shard_map/ppermute | solution.py:365
  27.2 8.2 %collective-permute-start.11 = (bf16[256,768]{1,0:T(8,128)(2,1)}, bf16[256,768]{1,0:T(8,128)(2,1)S(1)}, u32[]{:S(2)}, u32[]{:S(2)}) collective-permute-start(bf16[256,768]{1,0:T(8,128)(2,1)} %collective-permute-done.2.refs_9_), channel_id=1, source_target_pairs={{0,1},{1,0},{2,3},{3,2},{4,5},{5,4},{6,7},{7,6},{8,9},{9,8},{10,11... | collective-permute-start | bytes 1179656 | tf_op jit(solution)/shard_map/ppermute | solution.py:365
  32.4 11.0 %collective-permute-start.3 = (bf16[256,768]{1,0:T(8,128)(2,1)}, bf16[256,768]{1,0:T(8,128)(2,1)S(1)}, u32[]{:S(2)}, u32[]{:S(2)}) collective-permute-start(bf16[256,768]{1,0:T(8,128)(2,1)} %collective-permute-done.2.refs_9_), channel_id=1, source_target_pairs={{0,6},{2,0},{4,2},{6,4},{1,7},{3,1},{5,3},{7,5},{8,14},{10,8},{12,... | collective-permute-start | bytes 1179656 | tf_op jit(solution)/shard_map/ppermute | solution.py:361
  35.3 11.4 %collective-permute-start.1 = (bf16[256,768]{1,0:T(8,128)(2,1)}, bf16[256,768]{1,0:T(8,128)(2,1)S(1)}, u32[]{:S(2)}, u32[]{:S(2)}) collective-permute-start(bf16[256,768]{1,0:T(8,128)(2,1)} %collective-permute-done.refs_4_), channel_id=1, source_target_pairs={{0,2},{2,4},{4,6},{6,0},{1,3},{3,5},{5,7},{7,1},{8,10},{10,12},{12... | collective-permute-start | bytes 1179656 | tf_op jit(solution)/shard_map/ppermute | solution.py:357
  35.3 11.5 %copy-start.10 = (bf16[256,768]{1,0:T(8,128)(2,1)}, bf16[256,768]{1,0:T(8,128)(2,1)S(1)}, u32[]{:S(2)}) copy-start(bf16[256,768]{1,0:T(8,128)(2,1)S(1)} %collective-permute-done.8.refs_7_) | copy-start | bytes 1179652
  35.3 11.5 %collective-permute-start.7 = (bf16[256,768]{1,0:T(8,128)(2,1)}, bf16[256,768]{1,0:T(8,128)(2,1)S(1)}, u32[]{:S(2)}, u32[]{:S(2)}) collective-permute-start(bf16[256,768]{1,0:T(8,128)(2,1)} %collective-permute-done.refs_4_), channel_id=1, source_target_pairs={{0,1},{1,0},{2,3},{3,2},{4,5},{5,4},{6,7},{7,6},{8,9},{9,8},{10,11... | collective-permute-start | bytes 1179656 | tf_op jit(solution)/shard_map/ppermute | solution.py:365
  35.4 13.3 %copy-start.11 = (bf16[256,768]{1,0:T(8,128)(2,1)}, bf16[256,768]{1,0:T(8,128)(2,1)S(1)}, u32[]{:S(2)}) copy-start(bf16[256,768]{1,0:T(8,128)(2,1)S(1)} %collective-permute-done.11.refs_11_) | copy-start | bytes 1179652
  35.4 11.3 %collective-permute-start.10 = (bf16[256,768]{1,0:T(8,128)(2,1)}, bf16[256,768]{1,0:T(8,128)(2,1)S(1)}, u32[]{:S(2)}, u32[]{:S(2)}) collective-permute-start(bf16[256,768]{1,0:T(8,128)(2,1)} %collective-permute-done.9.refs_8_), channel_id=1, source_target_pairs={{0,1},{1,0},{2,3},{3,2},{4,5},{5,4},{6,7},{7,6},{8,9},{9,8},{10,11... | collective-permute-start | bytes 1179656 | tf_op jit(solution)/shard_map/ppermute | solution.py:365
  43.4 3.4 %copy-start.12 = (bf16[256,768]{1,0:T(8,128)(2,1)}, bf16[256,768]{1,0:T(8,128)(2,1)S(1)}, u32[]{:S(2)}) copy-start(bf16[256,768]{1,0:T(8,128)(2,1)S(1)} %collective-permute-done.3.refs_1_) | copy-start | bytes 1179652
  43.4 3.4 %collective-permute-start.5 = (bf16[256,768]{1,0:T(8,128)(2,1)S(1)}, bf16[256,768]{1,0:T(8,128)(2,1)S(1)}, u32[]{:S(2)}, u32[]{:S(2)}) collective-permute-start(bf16[256,768]{1,0:T(8,128)(2,1)S(1)} %collective-permute-done.3.refs_1_), channel_id=1, source_target_pairs={{0,1},{1,0},{2,3},{3,2},{4,5},{5,4},{6,7},{7,6},{8,9},{9,8},{10,11... | collective-permute-start | bytes 1179656 | tf_op jit(solution)/shard_map/ppermute | solution.py:365
  46.7 2.0 %copy-start.13 = (bf16[256,768]{1,0:T(8,128)(2,1)}, bf16[256,768]{1,0:T(8,128)(2,1)S(1)}, u32[]{:S(2)}) copy-start(bf16[256,768]{1,0:T(8,128)(2,1)S(1)} %collective-permute-done.1.refs_0_) | copy-start | bytes 1179652
  46.7 2.0 %collective-permute-start.4 = (bf16[256,768]{1,0:T(8,128)(2,1)S(1)}, bf16[256,768]{1,0:T(8,128)(2,1)}, u32[]{:S(2)}, u32[]{:S(2)}) collective-permute-start(bf16[256,768]{1,0:T(8,128)(2,1)S(1)} %collective-permute-done.1.refs_0_), channel_id=1, source_target_pairs={{0,1},{1,0},{2,3},{3,2},{4,5},{5,4},{6,7},{7,6},{8,9},{9,8},{10,11... | collective-permute-start | bytes 1179656 | tf_op jit(solution)/shard_map/ppermute | solution.py:365
  46.7 0.8 copy-start.15
  46.7 0.9 copy-start.14
  46.8 1.2 copy-start.8
  47.9 0.8 copy-start.16
  48.7 1.0 copy-start.6
  70.8 8.3 %collective-permute-start.15 = (bf16[512,768]{1,0:T(8,128)(2,1)}, bf16[512,768]{1,0:T(8,128)(2,1)S(1)}, u32[]{:S(2)}, u32[]{:S(2)}) collective-permute-start(bf16[512,768]{1,0:T(8,128)(2,1)} %get-tuple-element.33), channel_id=1, source_target_pairs={{0,1},{1,0},{2,3},{3,2},{4,5},{5,4},{6,7},{7,6},{8,9},{9,8},{10,11... | collective-permute-start | bytes 2359304 | tf_op jit(solution)/shard_map/ppermute | solution.py:365
  71.3 7.8 %copy-start = (bf16[512,768]{1,0:T(8,128)(2,1)S(1)}, bf16[512,768]{1,0:T(8,128)(2,1)}, u32[]{:S(2)}) copy-start(bf16[512,768]{1,0:T(8,128)(2,1)} %get-tuple-element.32.refs_0_.refs_2_) | copy-start | bytes 2359300
  71.3 25.6 %all-to-all-start.2 = ((bf16[16,304,128]{2,1,0:T(8,128)(2,1)}), bf16[16,304,128]{2,1,0:T(8,128)(2,1)S(1)}, u32[]{:S(2)}, u32[]{:S(2)}) async-start(bf16[16,304,128]{2,1,0:T(8,128)(2,1)} %get-tuple-element.42), calls=%async_computation.2 | async-start | bytes 2490368 | tf_op jit(solution)/shard_map/all_to_all | solution.py:369
  78.6 4.1 %collective-permute-start.14 = (bf16[512,768]{1,0:T(8,128)(2,1)}, bf16[512,768]{1,0:T(8,128)(2,1)S(1)}, u32[]{:S(2)}, u32[]{:S(2)}) collective-permute-start(bf16[512,768]{1,0:T(8,128)(2,1)} %get-tuple-element.31), channel_id=1, source_target_pairs={{0,1},{1,0},{2,3},{3,2},{4,5},{5,4},{6,7},{7,6},{8,9},{9,8},{10,11... | collective-permute-start | bytes 2359304 | tf_op jit(solution)/shard_map/ppermute | solution.py:365
  78.6 4.1 %collective-permute-start.17 = (bf16[512,768]{1,0:T(8,128)(2,1)}, bf16[512,768]{1,0:T(8,128)(2,1)S(1)}, u32[]{:S(2)}, u32[]{:S(2)}) collective-permute-start(bf16[512,768]{1,0:T(8,128)(2,1)} %get-tuple-element.36), channel_id=1, source_target_pairs={{0,1},{1,0},{2,3},{3,2},{4,5},{5,4},{6,7},{7,6},{8,9},{9,8},{10,11... | collective-permute-start | bytes 2359304 | tf_op jit(solution)/shard_map/ppermute | solution.py:365
  79.1 3.6 %copy-start.1 = (bf16[512,768]{1,0:T(8,128)(2,1)S(1)}, bf16[512,768]{1,0:T(8,128)(2,1)}, u32[]{:S(2)}) copy-start(bf16[512,768]{1,0:T(8,128)(2,1)} %get-tuple-element.35.refs_3_.refs_2_) | copy-start | bytes 2359300
  79.1 3.6 %copy-start.2 = (bf16[512,768]{1,0:T(8,128)(2,1)S(1)}, bf16[512,768]{1,0:T(8,128)(2,1)}, u32[]{:S(2)}) copy-start(bf16[512,768]{1,0:T(8,128)(2,1)} %get-tuple-element.30.refs_0_) | copy-start | bytes 2359300
  79.4 13.3 %collective-permute-start.16 = (bf16[256,768]{1,0:T(8,128)(2,1)S(1)}, bf16[256,768]{1,0:T(8,128)(2,1)S(1)}, u32[]{:S(2)}, u32[]{:S(2)}) collective-permute-start(bf16[256,768]{1,0:T(8,128)(2,1)S(1)} %get-tuple-element.34), channel_id=1, source_target_pairs={{0,2},{2,4},{4,6},{6,0},{1,3},{3,5},{5,7},{7,1},{8,10},{10,12},{12... | collective-permute-start | bytes 1179656 | tf_op jit(solution)/shard_map/ppermute | solution.py:357
  79.4 13.2 %collective-permute-start.18 = (bf16[256,768]{1,0:T(8,128)(2,1)S(1)}, bf16[256,768]{1,0:T(8,128)(2,1)S(1)}, u32[]{:S(2)}, u32[]{:S(2)}) collective-permute-start(bf16[256,768]{1,0:T(8,128)(2,1)S(1)} %get-tuple-element.37), channel_id=1, source_target_pairs={{0,6},{2,0},{4,2},{6,4},{1,7},{3,1},{5,3},{7,5},{8,14},{10,8},{12,... | collective-permute-start | bytes 1179656 | tf_op jit(solution)/shard_map/ppermute | solution.py:361
  82.7 31.2 %collective-permute-start.13 = (bf16[512,768]{1,0:T(8,128)(2,1)}, bf16[512,768]{1,0:T(8,128)(2,1)S(1)}, u32[]{:S(2)}, u32[]{:S(2)}) collective-permute-start(bf16[512,768]{1,0:T(8,128)(2,1)} %get-tuple-element.29), channel_id=1, source_target_pairs={{0,1},{1,0},{2,3},{3,2},{4,5},{5,4},{6,7},{7,6},{8,9},{9,8},{10,11... | collective-permute-start | bytes 2359304 | tf_op jit(solution)/shard_map/ppermute | solution.py:365
  83.7 30.2 %collective-permute-start.20 = (bf16[256,768]{1,0:T(8,128)(2,1)}, bf16[256,768]{1,0:T(8,128)(2,1)S(1)}, u32[]{:S(2)}, u32[]{:S(2)}) collective-permute-start(bf16[256,768]{1,0:T(8,128)(2,1)} %get-tuple-element.39), channel_id=1, source_target_pairs={{0,6},{2,0},{4,2},{6,4},{1,7},{3,1},{5,3},{7,5},{8,14},{10,8},{12,... | collective-permute-start | bytes 1179656 | tf_op jit(solution)/shard_map/ppermute | solution.py:361
  83.8 30.1 %collective-permute-start.21 = (bf16[256,768]{1,0:T(8,128)(2,1)}, bf16[256,768]{1,0:T(8,128)(2,1)S(1)}, u32[]{:S(2)}, u32[]{:S(2)}) collective-permute-start(bf16[256,768]{1,0:T(8,128)(2,1)} %get-tuple-element.40), channel_id=1, source_target_pairs={{0,2},{2,4},{4,6},{6,0},{1,3},{3,5},{5,7},{7,1},{8,10},{10,12},{12... | collective-permute-start | bytes 1179656 | tf_op jit(solution)/shard_map/ppermute | solution.py:357
  93.6 16.1 %copy-start.4 = (bf16[8,768]{1,0:T(8,128)(2,1)S(1)}, bf16[8,768]{1,0:T(8,128)(2,1)}, u32[]{:S(2)}) copy-start(bf16[8,768]{1,0:T(8,128)(2,1)} %q_ref.3) | copy-start | bytes 36868
  93.6 20.3 %collective-permute-start.19 = (bf16[256,768]{1,0:T(8,128)(2,1)}, bf16[256,768]{1,0:T(8,128)(2,1)S(1)}, u32[]{:S(2)}, u32[]{:S(2)}) collective-permute-start(bf16[256,768]{1,0:T(8,128)(2,1)} %get-tuple-element.38), channel_id=1, source_target_pairs={{0,2},{2,4},{4,6},{6,0},{1,3},{3,5},{5,7},{7,1},{8,10},{10,12},{12... | collective-permute-start | bytes 1179656 | tf_op jit(solution)/shard_map/ppermute | solution.py:357
  93.6 20.3 %collective-permute-start.22 = (bf16[256,768]{1,0:T(8,128)(2,1)}, bf16[256,768]{1,0:T(8,128)(2,1)}, u32[]{:S(2)}, u32[]{:S(2)}) collective-permute-start(bf16[256,768]{1,0:T(8,128)(2,1)} %get-tuple-element.41), channel_id=1, source_target_pairs={{0,6},{2,0},{4,2},{6,4},{1,7},{3,1},{5,3},{7,5},{8,14},{10,8},{12,... | collective-permute-start | bytes 1179656 | tf_op jit(solution)/shard_map/ppermute | solution.py:361
  97.2 16.8 %copy-start.3 = (bf16[512,768]{1,0:T(8,128)(2,1)S(1)}, bf16[512,768]{1,0:T(8,128)(2,1)}, u32[]{:S(2)}) copy-start(bf16[512,768]{1,0:T(8,128)(2,1)} %get-tuple-element.28.mine_ref) | copy-start | bytes 2359300

commit v2 on v1

--- a/solution.py
+++ b/solution.py
@@ -40,13 +40,19 @@
     return lax.dot_general(a, b, dims, preferred_element_type=F32)
 
 
-def gen_kernel(q_ref, w_ref, hb_ref, t_ref, out_ref, wbuf, sem):
+def gen_kernel(q_ref, w_ref, hb_ref, t_ref, d_ref, out_ref, low_ref, high_ref, wbuf, dbuf, sem):
     def columns(n):
         cols = pl.ds(n * D, D)
         return pltpu.make_async_copy(w_ref.at[:, cols], wbuf.at[:, cols], sem.at[n])
 
+    half = DOCS // 2
+    docs_in = pltpu.make_async_copy(d_ref, dbuf, sem.at[ROWS])
+    low_out = pltpu.make_async_copy(dbuf.at[0:half], low_ref, sem.at[ROWS + 1])
+    high_out = pltpu.make_async_copy(dbuf.at[half:DOCS], high_ref, sem.at[ROWS + 2])
     for n in range(ROWS):
         columns(n).start()
+        if n == 2:
+            docs_in.start()
     row, col = iota((64, Q), 0), iota((64, Q), 1)
     sub = iota((64, D), 0) % 8
     rep = mm(one_hot(row // 8 == col), q_ref[...])
@@ -57,6 +63,10 @@
     for n in range(ROWS):
         placed = jnp.where(sub == n, rep, 0.0).astype(BF16)
         columns(n).wait()
+        if n == ROWS - 2:
+            docs_in.wait()
+            low_out.start()
+            high_out.start()
         total = total + mm(placed, wbuf[:, n * D : (n + 1) * D])
     out_ref[:, DOCS:] = total[:, DOCS:].astype(BF16)
     total = total[:, 0:DOCS] + targets
@@ -65,22 +75,30 @@
     bias = jnp.concatenate([bias, jnp.zeros((64, 2), F32)], axis=1).astype(BF16)
     bias = mm(bias, one_hot(m == l))
     out_ref[:, 0:128] = (total[:, 0:128] + bias).astype(BF16)
-
-
-def generate(queries, weight, bias_t, teacher_t):
+    low_out.wait()
+    high_out.wait()
+
+
+def generate(queries, weight, bias_t, teacher_t, documents):
+    hbm = pl.BlockSpec(memory_space=pl.ANY)
     vmem = pl.BlockSpec(memory_space=pltpu.VMEM)
     return pl.pallas_call(
         gen_kernel,
-        in_specs=[vmem, pl.BlockSpec(memory_space=pl.ANY), vmem, vmem],
-        out_specs=vmem,
-        out_shape=jax.ShapeDtypeStruct((64, D), BF16),
-        scratch_shapes=[pltpu.VMEM((D, ROWS * D), BF16), pltpu.SemaphoreType.DMA((ROWS,))],
+        in_specs=[vmem, hbm, vmem, vmem, hbm],
+        out_specs=[vmem, hbm, hbm],
+        out_shape=[jax.ShapeDtypeStruct((64, D), BF16)]
+        + [jax.ShapeDtypeStruct((DOCS // 2, D), BF16)] * 2,
+        scratch_shapes=[
+            pltpu.VMEM((D, ROWS * D), BF16),
+            pltpu.VMEM((DOCS, D), BF16),
+            pltpu.SemaphoreType.DMA((ROWS + 3,)),
+        ],
         compiler_params=pltpu.CompilerParams(vmem_limit_bytes=60 << 20),
         cost_estimate=pl.CostEstimate(
             flops=2 * 64 * D * D * 6, bytes_accessed=D * D * 12, transcendentals=0
         ),
         name="generate",
-    )(queries, weight, bias_t, teacher_t)
+    )(queries, weight, bias_t, teacher_t, documents)
 
 
 def assemble_kernel(src_ref, r_ref, out_ref, tgt_ref):
@@ -222,7 +240,7 @@
             pltpu.SemaphoreType.DMA((8,)),
             pltpu.SemaphoreType.DMA((8,)),
         ],
-        compiler_params=pltpu.CompilerParams(vmem_limit_bytes=60 << 20),
+        compiler_params=pltpu.CompilerParams(vmem_limit_bytes=51 << 20),
         cost_estimate=pl.CostEstimate(
             flops=6 * 8 * DOCS * D * D, bytes_accessed=32 * DOCS * D, transcendentals=0
         ),
@@ -370,11 +388,10 @@
 
 
 def step(queries, hyper_weight, hyper_bias, documents, teacher):
-    half = DOCS // 2
     z, c = lax.axis_index("z"), lax.axis_index("c")
-    generated = generate(queries, hyper_weight, hyper_bias.T, teacher.T)
-    documents, generated = lax.optimization_barrier((documents, generated))
-    low, high = documents[:half], documents[half:]
+    generated, low, high = generate(
+        queries, hyper_weight, hyper_bias.T, teacher.T, documents
+    )
     below_low = up(low)
     above_high = down(high)
     below_high = up(high)

time: 117 us -> 117 us (level)
  local copies, waits for them, and re-layouts: 3.8 us -> 0.13 us
  starting transfers between devices: 38.8 us -> 40.7 us
  Pallas kernels: 36.7 us -> 38 us
    ppermute x6, waiting for transfers between devices: 12.7 us -> 5.14 us  [down(): return lax.ppermute(a, 'z', [(i, (i + 3) % 4) for i in range(4)])]
    ppermute x6, waiting for transfers between devices: 10.2 us -> 17.1 us  [up(): return lax.ppermute(a, 'z', [(i, (i + 1) % 4) for i in range(4)])]
    unnamed x34 -> x22, local copies, waits for them, and re-layouts: 3.66 us -> 0.04 us
    ppermute x6, starting transfers between devices: 12.6 us -> 16.2 us  [down(): return lax.ppermute(a, 'z', [(i, (i + 3) % 4) for i in range(4)])]
    ppermute x6, starting transfers between devices: 4.16 us -> 2.16 us  [up(): return lax.ppermute(a, 'z', [(i, (i + 1) % 4) for i in range(4)])]
    ppermute x11, waiting for transfers between devices: 0.03 us -> 1.75 us  [swap(): return lax.ppermute(a, 'c', [(0, 1), (1, 0)])]
  transfers between devices with their start and end apart: 26 -> 26, of which waited for: 5 -> 6; matrix products, arithmetic and copies ran while one was open for 0% -> 0% of each run, Pallas kernels for 7% -> 7%
where the time goes in v2:
time: 117 us; the launch traced here: 116 us
  starting transfers between devices  40.7 us (35%)
  Pallas kernels  38 us (32%)
  waiting for transfers between devices  24 us (21%)
  blocking collectives  12.4 us (11%)
    pallas_call x1, Pallas kernels, gradients(): pl.pallas_call(main_kernel, in_specs=[vmem, vmem] + [hbm] * 14, out_specs...  21.6 us
    all_to_all x3, starting transfers between devices, exchange(): return lax.all_to_all(a, axes, split_axis=0, concat_axis=0, tiled=True)  20 us
    ppermute x6, waiting for transfers between devices, up(): return lax.ppermute(a, 'z', [(i, (i + 1) % 4) for i in range(4)])  17.1 us
    ppermute x6, starting transfers between devices, down(): return lax.ppermute(a, 'z', [(i, (i + 3) % 4) for i in range(4)])  16.2 us
    all_to_all x1, blocking collectives, exchange(): return lax.all_to_all(a, axes, split_axis=0, concat_axis=0, tiled=True)  12.4 us
    pallas_call x1, Pallas kernels, generate(): pl.pallas_call(gen_kernel, in_specs=[vmem, hbm, vmem, vmem, hbm], out_spe...  5.55 us
    ppermute x6, waiting for transfers between devices, down(): return lax.ppermute(a, 'z', [(i, (i + 3) % 4) for i in range(4)])  5.14 us
    pallas_call x1, Pallas kernels, weight_gradients(): pl.pallas_call(weight_kernel, in_specs=[vmem, vmem], out_specs=[pl.BlockS...  4.23 us
  transfers between devices with their start and end apart: 26, of which 6 were waited for; matrix products, arithmetic and copies ran while one was open for 0% of the time, Pallas kernels for 7%

profile of v2, /device:TPU:24, one launch (start us, length us, event | category | flops | bytes accessed | tf_op | source)
XLA Modules:
  0.0 116.2 jit_solution(16796076748279420894)
XLA Ops:
  0.6 0.0 copy-start.5
  0.6 5.5 %generate.1 = (bf16[64,768]{1,0:T(8,128)(2,1)}, bf16[256,768]{1,0:T(8,128)(2,1)}, bf16[256,768]{1,0:T(8,128)(2,1)}) custom-call(bf16[8,768]{1,0:T(8,128)(2,1)} %q_ref.3, bf16[768,4608]{1,0:T(8,128)(2,1)} %w_ref.1, bf16[6,768]{1,0:T(8,128)(2,1)} %bitcast.19, bf16[8,512]{1,0:T(8,128)(2,1)} %bitcast.20, bf16[512,768]{1,0:T(8,128)(2,1)} %refs_12_.1), custom_call_target="tpu_custom_call" | custom-call | flops 452984832 | bytes 7077888 | tf_op jit(solution)/shard_map/generate/pallas_call | solution.py:85
  6.2 5.3 %all-to-all-start = ((bf16[8,8,768]{2,1,0:T(8,128)(2,1)}), bf16[8,8,768]{2,1,0:T(8,128)(2,1)S(1)}, u32[]{:S(2)}, u32[]{:S(2)}) async-start(bf16[8,8,768]{2,1,0:T(8,128)(2,1)} %bitcast.18), calls=%async_computation | async-start | bytes 196608 | tf_op jit(solution)/shard_map/all_to_all | solution.py:387
  11.5 0.5 collective-permute-start.12
  12.0 2.8 %collective-permute-start.9 = (bf16[256,768]{1,0:T(8,128)(2,1)}, bf16[256,768]{1,0:T(8,128)(2,1)S(1)}, u32[]{:S(2)}, u32[]{:S(2)}) collective-permute-start(bf16[256,768]{1,0:T(8,128)(2,1)} %get-tuple-element.28), channel_id=1, source_target_pairs={{0,6},{2,0},{4,2},{6,4},{1,7},{3,1},{5,3},{7,5},{8,14},{10,8},{12,... | collective-permute-start | bytes 1179656 | tf_op jit(solution)/shard_map/ppermute | solution.py:379
  14.9 0.0 collective-permute-start
  14.9 3.2 %collective-permute-start.2 = (bf16[256,768]{1,0:T(8,128)(2,1)}, bf16[256,768]{1,0:T(8,128)(2,1)}, u32[]{:S(2)}, u32[]{:S(2)}) collective-permute-start(bf16[256,768]{1,0:T(8,128)(2,1)} %get-tuple-element.29), channel_id=1, source_target_pairs={{0,6},{2,0},{4,2},{6,4},{1,7},{3,1},{5,3},{7,5},{8,14},{10,8},{12,... | collective-permute-start | bytes 1179656 | tf_op jit(solution)/shard_map/ppermute | solution.py:379
  18.1 0.1 stack.35.src_ref
  18.2 0.0 all-to-all-done
  18.2 1.8 %assemble.1 = (bf16[16,304,128]{2,1,0:T(8,128)(2,1)}, f32[512,8]{1,0:T(8,128)S(1)}) custom-call(s32[8]{0:T(128)S(1)} %stack.35.src_ref, bf16[64,768]{1,0:T(8,128)(2,1)S(1)} %bitcast.15), custom_call_target="tpu_custom_call" | custom-call | tf_op jit(solution)/shard_map/assemble/pallas_call | solution.py:129
  20.0 7.3 %all-to-all-start.1 = ((bf16[16,304,128]{2,1,0:T(8,128)(2,1)}), bf16[16,304,128]{2,1,0:T(8,128)(2,1)}, u32[]{:S(2)}, u32[]{:S(2)}) async-start(bf16[16,304,128]{2,1,0:T(8,128)(2,1)} %get-tuple-element.27), calls=%async_computation.1 | async-start | bytes 2490368 | tf_op jit(solution)/shard_map/all_to_all | solution.py:387
  27.3 0.1 collective-permute-start.6
  27.4 0.0 collective-permute-done.9.refs_8_
  27.4 0.1 collective-permute-start.10
  27.5 0.0 collective-permute-done.refs_4_
  27.5 0.1 collective-permute-start.1
  27.6 5.1 %collective-permute-done.2.refs_9_ = bf16[256,768]{1,0:T(8,128)(2,1)} collective-permute-done((bf16[256,768]{1,0:T(8,128)(2,1)}, bf16[256,768]{1,0:T(8,128)(2,1)}, u32[]{:S(2)}, u32[]{:S(2)}) %collective-permute-start.2) | collective-permute-done | bytes 393248 | tf_op jit(solution)/shard_map/ppermute | solution.py:379
  32.7 3.5 %collective-permute-start.3 = (bf16[256,768]{1,0:T(8,128)(2,1)}, bf16[256,768]{1,0:T(8,128)(2,1)S(1)}, u32[]{:S(2)}, u32[]{:S(2)}) collective-permute-start(bf16[256,768]{1,0:T(8,128)(2,1)} %collective-permute-done.2.refs_9_), channel_id=1, source_target_pairs={{0,6},{2,0},{4,2},{6,4},{1,7},{3,1},{5,3},{7,5},{8,14},{10,8},{12,... | collective-permute-start | bytes 1179656 | tf_op jit(solution)/shard_map/ppermute | solution.py:379
  36.2 4.3 %collective-permute-done.6.refs_5_ = bf16[256,768]{1,0:T(8,128)(2,1)S(1)} collective-permute-done((bf16[256,768]{1,0:T(8,128)(2,1)S(1)}, bf16[256,768]{1,0:T(8,128)(2,1)S(1)}, u32[]{:S(2)}, u32[]{:S(2)}) %collective-permute-start.6) | collective-permute-done | bytes 393248 | tf_op jit(solution)/shard_map/ppermute | solution.py:375
  40.6 0.0 collective-permute-start.7
  40.6 0.0 collective-permute-done.12.refs_13_
  40.6 0.5 collective-permute-start.11
  41.1 0.0 collective-permute-done.10.refs_10_
  41.1 0.1 collective-permute-start.8
  41.2 5.8 %collective-permute-done.1.refs_0_ = bf16[256,768]{1,0:T(8,128)(2,1)S(1)} collective-permute-done((bf16[256,768]{1,0:T(8,128)(2,1)S(1)}, bf16[256,768]{1,0:T(8,128)(2,1)S(1)}, u32[]{:S(2)}, u32[]{:S(2)}) %collective-permute-start.1) | collective-permute-done | bytes 393248 | tf_op jit(solution)/shard_map/ppermute | solution.py:375
  47.0 0.0 collective-permute-start.4
  47.0 0.0 collective-permute-done.3.refs_1_
  47.0 0.5 collective-permute-start.5
  47.6 0.0 collective-permute-done.7.refs_6_
  47.6 0.0 collective-permute-done.8.refs_7_
  47.6 0.0 collective-permute-done.11.refs_11_
  47.6 1.2 %collective-permute-done.4.refs_2_ = bf16[256,768]{1,0:T(8,128)(2,1)S(1)} collective-permute-done((bf16[256,768]{1,0:T(8,128)(2,1)S(1)}, bf16[256,768]{1,0:T(8,128)(2,1)S(1)}, u32[]{:S(2)}, u32[]{:S(2)}) %collective-permute-start.4) | collective-permute-done | bytes 393248 | tf_op jit(solution)/shard_map/ppermute | solution.py:383
  48.8 0.6 collective-permute-done.5.refs_3_
  49.3 0.0 all-to-all-done.1.g_ref
  49.3 21.6 %gradients.1 = (bf16[512,768]{1,0:T(8,128)(2,1)}, bf16[512,768]{1,0:T(8,128)(2,1)}, bf16[512,768]{1,0:T(8,128)(2,1)}, bf16[512,768]{1,0:T(8,128)(2,1)}, bf16[512...) custom-call(f32[512,8]{1,0:T(8,128)S(1)} %get-tuple-element.26.tgt_r, ...), custom_call_target="tpu_custom_call" | custom-call | flops 14495514624 | bytes 12582912 | tf_op jit(solution)/shard_map/gradients/pallas_call | solution.py:228
  71.0 0.2 collective-permute-start.15
  71.2 7.4 %all-to-all-start.2 = ((bf16[16,304,128]{2,1,0:T(8,128)(2,1)}), bf16[16,304,128]{2,1,0:T(8,128)(2,1)S(1)}, u32[]{:S(2)}, u32[]{:S(2)}) async-start(bf16[16,304,128]{2,1,0:T(8,128)(2,1)} %get-tuple-element.44), calls=%async_computation.2 | async-start | bytes 2490368 | tf_op jit(solution)/shard_map/all_to_all | solution.py:387
  78.5 0.0 collective-permute-start.14
  78.5 0.5 collective-permute-start.17
  79.0 0.0 collective-permute-done.15.refs_1_.refs_3_
  79.1 0.2 shard_map.76
  79.3 0.1 collective-permute-start.16
  79.4 3.2 %collective-permute-start.18 = (bf16[256,768]{1,0:T(8,128)(2,1)S(1)}, bf16[256,768]{1,0:T(8,128)(2,1)S(1)}, u32[]{:S(2)}, u32[]{:S(2)}) collective-permute-start(bf16[256,768]{1,0:T(8,128)(2,1)S(1)} %get-tuple-element.39), channel_id=1, source_target_pairs={{0,6},{2,0},{4,2},{6,4},{1,7},{3,1},{5,3},{7,5},{8,14},{10,8},{12,... | collective-permute-start | bytes 1179656 | tf_op jit(solution)/shard_map/ppermute | solution.py:379
  82.6 0.0 collective-permute-start.13
  82.6 0.0 collective-permute-done.14.refs_1_
  82.6 0.0 collective-permute-done.17.refs_4_.refs_3_
  82.6 1.0 shard_map.78
  83.6 0.1 collective-permute-start.20
  83.7 1.9 %collective-permute-start.21 = (bf16[256,768]{1,0:T(8,128)(2,1)}, bf16[256,768]{1,0:T(8,128)(2,1)S(1)}, u32[]{:S(2)}, u32[]{:S(2)}) collective-permute-start(bf16[256,768]{1,0:T(8,128)(2,1)} %get-tuple-element.42), channel_id=1, source_target_pairs={{0,2},{2,4},{4,6},{6,0},{1,3},{3,5},{5,7},{7,1},{8,10},{10,12},{12... | collective-permute-start | bytes 1179656 | tf_op jit(solution)/shard_map/ppermute | solution.py:375
  85.6 6.9 %collective-permute-done.16.refs_2_ = bf16[256,768]{1,0:T(8,128)(2,1)S(1)} collective-permute-done((bf16[256,768]{1,0:T(8,128)(2,1)S(1)}, bf16[256,768]{1,0:T(8,128)(2,1)S(1)}, u32[]{:S(2)}, u32[]{:S(2)}) %collective-permute-start.16) | collective-permute-done | bytes 393248 | tf_op jit(solution)/shard_map/ppermute | solution.py:375
  92.6 0.0 collective-permute-done.18.refs_5_
  92.6 1.0 shard_map.77
  93.6 0.0 collective-permute-start.19
  93.6 3.3 %collective-permute-start.22 = (bf16[256,768]{1,0:T(8,128)(2,1)}, bf16[256,768]{1,0:T(8,128)(2,1)}, u32[]{:S(2)}, u32[]{:S(2)}) collective-permute-start(bf16[256,768]{1,0:T(8,128)(2,1)} %get-tuple-element.43), channel_id=1, source_target_pairs={{0,6},{2,0},{4,2},{6,4},{1,7},{3,1},{5,3},{7,5},{8,14},{10,8},{12,... | collective-permute-start | bytes 1179656 | tf_op jit(solution)/shard_map/ppermute | solution.py:379
  96.8 0.0 all-to-all-done.2.y_ref
  96.8 0.3 reduced.1
  97.1 12.4 %all_to_all.32 = bf16[8,8,768]{2,1,0:T(8,128)(2,1)S(1)} all-to-all(bf16[8,8,768]{2,1,0:T(8,128)(2,1)S(1)} %bitcast.16), channel_id=1, replica_groups=mesh['xl'=2,'xh'=2,'y'=4,'z'=4,'c'=2] {'z','c'}, dimensions={0} | all-to-all | bytes 196608 | tf_op jit(solution)/shard_map/all_to_all | solution.py:387
  109.6 4.2 %weight_gradients.1 = (bf16[768,4608]{1,0:T(8,128)(2,1)}, bf16[6,768]{1,0:T(8,128)(2,1)}) custom-call(bf16[8,768]{1,0:T(8,128)(2,1)S(1)} %copy-done.4, bf16[64,768]{1,0:T(8,128)(2,1)S(1)} %bitcast.17), custom_call_target="tpu_custom_call" | custom-call | flops 452984832 | bytes 7077888 | tf_op jit(solution)/shard_map/weight_gradients/pallas_call | solution.py:305
  113.8 0.0 collective-permute-done.13.other_ref
  113.8 0.0 collective-permute-done.20.dl_ref
  113.9 0.0 collective-permute-done.21.uh_ref
  113.9 0.0 collective-permute-done.19.ul_ref
  113.9 0.0 collective-permute-done.22.dh_ref
  113.9 2.3 %document_sum.1 = bf16[512,768]{1,0:T(8,128)(2,1)} custom-call(bf16[512,768]{1,0:T(8,128)(2,1)S(1)} %copy-done.3, bf16[512,768]{1,0:T(8,128)(2,1)S(1)} %collective-permute-done.13.other_ref, bf16[256,768]{1,0:T(8,128)(2,1)S(1)} %collective-permute-done.19.ul_ref, bf16[256,768]{1,0:T(8,128)(2,1)S(1)} %collective-permute-done.20.dl_ref, ...), custom_call_target="tpu_custom_call" | custom-call | flops 1572864 | bytes 3932160 | tf_op jit(solution)/shard_map/document_sum/pallas_call | solution.py:363
  (21 shorter events, 0.0 us)
Async XLA Ops:
  0.6 10.9 %copy-start.5 = (bf16[512,768]{1,0:T(8,128)(2,1)S(1)}, bf16[512,768]{1,0:T(8,128)(2,1)}, u32[]{:S(2)}) copy-start(bf16[512,768]{1,0:T(8,128)(2,1)} %refs_12_.1) | copy-start | bytes 2359300
  6.2 12.0 %all-to-all-start = ((bf16[8,8,768]{2,1,0:T(8,128)(2,1)}), bf16[8,8,768]{2,1,0:T(8,128)(2,1)S(1)}, u32[]{:S(2)}, u32[]{:S(2)}) async-start(bf16[8,8,768]{2,1,0:T(8,128)(2,1)} %bitcast.18), calls=%async_computation | async-start | bytes 196608 | tf_op jit(solution)/shard_map/all_to_all | solution.py:387
  11.5 29.1 %collective-permute-start.12 = (bf16[512,768]{1,0:T(8,128)(2,1)S(1)}, bf16[512,768]{1,0:T(8,128)(2,1)}, u32[]{:S(2)}, u32[]{:S(2)}) collective-permute-start(bf16[512,768]{1,0:T(8,128)(2,1)S(1)} %copy-done.5), channel_id=1, source_target_pairs={{0,1},{1,0},{2,3},{3,2},{4,5},{5,4},{6,7},{7,6},{8,9},{9,8},{10,11... | collective-permute-start | bytes 2359304 | tf_op jit(solution)/shard_map/ppermute | solution.py:383
  12.0 15.4 %collective-permute-start.9 = (bf16[256,768]{1,0:T(8,128)(2,1)}, bf16[256,768]{1,0:T(8,128)(2,1)S(1)}, u32[]{:S(2)}, u32[]{:S(2)}) collective-permute-start(bf16[256,768]{1,0:T(8,128)(2,1)} %get-tuple-element.28), channel_id=1, source_target_pairs={{0,6},{2,0},{4,2},{6,4},{1,7},{3,1},{5,3},{7,5},{8,14},{10,8},{12,... | collective-permute-start | bytes 1179656 | tf_op jit(solution)/shard_map/ppermute | solution.py:379
  14.9 12.6 %collective-permute-start = (bf16[256,768]{1,0:T(8,128)(2,1)}, bf16[256,768]{1,0:T(8,128)(2,1)S(1)}, u32[]{:S(2)}, u32[]{:S(2)}) collective-permute-start(bf16[256,768]{1,0:T(8,128)(2,1)} %get-tuple-element.28), channel_id=1, source_target_pairs={{0,2},{2,4},{4,6},{6,0},{1,3},{3,5},{5,7},{7,1},{8,10},{10,12},{12... | collective-permute-start | bytes 1179656 | tf_op jit(solution)/shard_map/ppermute | solution.py:375
  14.9 17.8 %collective-permute-start.2 = (bf16[256,768]{1,0:T(8,128)(2,1)}, bf16[256,768]{1,0:T(8,128)(2,1)}, u32[]{:S(2)}, u32[]{:S(2)}) collective-permute-start(bf16[256,768]{1,0:T(8,128)(2,1)} %get-tuple-element.29), channel_id=1, source_target_pairs={{0,6},{2,0},{4,2},{6,4},{1,7},{3,1},{5,3},{7,5},{8,14},{10,8},{12,... | collective-permute-start | bytes 1179656 | tf_op jit(solution)/shard_map/ppermute | solution.py:379
  20.0 7.3 %copy-start.7 = (bf16[256,768]{1,0:T(8,128)(2,1)S(1)}, bf16[256,768]{1,0:T(8,128)(2,1)}, u32[]{:S(2)}) copy-start(bf16[256,768]{1,0:T(8,128)(2,1)} %get-tuple-element.29) | copy-start | bytes 1179652
  20.0 29.3 %all-to-all-start.1 = ((bf16[16,304,128]{2,1,0:T(8,128)(2,1)}), bf16[16,304,128]{2,1,0:T(8,128)(2,1)}, u32[]{:S(2)}, u32[]{:S(2)}) async-start(bf16[16,304,128]{2,1,0:T(8,128)(2,1)} %get-tuple-element.27), calls=%async_computation.1 | async-start | bytes 2490368 | tf_op jit(solution)/shard_map/all_to_all | solution.py:387
  27.3 13.3 %collective-permute-start.6 = (bf16[256,768]{1,0:T(8,128)(2,1)S(1)}, bf16[256,768]{1,0:T(8,128)(2,1)S(1)}, u32[]{:S(2)}, u32[]{:S(2)}) collective-permute-start(bf16[256,768]{1,0:T(8,128)(2,1)S(1)} %copy-done.7), channel_id=1, source_target_pairs={{0,2},{2,4},{4,6},{6,0},{1,3},{3,5},{5,7},{7,1},{8,10},{10,12},{12... | collective-permute-start | bytes 1179656 | tf_op jit(solution)/shard_map/ppermute | solution.py:375
  27.4 21.9 %copy-start.6 = (bf16[256,768]{1,0:T(8,128)(2,1)}, bf16[256,768]{1,0:T(8,128)(2,1)S(1)}, u32[]{:S(2)}) copy-start(bf16[256,768]{1,0:T(8,128)(2,1)S(1)} %collective-permute-done.9.refs_8_) | copy-start | bytes 1179652
  27.4 13.7 %collective-permute-start.10 = (bf16[256,768]{1,0:T(8,128)(2,1)S(1)}, bf16[256,768]{1,0:T(8,128)(2,1)S(1)}, u32[]{:S(2)}, u32[]{:S(2)}) collective-permute-start(bf16[256,768]{1,0:T(8,128)(2,1)S(1)} %collective-permute-done.9.refs_8_), channel_id=1, source_target_pairs={{0,1},{1,0},{2,3},{3,2},{4,5},{5,4},{6,7},{7,6},{8,9},{9,8},{10,11... | collective-permute-start | bytes 1179656 | tf_op jit(solution)/shard_map/ppermute | solution.py:383
  27.5 19.5 %collective-permute-start.1 = (bf16[256,768]{1,0:T(8,128)(2,1)S(1)}, bf16[256,768]{1,0:T(8,128)(2,1)S(1)}, u32[]{:S(2)}, u32[]{:S(2)}) collective-permute-start(bf16[256,768]{1,0:T(8,128)(2,1)S(1)} %collective-permute-done.refs_4_), channel_id=1, source_target_pairs={{0,2},{2,4},{4,6},{6,0},{1,3},{3,5},{5,7},{7,1},{8,10},{10,12},{12... | collective-permute-start | bytes 1179656 | tf_op jit(solution)/shard_map/ppermute | solution.py:375
  32.7 14.3 %collective-permute-start.3 = (bf16[256,768]{1,0:T(8,128)(2,1)}, bf16[256,768]{1,0:T(8,128)(2,1)S(1)}, u32[]{:S(2)}, u32[]{:S(2)}) collective-permute-start(bf16[256,768]{1,0:T(8,128)(2,1)} %collective-permute-done.2.refs_9_), channel_id=1, source_target_pairs={{0,6},{2,0},{4,2},{6,4},{1,7},{3,1},{5,3},{7,5},{8,14},{10,8},{12,... | collective-permute-start | bytes 1179656 | tf_op jit(solution)/shard_map/ppermute | solution.py:379
  40.6 7.0 %collective-permute-start.7 = (bf16[256,768]{1,0:T(8,128)(2,1)S(1)}, bf16[256,768]{1,0:T(8,128)(2,1)S(1)}, u32[]{:S(2)}, u32[]{:S(2)}) collective-permute-start(bf16[256,768]{1,0:T(8,128)(2,1)S(1)} %collective-permute-done.refs_4_), channel_id=1, source_target_pairs={{0,1},{1,0},{2,3},{3,2},{4,5},{5,4},{6,7},{7,6},{8,9},{9,8},{10,11... | collective-permute-start | bytes 1179656 | tf_op jit(solution)/shard_map/ppermute | solution.py:383
  40.6 7.0 %collective-permute-start.11 = (bf16[256,768]{1,0:T(8,128)(2,1)}, bf16[256,768]{1,0:T(8,128)(2,1)S(1)}, u32[]{:S(2)}, u32[]{:S(2)}) collective-permute-start(bf16[256,768]{1,0:T(8,128)(2,1)} %collective-permute-done.2.refs_9_), channel_id=1, source_target_pairs={{0,1},{1,0},{2,3},{3,2},{4,5},{5,4},{6,7},{7,6},{8,9},{9,8},{10,11... | collective-permute-start | bytes 1179656 | tf_op jit(solution)/shard_map/ppermute | solution.py:383
  41.1 7.7 %copy-start.8 = (bf16[256,768]{1,0:T(8,128)(2,1)}, bf16[256,768]{1,0:T(8,128)(2,1)S(1)}, u32[]{:S(2)}) copy-start(bf16[256,768]{1,0:T(8,128)(2,1)S(1)} %collective-permute-done.10.refs_10_) | copy-start | bytes 1179652
  41.1 6.5 %collective-permute-start.8 = (bf16[256,768]{1,0:T(8,128)(2,1)S(1)}, bf16[256,768]{1,0:T(8,128)(2,1)S(1)}, u32[]{:S(2)}, u32[]{:S(2)}) collective-permute-start(bf16[256,768]{1,0:T(8,128)(2,1)S(1)} %collective-permute-done.6.refs_5_), channel_id=1, source_target_pairs={{0,1},{1,0},{2,3},{3,2},{4,5},{5,4},{6,7},{7,6},{8,9},{9,8},{10,11... | collective-permute-start | bytes 1179656 | tf_op jit(solution)/shard_map/ppermute | solution.py:383
  47.0 1.7 %collective-permute-start.4 = (bf16[256,768]{1,0:T(8,128)(2,1)S(1)}, bf16[256,768]{1,0:T(8,128)(2,1)S(1)}, u32[]{:S(2)}, u32[]{:S(2)}) collective-permute-start(bf16[256,768]{1,0:T(8,128)(2,1)S(1)} %collective-permute-done.1.refs_0_), channel_id=1, source_target_pairs={{0,1},{1,0},{2,3},{3,2},{4,5},{5,4},{6,7},{7,6},{8,9},{9,8},{10,11... | collective-permute-start | bytes 1179656 | tf_op jit(solution)/shard_map/ppermute | solution.py:383
  47.0 2.3 %collective-permute-start.5 = (bf16[256,768]{1,0:T(8,128)(2,1)S(1)}, bf16[256,768]{1,0:T(8,128)(2,1)S(1)}, u32[]{:S(2)}, u32[]{:S(2)}) collective-permute-start(bf16[256,768]{1,0:T(8,128)(2,1)S(1)} %collective-permute-done.3.refs_1_), channel_id=1, source_target_pairs={{0,1},{1,0},{2,3},{3,2},{4,5},{5,4},{6,7},{7,6},{8,9},{9,8},{10,11... | collective-permute-start | bytes 1179656 | tf_op jit(solution)/shard_map/ppermute | solution.py:383
  47.6 1.2 %copy-start.10 = (bf16[256,768]{1,0:T(8,128)(2,1)}, bf16[256,768]{1,0:T(8,128)(2,1)S(1)}, u32[]{:S(2)}) copy-start(bf16[256,768]{1,0:T(8,128)(2,1)S(1)} %collective-permute-done.8.refs_7_) | copy-start | bytes 1179652
  47.6 1.2 %copy-start.9 = (bf16[256,768]{1,0:T(8,128)(2,1)}, bf16[256,768]{1,0:T(8,128)(2,1)S(1)}, u32[]{:S(2)}) copy-start(bf16[256,768]{1,0:T(8,128)(2,1)S(1)} %collective-permute-done.11.refs_11_) | copy-start | bytes 1179652
  71.0 8.1 %collective-permute-start.15 = (bf16[512,768]{1,0:T(8,128)(2,1)}, bf16[512,768]{1,0:T(8,128)(2,1)S(1)}, u32[]{:S(2)}, u32[]{:S(2)}) collective-permute-start(bf16[512,768]{1,0:T(8,128)(2,1)} %get-tuple-element.35), channel_id=1, source_target_pairs={{0,1},{1,0},{2,3},{3,2},{4,5},{5,4},{6,7},{7,6},{8,9},{9,8},{10,11... | collective-permute-start | bytes 2359304 | tf_op jit(solution)/shard_map/ppermute | solution.py:383
  71.2 7.9 %copy-start = (bf16[512,768]{1,0:T(8,128)(2,1)S(1)}, bf16[512,768]{1,0:T(8,128)(2,1)}, u32[]{:S(2)}) copy-start(bf16[512,768]{1,0:T(8,128)(2,1)} %get-tuple-element.34.refs_0_.refs_2_) | copy-start | bytes 2359300
  71.2 25.6 %all-to-all-start.2 = ((bf16[16,304,128]{2,1,0:T(8,128)(2,1)}), bf16[16,304,128]{2,1,0:T(8,128)(2,1)S(1)}, u32[]{:S(2)}, u32[]{:S(2)}) async-start(bf16[16,304,128]{2,1,0:T(8,128)(2,1)} %get-tuple-element.44), calls=%async_computation.2 | async-start | bytes 2490368 | tf_op jit(solution)/shard_map/all_to_all | solution.py:387
  78.5 4.1 %collective-permute-start.14 = (bf16[512,768]{1,0:T(8,128)(2,1)}, bf16[512,768]{1,0:T(8,128)(2,1)S(1)}, u32[]{:S(2)}, u32[]{:S(2)}) collective-permute-start(bf16[512,768]{1,0:T(8,128)(2,1)} %get-tuple-element.33), channel_id=1, source_target_pairs={{0,1},{1,0},{2,3},{3,2},{4,5},{5,4},{6,7},{7,6},{8,9},{9,8},{10,11... | collective-permute-start | bytes 2359304 | tf_op jit(solution)/shard_map/ppermute | solution.py:383
  78.5 4.1 %collective-permute-start.17 = (bf16[512,768]{1,0:T(8,128)(2,1)}, bf16[512,768]{1,0:T(8,128)(2,1)S(1)}, u32[]{:S(2)}, u32[]{:S(2)}) collective-permute-start(bf16[512,768]{1,0:T(8,128)(2,1)} %get-tuple-element.38), channel_id=1, source_target_pairs={{0,1},{1,0},{2,3},{3,2},{4,5},{5,4},{6,7},{7,6},{8,9},{9,8},{10,11... | collective-permute-start | bytes 2359304 | tf_op jit(solution)/shard_map/ppermute | solution.py:383
  79.0 3.6 %copy-start.1 = (bf16[512,768]{1,0:T(8,128)(2,1)S(1)}, bf16[512,768]{1,0:T(8,128)(2,1)}, u32[]{:S(2)}) copy-start(bf16[512,768]{1,0:T(8,128)(2,1)} %get-tuple-element.37.refs_3_.refs_2_) | copy-start | bytes 2359300
  79.0 3.6 %copy-start.2 = (bf16[512,768]{1,0:T(8,128)(2,1)S(1)}, bf16[512,768]{1,0:T(8,128)(2,1)}, u32[]{:S(2)}) copy-start(bf16[512,768]{1,0:T(8,128)(2,1)} %get-tuple-element.32.refs_0_) | copy-start | bytes 2359300
  79.3 13.3 %collective-permute-start.16 = (bf16[256,768]{1,0:T(8,128)(2,1)S(1)}, bf16[256,768]{1,0:T(8,128)(2,1)S(1)}, u32[]{:S(2)}, u32[]{:S(2)}) collective-permute-start(bf16[256,768]{1,0:T(8,128)(2,1)S(1)} %get-tuple-element.36), channel_id=1, source_target_pairs={{0,2},{2,4},{4,6},{6,0},{1,3},{3,5},{5,7},{7,1},{8,10},{10,12},{12... | collective-permute-start | bytes 1179656 | tf_op jit(solution)/shard_map/ppermute | solution.py:375
  79.4 13.2 %collective-permute-start.18 = (bf16[256,768]{1,0:T(8,128)(2,1)S(1)}, bf16[256,768]{1,0:T(8,128)(2,1)S(1)}, u32[]{:S(2)}, u32[]{:S(2)}) collective-permute-start(bf16[256,768]{1,0:T(8,128)(2,1)S(1)} %get-tuple-element.39), channel_id=1, source_target_pairs={{0,6},{2,0},{4,2},{6,4},{1,7},{3,1},{5,3},{7,5},{8,14},{10,8},{12,... | collective-permute-start | bytes 1179656 | tf_op jit(solution)/shard_map/ppermute | solution.py:379
  82.6 31.2 %collective-permute-start.13 = (bf16[512,768]{1,0:T(8,128)(2,1)}, bf16[512,768]{1,0:T(8,128)(2,1)S(1)}, u32[]{:S(2)}, u32[]{:S(2)}) collective-permute-start(bf16[512,768]{1,0:T(8,128)(2,1)} %get-tuple-element.31), channel_id=1, source_target_pairs={{0,1},{1,0},{2,3},{3,2},{4,5},{5,4},{6,7},{7,6},{8,9},{9,8},{10,11... | collective-permute-start | bytes 2359304 | tf_op jit(solution)/shard_map/ppermute | solution.py:383
  83.6 30.2 %collective-permute-start.20 = (bf16[256,768]{1,0:T(8,128)(2,1)}, bf16[256,768]{1,0:T(8,128)(2,1)S(1)}, u32[]{:S(2)}, u32[]{:S(2)}) collective-permute-start(bf16[256,768]{1,0:T(8,128)(2,1)} %get-tuple-element.41), channel_id=1, source_target_pairs={{0,6},{2,0},{4,2},{6,4},{1,7},{3,1},{5,3},{7,5},{8,14},{10,8},{12,... | collective-permute-start | bytes 1179656 | tf_op jit(solution)/shard_map/ppermute | solution.py:379
  83.7 30.2 %collective-permute-start.21 = (bf16[256,768]{1,0:T(8,128)(2,1)}, bf16[256,768]{1,0:T(8,128)(2,1)S(1)}, u32[]{:S(2)}, u32[]{:S(2)}) collective-permute-start(bf16[256,768]{1,0:T(8,128)(2,1)} %get-tuple-element.42), channel_id=1, source_target_pairs={{0,2},{2,4},{4,6},{6,0},{1,3},{3,5},{5,7},{7,1},{8,10},{10,12},{12... | collective-permute-start | bytes 1179656 | tf_op jit(solution)/shard_map/ppermute | solution.py:375
  93.6 16.0 %copy-start.4 = (bf16[8,768]{1,0:T(8,128)(2,1)S(1)}, bf16[8,768]{1,0:T(8,128)(2,1)}, u32[]{:S(2)}) copy-start(bf16[8,768]{1,0:T(8,128)(2,1)} %q_ref.3) | copy-start | bytes 36868
  93.6 20.3 %collective-permute-start.19 = (bf16[256,768]{1,0:T(8,128)(2,1)}, bf16[256,768]{1,0:T(8,128)(2,1)S(1)}, u32[]{:S(2)}, u32[]{:S(2)}) collective-permute-start(bf16[256,768]{1,0:T(8,128)(2,1)} %get-tuple-element.40), channel_id=1, source_target_pairs={{0,2},{2,4},{4,6},{6,0},{1,3},{3,5},{5,7},{7,1},{8,10},{10,12},{12... | collective-permute-start | bytes 1179656 | tf_op jit(solution)/shard_map/ppermute | solution.py:375
  93.6 20.3 %collective-permute-start.22 = (bf16[256,768]{1,0:T(8,128)(2,1)}, bf16[256,768]{1,0:T(8,128)(2,1)}, u32[]{:S(2)}, u32[]{:S(2)}) collective-permute-start(bf16[256,768]{1,0:T(8,128)(2,1)} %get-tuple-element.43), channel_id=1, source_target_pairs={{0,6},{2,0},{4,2},{6,4},{1,7},{3,1},{5,3},{7,5},{8,14},{10,8},{12,... | collective-permute-start | bytes 1179656 | tf_op jit(solution)/shard_map/ppermute | solution.py:379
  97.1 16.8 %copy-start.3 = (bf16[512,768]{1,0:T(8,128)(2,1)S(1)}, bf16[512,768]{1,0:T(8,128)(2,1)}, u32[]{:S(2)}) copy-start(bf16[512,768]{1,0:T(8,128)(2,1)} %get-tuple-element.30.mine_ref) | copy-start | bytes 2359300

commit v3 on v2

--- a/solution.py
+++ b/solution.py
@@ -18,7 +18,7 @@
 CHIPS = 16
 CHUNK = 48
 DOCS = 512
-WIRE = 304
+WIRE = 296
 TALL = 128
 SCALE = D ** (-0.5)
 F32 = jnp.float32
@@ -110,14 +110,14 @@
     spread = mm(r[:, 0:128], one_hot((m % 6 == l) & (l < 6) & (m < CHUNK)))
     spread = jnp.where((lane // 6 == row // 8) & (row % 8 == 6), spread, 0.0)
     bias = jnp.sum(spread, axis=0, keepdims=True)
-    bias = jnp.where(iota((16, 128), 0) == 0, bias, 0.0).astype(BF16)
+    bias = jnp.where(iota((8, 128), 0) == 0, bias, 0.0).astype(BF16)
     for chip in range(CHIPS):
         for rb in range(3):
             for cb in range(6):
                 out_ref[chip, (rb * 6 + cb) * 16 : (rb * 6 + cb + 1) * 16, :] = rows[
                     rb * 16 : (rb + 1) * 16, cb * 128 : (cb + 1) * 128
                 ]
-        out_ref[chip, 288:304, :] = bias
+        out_ref[chip, 288:296, :] = bias
     row8, col8 = iota((64, 8), 0), iota((64, 8), 1)
     pick = jnp.zeros((64, 8), F32)
     for k in range(8):
@@ -162,7 +162,7 @@
     chip_row = iota((CHIPS, 128), 0)
     pieces = jnp.zeros((CHIPS, 128), F32)
     for chip in range(CHIPS):
-        piece = g_ref[chip, 288:304, :].astype(F32)[0:1, :]
+        piece = g_ref[chip, 288:296, :].astype(F32)[0:1, :]
         pieces = jnp.where(chip_row == chip, piece, pieces)
     l, j = iota((128, D), 0), iota((128, D), 1)
     spread = mm(pieces.astype(BF16), one_hot((j % CHUNK == l) & (l < CHUNK)))
@@ -183,9 +183,10 @@
         tgt = tgt_ref[block(n % 2, half)]
         tgt = jnp.sum(jnp.where(iota((half, 8), 1) == n // 2, tgt, 0.0), axis=1, keepdims=True)
         scores = jnp.sum(jnp.maximum(preact, 0.0), axis=1, keepdims=True) * SCALE
-        back = jnp.where(preact > 0, (scores - tgt) * SCALE, 0.0).astype(BF16)
-        bbuf[block(n, half)] = back
-        bacc[...] += jnp.sum(back.astype(F32).reshape(-1, 8, D), axis=0)
+        errors = ((scores - tgt) * SCALE).astype(BF16).astype(F32)
+        back = jnp.where(preact > 0, errors, 0.0)
+        bbuf[block(n, half)] = back.astype(BF16)
+        bacc[...] += jnp.sum(back.reshape(-1, 8, D), axis=0)
 
     product(0)
     for n in range(steps):
@@ -193,10 +194,10 @@
             product(n + 1)
         errors_of(n)
 
-    for n in range(4):
-        rows = block(n, 2 * DOCS)
+    for n in range(2):
+        rows = block(n, 4 * DOCS)
         pbuf[rows] = mm(bbuf[rows], layer[...], NT).astype(BF16)
-        for k in (2 * n, 2 * n + 1):
+        for k in range(4 * n, 4 * n + 4):
             pltpu.make_async_copy(pbuf.at[block(k)], outs[k], out_sem.at[k]).start()
 
     grad = mm(dbuf[...], bbuf[...], TN).astype(BF16)
@@ -214,10 +215,10 @@
     fold = one_hot((j % CHUNK == l) & (l < CHUNK))
     high = mm(jnp.where(own, high.astype(F32), 0.0).astype(BF16), fold)
     low = mm(jnp.where(own, low.astype(F32), 0.0).astype(BF16), fold)
-    sub = iota((16, 128), 0)
+    sub = iota((8, 128), 0)
     for chip in range(CHIPS):
         tile = jnp.where(sub == 0, high[chip : chip + 1], jnp.where(sub == 1, low[chip : chip + 1], 0.0))
-        lg_ref[chip, 288:304, :] = tile.astype(BF16)
+        lg_ref[chip, 288:296, :] = tile.astype(BF16)
     for n in range(8):
         pltpu.make_async_copy(pbuf.at[block(n)], outs[n], out_sem.at[n]).wait()
 
@@ -263,7 +264,7 @@
     ).astype(BF16)
     a, b = iota((64, CHUNK), 0), iota((64, CHUNK), 1)
     pieces = mm(one_hot((b // 6 == a // 8) & (b % 6 == a % 8)), rows)
-    bias = jnp.sum(total[288:304], axis=0, keepdims=True).astype(BF16).astype(F32)
+    bias = jnp.sum(total[288:296], axis=0, keepdims=True).astype(BF16).astype(F32)
     row, lane = iota((64, 128), 0), iota((64, 128), 1)
     mine = jnp.where((lane // 6 == row // 8) & (row % 8 == 6) & (lane < CHUNK), bias, 0.0)
     m, l = iota((128, 128), 0), iota((128, 128), 1)

time: 117 us -> 117 us (level)
  no operation moved by 1% of the time
where the time goes in v3:
time: 117 us; the launch traced here: 116 us
  starting transfers between devices  40.7 us (35%)
  Pallas kernels  37.6 us (32%)
  waiting for transfers between devices  24 us (21%)
  blocking collectives  12.4 us (11%)
    pallas_call x1, Pallas kernels, gradients(): pl.pallas_call(main_kernel, in_specs=[vmem, vmem] + [hbm] * 14, out_specs...  21.2 us
    all_to_all x3, starting transfers between devices, exchange(): return lax.all_to_all(a, axes, split_axis=0, concat_axis=0, tiled=True)  20 us
    ppermute x6, waiting for transfers between devices, up(): return lax.ppermute(a, 'z', [(i, (i + 1) % 4) for i in range(4)])  17.1 us
    ppermute x6, starting transfers between devices, down(): return lax.ppermute(a, 'z', [(i, (i + 3) % 4) for i in range(4)])  16.2 us
    all_to_all x1, blocking collectives, exchange(): return lax.all_to_all(a, axes, split_axis=0, concat_axis=0, tiled=True)  12.4 us
    pallas_call x1, Pallas kernels, generate(): pl.pallas_call(gen_kernel, in_specs=[vmem, hbm, vmem, vmem, hbm], out_spe...  5.56 us
    ppermute x6, waiting for transfers between devices, down(): return lax.ppermute(a, 'z', [(i, (i + 3) % 4) for i in range(4)])  5.15 us
    pallas_call x1, Pallas kernels, weight_gradients(): pl.pallas_call(weight_kernel, in_specs=[vmem, vmem], out_specs=[pl.BlockS...  4.23 us
  transfers between devices with their start and end apart: 26, of which 6 were waited for; matrix products, arithmetic and copies ran while one was open for 0% of the time, Pallas kernels for 7%

profile of v3, /device:TPU:24, one launch (start us, length us, event | category | flops | bytes accessed | tf_op | source)
XLA Modules:
  0.0 115.8 jit_solution(12619415178943524506)
XLA Ops:
  0.6 0.0 copy-start.5
  0.6 5.6 %generate.1 = (bf16[64,768]{1,0:T(8,128)(2,1)}, bf16[256,768]{1,0:T(8,128)(2,1)}, bf16[256,768]{1,0:T(8,128)(2,1)}) custom-call(bf16[8,768]{1,0:T(8,128)(2,1)} %q_ref.3, bf16[768,4608]{1,0:T(8,128)(2,1)} %w_ref.1, bf16[6,768]{1,0:T(8,128)(2,1)} %bitcast.19, bf16[8,512]{1,0:T(8,128)(2,1)} %bitcast.20, bf16[512,768]{1,0:T(8,128)(2,1)} %refs_12_.1), custom_call_target="tpu_custom_call" | custom-call | flops 452984832 | bytes 7077888 | tf_op jit(solution)/shard_map/generate/pallas_call | solution.py:85
  6.2 5.3 %all-to-all-start = ((bf16[8,8,768]{2,1,0:T(8,128)(2,1)}), bf16[8,8,768]{2,1,0:T(8,128)(2,1)S(1)}, u32[]{:S(2)}, u32[]{:S(2)}) async-start(bf16[8,8,768]{2,1,0:T(8,128)(2,1)} %bitcast.18), calls=%async_computation | async-start | bytes 196608 | tf_op jit(solution)/shard_map/all_to_all | solution.py:388
  11.5 0.5 collective-permute-start.12
  12.0 2.8 %collective-permute-start.9 = (bf16[256,768]{1,0:T(8,128)(2,1)}, bf16[256,768]{1,0:T(8,128)(2,1)S(1)}, u32[]{:S(2)}, u32[]{:S(2)}) collective-permute-start(bf16[256,768]{1,0:T(8,128)(2,1)} %get-tuple-element.28), channel_id=1, source_target_pairs={{0,6},{2,0},{4,2},{6,4},{1,7},{3,1},{5,3},{7,5},{8,14},{10,8},{12,... | collective-permute-start | bytes 1179656 | tf_op jit(solution)/shard_map/ppermute | solution.py:380
  14.9 0.0 collective-permute-start
  14.9 3.2 %collective-permute-start.2 = (bf16[256,768]{1,0:T(8,128)(2,1)}, bf16[256,768]{1,0:T(8,128)(2,1)}, u32[]{:S(2)}, u32[]{:S(2)}) collective-permute-start(bf16[256,768]{1,0:T(8,128)(2,1)} %get-tuple-element.29), channel_id=1, source_target_pairs={{0,6},{2,0},{4,2},{6,4},{1,7},{3,1},{5,3},{7,5},{8,14},{10,8},{12,... | collective-permute-start | bytes 1179656 | tf_op jit(solution)/shard_map/ppermute | solution.py:380
  18.1 0.1 stack.35.src_ref
  18.2 0.0 all-to-all-done
  18.2 1.8 %assemble.1 = (bf16[16,296,128]{2,1,0:T(8,128)(2,1)}, f32[512,8]{1,0:T(8,128)S(1)}) custom-call(s32[8]{0:T(128)S(1)} %stack.35.src_ref, bf16[64,768]{1,0:T(8,128)(2,1)S(1)} %bitcast.15), custom_call_target="tpu_custom_call" | custom-call | tf_op jit(solution)/shard_map/assemble/pallas_call | solution.py:129
  20.0 7.3 %all-to-all-start.1 = ((bf16[16,296,128]{2,1,0:T(8,128)(2,1)}), bf16[16,296,128]{2,1,0:T(8,128)(2,1)}, u32[]{:S(2)}, u32[]{:S(2)}) async-start(bf16[16,296,128]{2,1,0:T(8,128)(2,1)} %get-tuple-element.27), calls=%async_computation.1 | async-start | bytes 2424832 | tf_op jit(solution)/shard_map/all_to_all | solution.py:388
  27.3 0.1 collective-permute-start.6
  27.4 0.0 collective-permute-done.9.refs_8_
  27.4 0.1 collective-permute-start.10
  27.5 0.0 collective-permute-done.refs_4_
  27.5 0.1 collective-permute-start.1
  27.6 5.1 %collective-permute-done.2.refs_9_ = bf16[256,768]{1,0:T(8,128)(2,1)} collective-permute-done((bf16[256,768]{1,0:T(8,128)(2,1)}, bf16[256,768]{1,0:T(8,128)(2,1)}, u32[]{:S(2)}, u32[]{:S(2)}) %collective-permute-start.2) | collective-permute-done | bytes 393248 | tf_op jit(solution)/shard_map/ppermute | solution.py:380
  32.7 3.5 %collective-permute-start.3 = (bf16[256,768]{1,0:T(8,128)(2,1)}, bf16[256,768]{1,0:T(8,128)(2,1)S(1)}, u32[]{:S(2)}, u32[]{:S(2)}) collective-permute-start(bf16[256,768]{1,0:T(8,128)(2,1)} %collective-permute-done.2.refs_9_), channel_id=1, source_target_pairs={{0,6},{2,0},{4,2},{6,4},{1,7},{3,1},{5,3},{7,5},{8,14},{10,8},{12,... | collective-permute-start | bytes 1179656 | tf_op jit(solution)/shard_map/ppermute | solution.py:380
  36.3 4.3 %collective-permute-done.6.refs_5_ = bf16[256,768]{1,0:T(8,128)(2,1)S(1)} collective-permute-done((bf16[256,768]{1,0:T(8,128)(2,1)S(1)}, bf16[256,768]{1,0:T(8,128)(2,1)S(1)}, u32[]{:S(2)}, u32[]{:S(2)}) %collective-permute-start.6) | collective-permute-done | bytes 393248 | tf_op jit(solution)/shard_map/ppermute | solution.py:376
  40.6 0.0 collective-permute-start.7
  40.6 0.0 collective-permute-done.12.refs_13_
  40.6 0.5 collective-permute-start.11
  41.1 0.0 collective-permute-done.10.refs_10_
  41.1 0.1 collective-permute-start.8
  41.2 5.8 %collective-permute-done.1.refs_0_ = bf16[256,768]{1,0:T(8,128)(2,1)S(1)} collective-permute-done((bf16[256,768]{1,0:T(8,128)(2,1)S(1)}, bf16[256,768]{1,0:T(8,128)(2,1)S(1)}, u32[]{:S(2)}, u32[]{:S(2)}) %collective-permute-start.1) | collective-permute-done | bytes 393248 | tf_op jit(solution)/shard_map/ppermute | solution.py:376
  47.0 0.0 collective-permute-start.4
  47.0 0.0 collective-permute-done.3.refs_1_
  47.0 0.5 collective-permute-start.5
  47.5 0.0 collective-permute-done.7.refs_6_
  47.6 0.0 collective-permute-done.8.refs_7_
  47.6 0.0 collective-permute-done.11.refs_11_
  47.6 1.2 %collective-permute-done.4.refs_2_ = bf16[256,768]{1,0:T(8,128)(2,1)S(1)} collective-permute-done((bf16[256,768]{1,0:T(8,128)(2,1)S(1)}, bf16[256,768]{1,0:T(8,128)(2,1)S(1)}, u32[]{:S(2)}, u32[]{:S(2)}) %collective-permute-start.4) | collective-permute-done | bytes 393248 | tf_op jit(solution)/shard_map/ppermute | solution.py:384
  48.8 0.6 collective-permute-done.5.refs_3_
  49.3 0.0 all-to-all-done.1.g_ref
  49.3 21.2 %gradients.1 = (bf16[512,768]{1,0:T(8,128)(2,1)}, bf16[512,768]{1,0:T(8,128)(2,1)}, bf16[512,768]{1,0:T(8,128)(2,1)}, bf16[512,768]{1,0:T(8,128)(2,1)}, bf16[512...) custom-call(f32[512,8]{1,0:T(8,128)S(1)} %get-tuple-element.26.tgt_r, ...), custom_call_target="tpu_custom_call" | custom-call | flops 14495514624 | bytes 12582912 | tf_op jit(solution)/shard_map/gradients/pallas_call | solution.py:229
  70.6 0.2 collective-permute-start.15
  70.8 7.4 %all-to-all-start.2 = ((bf16[16,296,128]{2,1,0:T(8,128)(2,1)}), bf16[16,296,128]{2,1,0:T(8,128)(2,1)S(1)}, u32[]{:S(2)}, u32[]{:S(2)}) async-start(bf16[16,296,128]{2,1,0:T(8,128)(2,1)} %get-tuple-element.44), calls=%async_computation.2 | async-start | bytes 2424832 | tf_op jit(solution)/shard_map/all_to_all | solution.py:388
  78.1 0.0 collective-permute-start.14
  78.1 0.5 collective-permute-start.17
  78.6 0.0 collective-permute-done.15.refs_1_.refs_3_
  78.7 0.2 shard_map.76
  78.9 0.1 collective-permute-start.16
  79.0 3.2 %collective-permute-start.18 = (bf16[256,768]{1,0:T(8,128)(2,1)S(1)}, bf16[256,768]{1,0:T(8,128)(2,1)S(1)}, u32[]{:S(2)}, u32[]{:S(2)}) collective-permute-start(bf16[256,768]{1,0:T(8,128)(2,1)S(1)} %get-tuple-element.39), channel_id=1, source_target_pairs={{0,6},{2,0},{4,2},{6,4},{1,7},{3,1},{5,3},{7,5},{8,14},{10,8},{12,... | collective-permute-start | bytes 1179656 | tf_op jit(solution)/shard_map/ppermute | solution.py:380
  82.2 0.0 collective-permute-start.13
  82.2 0.0 collective-permute-done.14.refs_1_
  82.2 0.0 collective-permute-done.17.refs_4_.refs_3_
  82.2 1.0 shard_map.78
  83.2 0.1 collective-permute-start.20
  83.3 1.9 %collective-permute-start.21 = (bf16[256,768]{1,0:T(8,128)(2,1)}, bf16[256,768]{1,0:T(8,128)(2,1)S(1)}, u32[]{:S(2)}, u32[]{:S(2)}) collective-permute-start(bf16[256,768]{1,0:T(8,128)(2,1)} %get-tuple-element.42), channel_id=1, source_target_pairs={{0,2},{2,4},{4,6},{6,0},{1,3},{3,5},{5,7},{7,1},{8,10},{10,12},{12... | collective-permute-start | bytes 1179656 | tf_op jit(solution)/shard_map/ppermute | solution.py:376
  85.2 6.9 %collective-permute-done.16.refs_2_ = bf16[256,768]{1,0:T(8,128)(2,1)S(1)} collective-permute-done((bf16[256,768]{1,0:T(8,128)(2,1)S(1)}, bf16[256,768]{1,0:T(8,128)(2,1)S(1)}, u32[]{:S(2)}, u32[]{:S(2)}) %collective-permute-start.16) | collective-permute-done | bytes 393248 | tf_op jit(solution)/shard_map/ppermute | solution.py:376
  92.2 0.0 collective-permute-done.18.refs_5_
  92.2 1.0 shard_map.77
  93.2 0.0 collective-permute-start.19
  93.2 3.3 %collective-permute-start.22 = (bf16[256,768]{1,0:T(8,128)(2,1)}, bf16[256,768]{1,0:T(8,128)(2,1)}, u32[]{:S(2)}, u32[]{:S(2)}) collective-permute-start(bf16[256,768]{1,0:T(8,128)(2,1)} %get-tuple-element.43), channel_id=1, source_target_pairs={{0,6},{2,0},{4,2},{6,4},{1,7},{3,1},{5,3},{7,5},{8,14},{10,8},{12,... | collective-permute-start | bytes 1179656 | tf_op jit(solution)/shard_map/ppermute | solution.py:380
  96.4 0.0 all-to-all-done.2.y_ref
  96.4 0.3 reduced.1
  96.8 12.4 %all_to_all.32 = bf16[8,8,768]{2,1,0:T(8,128)(2,1)S(1)} all-to-all(bf16[8,8,768]{2,1,0:T(8,128)(2,1)S(1)} %bitcast.16), channel_id=1, replica_groups=mesh['xl'=2,'xh'=2,'y'=4,'z'=4,'c'=2] {'z','c'}, dimensions={0} | all-to-all | bytes 196608 | tf_op jit(solution)/shard_map/all_to_all | solution.py:388
  109.2 4.2 %weight_gradients.1 = (bf16[768,4608]{1,0:T(8,128)(2,1)}, bf16[6,768]{1,0:T(8,128)(2,1)}) custom-call(bf16[8,768]{1,0:T(8,128)(2,1)S(1)} %copy-done.4, bf16[64,768]{1,0:T(8,128)(2,1)S(1)} %bitcast.17), custom_call_target="tpu_custom_call" | custom-call | flops 452984832 | bytes 7077888 | tf_op jit(solution)/shard_map/weight_gradients/pallas_call | solution.py:306
  113.4 0.0 collective-permute-done.13.other_ref
  113.4 0.0 collective-permute-done.20.dl_ref
  113.5 0.0 collective-permute-done.21.uh_ref
  113.5 0.0 collective-permute-done.19.ul_ref
  113.5 0.0 collective-permute-done.22.dh_ref
  113.5 2.3 %document_sum.1 = bf16[512,768]{1,0:T(8,128)(2,1)} custom-call(bf16[512,768]{1,0:T(8,128)(2,1)S(1)} %copy-done.3, bf16[512,768]{1,0:T(8,128)(2,1)S(1)} %collective-permute-done.13.other_ref, bf16[256,768]{1,0:T(8,128)(2,1)S(1)} %collective-permute-done.19.ul_ref, bf16[256,768]{1,0:T(8,128)(2,1)S(1)} %collective-permute-done.20.dl_ref, ...), custom_call_target="tpu_custom_call" | custom-call | flops 1572864 | bytes 3932160 | tf_op jit(solution)/shard_map/document_sum/pallas_call | solution.py:364
  (21 shorter events, 0.0 us)
Async XLA Ops:
  0.6 10.9 %copy-start.5 = (bf16[512,768]{1,0:T(8,128)(2,1)S(1)}, bf16[512,768]{1,0:T(8,128)(2,1)}, u32[]{:S(2)}) copy-start(bf16[512,768]{1,0:T(8,128)(2,1)} %refs_12_.1) | copy-start | bytes 2359300
  6.2 12.0 %all-to-all-start = ((bf16[8,8,768]{2,1,0:T(8,128)(2,1)}), bf16[8,8,768]{2,1,0:T(8,128)(2,1)S(1)}, u32[]{:S(2)}, u32[]{:S(2)}) async-start(bf16[8,8,768]{2,1,0:T(8,128)(2,1)} %bitcast.18), calls=%async_computation | async-start | bytes 196608 | tf_op jit(solution)/shard_map/all_to_all | solution.py:388
  11.5 29.0 %collective-permute-start.12 = (bf16[512,768]{1,0:T(8,128)(2,1)S(1)}, bf16[512,768]{1,0:T(8,128)(2,1)}, u32[]{:S(2)}, u32[]{:S(2)}) collective-permute-start(bf16[512,768]{1,0:T(8,128)(2,1)S(1)} %copy-done.5), channel_id=1, source_target_pairs={{0,1},{1,0},{2,3},{3,2},{4,5},{5,4},{6,7},{7,6},{8,9},{9,8},{10,11... | collective-permute-start | bytes 2359304 | tf_op jit(solution)/shard_map/ppermute | solution.py:384
  12.0 15.4 %collective-permute-start.9 = (bf16[256,768]{1,0:T(8,128)(2,1)}, bf16[256,768]{1,0:T(8,128)(2,1)S(1)}, u32[]{:S(2)}, u32[]{:S(2)}) collective-permute-start(bf16[256,768]{1,0:T(8,128)(2,1)} %get-tuple-element.28), channel_id=1, source_target_pairs={{0,6},{2,0},{4,2},{6,4},{1,7},{3,1},{5,3},{7,5},{8,14},{10,8},{12,... | collective-permute-start | bytes 1179656 | tf_op jit(solution)/shard_map/ppermute | solution.py:380
  14.9 12.6 %collective-permute-start = (bf16[256,768]{1,0:T(8,128)(2,1)}, bf16[256,768]{1,0:T(8,128)(2,1)S(1)}, u32[]{:S(2)}, u32[]{:S(2)}) collective-permute-start(bf16[256,768]{1,0:T(8,128)(2,1)} %get-tuple-element.28), channel_id=1, source_target_pairs={{0,2},{2,4},{4,6},{6,0},{1,3},{3,5},{5,7},{7,1},{8,10},{10,12},{12... | collective-permute-start | bytes 1179656 | tf_op jit(solution)/shard_map/ppermute | solution.py:376
  14.9 17.8 %collective-permute-start.2 = (bf16[256,768]{1,0:T(8,128)(2,1)}, bf16[256,768]{1,0:T(8,128)(2,1)}, u32[]{:S(2)}, u32[]{:S(2)}) collective-permute-start(bf16[256,768]{1,0:T(8,128)(2,1)} %get-tuple-element.29), channel_id=1, source_target_pairs={{0,6},{2,0},{4,2},{6,4},{1,7},{3,1},{5,3},{7,5},{8,14},{10,8},{12,... | collective-permute-start | bytes 1179656 | tf_op jit(solution)/shard_map/ppermute | solution.py:380
  20.0 7.3 %copy-start.7 = (bf16[256,768]{1,0:T(8,128)(2,1)S(1)}, bf16[256,768]{1,0:T(8,128)(2,1)}, u32[]{:S(2)}) copy-start(bf16[256,768]{1,0:T(8,128)(2,1)} %get-tuple-element.29) | copy-start | bytes 1179652
  20.0 29.3 %all-to-all-start.1 = ((bf16[16,296,128]{2,1,0:T(8,128)(2,1)}), bf16[16,296,128]{2,1,0:T(8,128)(2,1)}, u32[]{:S(2)}, u32[]{:S(2)}) async-start(bf16[16,296,128]{2,1,0:T(8,128)(2,1)} %get-tuple-element.27), calls=%async_computation.1 | async-start | bytes 2424832 | tf_op jit(solution)/shard_map/all_to_all | solution.py:388
  27.3 13.3 %collective-permute-start.6 = (bf16[256,768]{1,0:T(8,128)(2,1)S(1)}, bf16[256,768]{1,0:T(8,128)(2,1)S(1)}, u32[]{:S(2)}, u32[]{:S(2)}) collective-permute-start(bf16[256,768]{1,0:T(8,128)(2,1)S(1)} %copy-done.7), channel_id=1, source_target_pairs={{0,2},{2,4},{4,6},{6,0},{1,3},{3,5},{5,7},{7,1},{8,10},{10,12},{12... | collective-permute-start | bytes 1179656 | tf_op jit(solution)/shard_map/ppermute | solution.py:376
  27.4 21.9 %copy-start.6 = (bf16[256,768]{1,0:T(8,128)(2,1)}, bf16[256,768]{1,0:T(8,128)(2,1)S(1)}, u32[]{:S(2)}) copy-start(bf16[256,768]{1,0:T(8,128)(2,1)S(1)} %collective-permute-done.9.refs_8_) | copy-start | bytes 1179652
  27.4 13.7 %collective-permute-start.10 = (bf16[256,768]{1,0:T(8,128)(2,1)S(1)}, bf16[256,768]{1,0:T(8,128)(2,1)S(1)}, u32[]{:S(2)}, u32[]{:S(2)}) collective-permute-start(bf16[256,768]{1,0:T(8,128)(2,1)S(1)} %collective-permute-done.9.refs_8_), channel_id=1, source_target_pairs={{0,1},{1,0},{2,3},{3,2},{4,5},{5,4},{6,7},{7,6},{8,9},{9,8},{10,11... | collective-permute-start | bytes 1179656 | tf_op jit(solution)/shard_map/ppermute | solution.py:384
  27.5 19.5 %collective-permute-start.1 = (bf16[256,768]{1,0:T(8,128)(2,1)S(1)}, bf16[256,768]{1,0:T(8,128)(2,1)S(1)}, u32[]{:S(2)}, u32[]{:S(2)}) collective-permute-start(bf16[256,768]{1,0:T(8,128)(2,1)S(1)} %collective-permute-done.refs_4_), channel_id=1, source_target_pairs={{0,2},{2,4},{4,6},{6,0},{1,3},{3,5},{5,7},{7,1},{8,10},{10,12},{12... | collective-permute-start | bytes 1179656 | tf_op jit(solution)/shard_map/ppermute | solution.py:376
  32.7 14.3 %collective-permute-start.3 = (bf16[256,768]{1,0:T(8,128)(2,1)}, bf16[256,768]{1,0:T(8,128)(2,1)S(1)}, u32[]{:S(2)}, u32[]{:S(2)}) collective-permute-start(bf16[256,768]{1,0:T(8,128)(2,1)} %collective-permute-done.2.refs_9_), channel_id=1, source_target_pairs={{0,6},{2,0},{4,2},{6,4},{1,7},{3,1},{5,3},{7,5},{8,14},{10,8},{12,... | collective-permute-start | bytes 1179656 | tf_op jit(solution)/shard_map/ppermute | solution.py:380
  40.6 7.0 %collective-permute-start.7 = (bf16[256,768]{1,0:T(8,128)(2,1)S(1)}, bf16[256,768]{1,0:T(8,128)(2,1)S(1)}, u32[]{:S(2)}, u32[]{:S(2)}) collective-permute-start(bf16[256,768]{1,0:T(8,128)(2,1)S(1)} %collective-permute-done.refs_4_), channel_id=1, source_target_pairs={{0,1},{1,0},{2,3},{3,2},{4,5},{5,4},{6,7},{7,6},{8,9},{9,8},{10,11... | collective-permute-start | bytes 1179656 | tf_op jit(solution)/shard_map/ppermute | solution.py:384
  40.6 7.0 %collective-permute-start.11 = (bf16[256,768]{1,0:T(8,128)(2,1)}, bf16[256,768]{1,0:T(8,128)(2,1)S(1)}, u32[]{:S(2)}, u32[]{:S(2)}) collective-permute-start(bf16[256,768]{1,0:T(8,128)(2,1)} %collective-permute-done.2.refs_9_), channel_id=1, source_target_pairs={{0,1},{1,0},{2,3},{3,2},{4,5},{5,4},{6,7},{7,6},{8,9},{9,8},{10,11... | collective-permute-start | bytes 1179656 | tf_op jit(solution)/shard_map/ppermute | solution.py:384
  41.1 7.7 %copy-start.8 = (bf16[256,768]{1,0:T(8,128)(2,1)}, bf16[256,768]{1,0:T(8,128)(2,1)S(1)}, u32[]{:S(2)}) copy-start(bf16[256,768]{1,0:T(8,128)(2,1)S(1)} %collective-permute-done.10.refs_10_) | copy-start | bytes 1179652
  41.1 6.5 %collective-permute-start.8 = (bf16[256,768]{1,0:T(8,128)(2,1)S(1)}, bf16[256,768]{1,0:T(8,128)(2,1)S(1)}, u32[]{:S(2)}, u32[]{:S(2)}) collective-permute-start(bf16[256,768]{1,0:T(8,128)(2,1)S(1)} %collective-permute-done.6.refs_5_), channel_id=1, source_target_pairs={{0,1},{1,0},{2,3},{3,2},{4,5},{5,4},{6,7},{7,6},{8,9},{9,8},{10,11... | collective-permute-start | bytes 1179656 | tf_op jit(solution)/shard_map/ppermute | solution.py:384
  47.0 1.7 %collective-permute-start.4 = (bf16[256,768]{1,0:T(8,128)(2,1)S(1)}, bf16[256,768]{1,0:T(8,128)(2,1)S(1)}, u32[]{:S(2)}, u32[]{:S(2)}) collective-permute-start(bf16[256,768]{1,0:T(8,128)(2,1)S(1)} %collective-permute-done.1.refs_0_), channel_id=1, source_target_pairs={{0,1},{1,0},{2,3},{3,2},{4,5},{5,4},{6,7},{7,6},{8,9},{9,8},{10,11... | collective-permute-start | bytes 1179656 | tf_op jit(solution)/shard_map/ppermute | solution.py:384
  47.0 2.3 %collective-permute-start.5 = (bf16[256,768]{1,0:T(8,128)(2,1)S(1)}, bf16[256,768]{1,0:T(8,128)(2,1)S(1)}, u32[]{:S(2)}, u32[]{:S(2)}) collective-permute-start(bf16[256,768]{1,0:T(8,128)(2,1)S(1)} %collective-permute-done.3.refs_1_), channel_id=1, source_target_pairs={{0,1},{1,0},{2,3},{3,2},{4,5},{5,4},{6,7},{7,6},{8,9},{9,8},{10,11... | collective-permute-start | bytes 1179656 | tf_op jit(solution)/shard_map/ppermute | solution.py:384
  47.6 1.2 %copy-start.10 = (bf16[256,768]{1,0:T(8,128)(2,1)}, bf16[256,768]{1,0:T(8,128)(2,1)S(1)}, u32[]{:S(2)}) copy-start(bf16[256,768]{1,0:T(8,128)(2,1)S(1)} %collective-permute-done.8.refs_7_) | copy-start | bytes 1179652
  47.6 1.2 %copy-start.9 = (bf16[256,768]{1,0:T(8,128)(2,1)}, bf16[256,768]{1,0:T(8,128)(2,1)S(1)}, u32[]{:S(2)}) copy-start(bf16[256,768]{1,0:T(8,128)(2,1)S(1)} %collective-permute-done.11.refs_11_) | copy-start | bytes 1179652
  70.6 8.1 %collective-permute-start.15 = (bf16[512,768]{1,0:T(8,128)(2,1)}, bf16[512,768]{1,0:T(8,128)(2,1)S(1)}, u32[]{:S(2)}, u32[]{:S(2)}) collective-permute-start(bf16[512,768]{1,0:T(8,128)(2,1)} %get-tuple-element.35), channel_id=1, source_target_pairs={{0,1},{1,0},{2,3},{3,2},{4,5},{5,4},{6,7},{7,6},{8,9},{9,8},{10,11... | collective-permute-start | bytes 2359304 | tf_op jit(solution)/shard_map/ppermute | solution.py:384
  70.8 7.9 %copy-start = (bf16[512,768]{1,0:T(8,128)(2,1)S(1)}, bf16[512,768]{1,0:T(8,128)(2,1)}, u32[]{:S(2)}) copy-start(bf16[512,768]{1,0:T(8,128)(2,1)} %get-tuple-element.34.refs_0_.refs_2_) | copy-start | bytes 2359300
  70.8 25.6 %all-to-all-start.2 = ((bf16[16,296,128]{2,1,0:T(8,128)(2,1)}), bf16[16,296,128]{2,1,0:T(8,128)(2,1)S(1)}, u32[]{:S(2)}, u32[]{:S(2)}) async-start(bf16[16,296,128]{2,1,0:T(8,128)(2,1)} %get-tuple-element.44), calls=%async_computation.2 | async-start | bytes 2424832 | tf_op jit(solution)/shard_map/all_to_all | solution.py:388
  78.1 4.1 %collective-permute-start.14 = (bf16[512,768]{1,0:T(8,128)(2,1)}, bf16[512,768]{1,0:T(8,128)(2,1)S(1)}, u32[]{:S(2)}, u32[]{:S(2)}) collective-permute-start(bf16[512,768]{1,0:T(8,128)(2,1)} %get-tuple-element.33), channel_id=1, source_target_pairs={{0,1},{1,0},{2,3},{3,2},{4,5},{5,4},{6,7},{7,6},{8,9},{9,8},{10,11... | collective-permute-start | bytes 2359304 | tf_op jit(solution)/shard_map/ppermute | solution.py:384
  78.1 4.1 %collective-permute-start.17 = (bf16[512,768]{1,0:T(8,128)(2,1)}, bf16[512,768]{1,0:T(8,128)(2,1)S(1)}, u32[]{:S(2)}, u32[]{:S(2)}) collective-permute-start(bf16[512,768]{1,0:T(8,128)(2,1)} %get-tuple-element.38), channel_id=1, source_target_pairs={{0,1},{1,0},{2,3},{3,2},{4,5},{5,4},{6,7},{7,6},{8,9},{9,8},{10,11... | collective-permute-start | bytes 2359304 | tf_op jit(solution)/shard_map/ppermute | solution.py:384
  78.7 3.6 %copy-start.1 = (bf16[512,768]{1,0:T(8,128)(2,1)S(1)}, bf16[512,768]{1,0:T(8,128)(2,1)}, u32[]{:S(2)}) copy-start(bf16[512,768]{1,0:T(8,128)(2,1)} %get-tuple-element.37.refs_3_.refs_2_) | copy-start | bytes 2359300
  78.7 3.6 %copy-start.2 = (bf16[512,768]{1,0:T(8,128)(2,1)S(1)}, bf16[512,768]{1,0:T(8,128)(2,1)}, u32[]{:S(2)}) copy-start(bf16[512,768]{1,0:T(8,128)(2,1)} %get-tuple-element.32.refs_0_) | copy-start | bytes 2359300
  78.9 13.3 %collective-permute-start.16 = (bf16[256,768]{1,0:T(8,128)(2,1)S(1)}, bf16[256,768]{1,0:T(8,128)(2,1)S(1)}, u32[]{:S(2)}, u32[]{:S(2)}) collective-permute-start(bf16[256,768]{1,0:T(8,128)(2,1)S(1)} %get-tuple-element.36), channel_id=1, source_target_pairs={{0,2},{2,4},{4,6},{6,0},{1,3},{3,5},{5,7},{7,1},{8,10},{10,12},{12... | collective-permute-start | bytes 1179656 | tf_op jit(solution)/shard_map/ppermute | solution.py:376
  79.0 13.2 %collective-permute-start.18 = (bf16[256,768]{1,0:T(8,128)(2,1)S(1)}, bf16[256,768]{1,0:T(8,128)(2,1)S(1)}, u32[]{:S(2)}, u32[]{:S(2)}) collective-permute-start(bf16[256,768]{1,0:T(8,128)(2,1)S(1)} %get-tuple-element.39), channel_id=1, source_target_pairs={{0,6},{2,0},{4,2},{6,4},{1,7},{3,1},{5,3},{7,5},{8,14},{10,8},{12,... | collective-permute-start | bytes 1179656 | tf_op jit(solution)/shard_map/ppermute | solution.py:380
  82.2 31.2 %collective-permute-start.13 = (bf16[512,768]{1,0:T(8,128)(2,1)}, bf16[512,768]{1,0:T(8,128)(2,1)S(1)}, u32[]{:S(2)}, u32[]{:S(2)}) collective-permute-start(bf16[512,768]{1,0:T(8,128)(2,1)} %get-tuple-element.31), channel_id=1, source_target_pairs={{0,1},{1,0},{2,3},{3,2},{4,5},{5,4},{6,7},{7,6},{8,9},{9,8},{10,11... | collective-permute-start | bytes 2359304 | tf_op jit(solution)/shard_map/ppermute | solution.py:384
  83.2 30.2 %collective-permute-start.20 = (bf16[256,768]{1,0:T(8,128)(2,1)}, bf16[256,768]{1,0:T(8,128)(2,1)S(1)}, u32[]{:S(2)}, u32[]{:S(2)}) collective-permute-start(bf16[256,768]{1,0:T(8,128)(2,1)} %get-tuple-element.41), channel_id=1, source_target_pairs={{0,6},{2,0},{4,2},{6,4},{1,7},{3,1},{5,3},{7,5},{8,14},{10,8},{12,... | collective-permute-start | bytes 1179656 | tf_op jit(solution)/shard_map/ppermute | solution.py:380
  83.3 30.2 %collective-permute-start.21 = (bf16[256,768]{1,0:T(8,128)(2,1)}, bf16[256,768]{1,0:T(8,128)(2,1)S(1)}, u32[]{:S(2)}, u32[]{:S(2)}) collective-permute-start(bf16[256,768]{1,0:T(8,128)(2,1)} %get-tuple-element.42), channel_id=1, source_target_pairs={{0,2},{2,4},{4,6},{6,0},{1,3},{3,5},{5,7},{7,1},{8,10},{10,12},{12... | collective-permute-start | bytes 1179656 | tf_op jit(solution)/shard_map/ppermute | solution.py:376
  93.2 16.0 %copy-start.4 = (bf16[8,768]{1,0:T(8,128)(2,1)S(1)}, bf16[8,768]{1,0:T(8,128)(2,1)}, u32[]{:S(2)}) copy-start(bf16[8,768]{1,0:T(8,128)(2,1)} %q_ref.3) | copy-start | bytes 36868
  93.2 20.3 %collective-permute-start.19 = (bf16[256,768]{1,0:T(8,128)(2,1)}, bf16[256,768]{1,0:T(8,128)(2,1)S(1)}, u32[]{:S(2)}, u32[]{:S(2)}) collective-permute-start(bf16[256,768]{1,0:T(8,128)(2,1)} %get-tuple-element.40), channel_id=1, source_target_pairs={{0,2},{2,4},{4,6},{6,0},{1,3},{3,5},{5,7},{7,1},{8,10},{10,12},{12... | collective-permute-start | bytes 1179656 | tf_op jit(solution)/shard_map/ppermute | solution.py:376
  93.2 20.3 %collective-permute-start.22 = (bf16[256,768]{1,0:T(8,128)(2,1)}, bf16[256,768]{1,0:T(8,128)(2,1)}, u32[]{:S(2)}, u32[]{:S(2)}) collective-permute-start(bf16[256,768]{1,0:T(8,128)(2,1)} %get-tuple-element.43), channel_id=1, source_target_pairs={{0,6},{2,0},{4,2},{6,4},{1,7},{3,1},{5,3},{7,5},{8,14},{10,8},{12,... | collective-permute-start | bytes 1179656 | tf_op jit(solution)/shard_map/ppermute | solution.py:380
  96.7 16.7 %copy-start.3 = (bf16[512,768]{1,0:T(8,128)(2,1)S(1)}, bf16[512,768]{1,0:T(8,128)(2,1)}, u32[]{:S(2)}) copy-start(bf16[512,768]{1,0:T(8,128)(2,1)} %get-tuple-element.30.mine_ref) | copy-start | bytes 2359300

commit v4 on v3

--- a/solution.py
+++ b/solution.py
@@ -189,10 +189,11 @@
         bacc[...] += jnp.sum(back.reshape(-1, 8, D), axis=0)
 
     product(0)
+    product(1)
     for n in range(steps):
-        if n + 1 < steps:
-            product(n + 1)
         errors_of(n)
+        if n + 2 < steps:
+            product(n + 2)
 
     for n in range(2):
         rows = block(n, 4 * DOCS)

time: 117 us -> 117 us (level)
  no operation moved by 1% of the time
where the time goes in v4:
time: 117 us; the launch traced here: 116 us
  starting transfers between devices  40.7 us (35%)
  Pallas kernels  37.6 us (32%)
  waiting for transfers between devices  24 us (21%)
  blocking collectives  12.4 us (11%)
    pallas_call x1, Pallas kernels, gradients(): pl.pallas_call(main_kernel, in_specs=[vmem, vmem] + [hbm] * 14, out_specs...  21.2 us
    all_to_all x3, starting transfers between devices, exchange(): return lax.all_to_all(a, axes, split_axis=0, concat_axis=0, tiled=True)  20 us
    ppermute x6, waiting for transfers between devices, up(): return lax.ppermute(a, 'z', [(i, (i + 1) % 4) for i in range(4)])  17.1 us
    ppermute x6, starting transfers between devices, down(): return lax.ppermute(a, 'z', [(i, (i + 3) % 4) for i in range(4)])  16.2 us
    all_to_all x1, blocking collectives, exchange(): return lax.all_to_all(a, axes, split_axis=0, concat_axis=0, tiled=True)  12.4 us
    pallas_call x1, Pallas kernels, generate(): pl.pallas_call(gen_kernel, in_specs=[vmem, hbm, vmem, vmem, hbm], out_spe...  5.56 us
    ppermute x6, waiting for transfers between devices, down(): return lax.ppermute(a, 'z', [(i, (i + 3) % 4) for i in range(4)])  5.15 us
    pallas_call x1, Pallas kernels, weight_gradients(): pl.pallas_call(weight_kernel, in_specs=[vmem, vmem], out_specs=[pl.BlockS...  4.23 us
  transfers between devices with their start and end apart: 26, of which 6 were waited for; matrix products, arithmetic and copies ran while one was open for 0% of the time, Pallas kernels for 7%

profile of v4, /device:TPU:24, one launch (start us, length us, event | category | flops | bytes accessed | tf_op | source)
XLA Modules:
  0.0 115.8 jit_solution(12619415178943524506)
XLA Ops:
  0.6 0.0 copy-start.5
  0.6 5.6 %generate.1 = (bf16[64,768]{1,0:T(8,128)(2,1)}, bf16[256,768]{1,0:T(8,128)(2,1)}, bf16[256,768]{1,0:T(8,128)(2,1)}) custom-call(bf16[8,768]{1,0:T(8,128)(2,1)} %q_ref.3, bf16[768,4608]{1,0:T(8,128)(2,1)} %w_ref.1, bf16[6,768]{1,0:T(8,128)(2,1)} %bitcast.19, bf16[8,512]{1,0:T(8,128)(2,1)} %bitcast.20, bf16[512,768]{1,0:T(8,128)(2,1)} %refs_12_.1), custom_call_target="tpu_custom_call" | custom-call | flops 452984832 | bytes 7077888 | tf_op jit(solution)/shard_map/generate/pallas_call | solution.py:85
  6.2 5.3 %all-to-all-start = ((bf16[8,8,768]{2,1,0:T(8,128)(2,1)}), bf16[8,8,768]{2,1,0:T(8,128)(2,1)S(1)}, u32[]{:S(2)}, u32[]{:S(2)}) async-start(bf16[8,8,768]{2,1,0:T(8,128)(2,1)} %bitcast.18), calls=%async_computation | async-start | bytes 196608 | tf_op jit(solution)/shard_map/all_to_all | solution.py:389
  11.5 0.5 collective-permute-start.12
  12.0 2.8 %collective-permute-start.9 = (bf16[256,768]{1,0:T(8,128)(2,1)}, bf16[256,768]{1,0:T(8,128)(2,1)S(1)}, u32[]{:S(2)}, u32[]{:S(2)}) collective-permute-start(bf16[256,768]{1,0:T(8,128)(2,1)} %get-tuple-element.28), channel_id=1, source_target_pairs={{0,6},{2,0},{4,2},{6,4},{1,7},{3,1},{5,3},{7,5},{8,14},{10,8},{12,... | collective-permute-start | bytes 1179656 | tf_op jit(solution)/shard_map/ppermute | solution.py:381
  14.9 0.0 collective-permute-start
  14.9 3.2 %collective-permute-start.2 = (bf16[256,768]{1,0:T(8,128)(2,1)}, bf16[256,768]{1,0:T(8,128)(2,1)}, u32[]{:S(2)}, u32[]{:S(2)}) collective-permute-start(bf16[256,768]{1,0:T(8,128)(2,1)} %get-tuple-element.29), channel_id=1, source_target_pairs={{0,6},{2,0},{4,2},{6,4},{1,7},{3,1},{5,3},{7,5},{8,14},{10,8},{12,... | collective-permute-start | bytes 1179656 | tf_op jit(solution)/shard_map/ppermute | solution.py:381
  18.1 0.1 stack.35.src_ref
  18.2 0.0 all-to-all-done
  18.2 1.8 %assemble.1 = (bf16[16,296,128]{2,1,0:T(8,128)(2,1)}, f32[512,8]{1,0:T(8,128)S(1)}) custom-call(s32[8]{0:T(128)S(1)} %stack.35.src_ref, bf16[64,768]{1,0:T(8,128)(2,1)S(1)} %bitcast.15), custom_call_target="tpu_custom_call" | custom-call | tf_op jit(solution)/shard_map/assemble/pallas_call | solution.py:129
  20.0 7.3 %all-to-all-start.1 = ((bf16[16,296,128]{2,1,0:T(8,128)(2,1)}), bf16[16,296,128]{2,1,0:T(8,128)(2,1)}, u32[]{:S(2)}, u32[]{:S(2)}) async-start(bf16[16,296,128]{2,1,0:T(8,128)(2,1)} %get-tuple-element.27), calls=%async_computation.1 | async-start | bytes 2424832 | tf_op jit(solution)/shard_map/all_to_all | solution.py:389
  27.3 0.1 collective-permute-start.6
  27.4 0.0 collective-permute-done.9.refs_8_
  27.4 0.1 collective-permute-start.10
  27.5 0.0 collective-permute-done.refs_4_
  27.5 0.1 collective-permute-start.1
  27.6 5.1 %collective-permute-done.2.refs_9_ = bf16[256,768]{1,0:T(8,128)(2,1)} collective-permute-done((bf16[256,768]{1,0:T(8,128)(2,1)}, bf16[256,768]{1,0:T(8,128)(2,1)}, u32[]{:S(2)}, u32[]{:S(2)}) %collective-permute-start.2) | collective-permute-done | bytes 393248 | tf_op jit(solution)/shard_map/ppermute | solution.py:381
  32.7 3.5 %collective-permute-start.3 = (bf16[256,768]{1,0:T(8,128)(2,1)}, bf16[256,768]{1,0:T(8,128)(2,1)S(1)}, u32[]{:S(2)}, u32[]{:S(2)}) collective-permute-start(bf16[256,768]{1,0:T(8,128)(2,1)} %collective-permute-done.2.refs_9_), channel_id=1, source_target_pairs={{0,6},{2,0},{4,2},{6,4},{1,7},{3,1},{5,3},{7,5},{8,14},{10,8},{12,... | collective-permute-start | bytes 1179656 | tf_op jit(solution)/shard_map/ppermute | solution.py:381
  36.3 4.3 %collective-permute-done.6.refs_5_ = bf16[256,768]{1,0:T(8,128)(2,1)S(1)} collective-permute-done((bf16[256,768]{1,0:T(8,128)(2,1)S(1)}, bf16[256,768]{1,0:T(8,128)(2,1)S(1)}, u32[]{:S(2)}, u32[]{:S(2)}) %collective-permute-start.6) | collective-permute-done | bytes 393248 | tf_op jit(solution)/shard_map/ppermute | solution.py:377
  40.6 0.0 collective-permute-start.7
  40.6 0.0 collective-permute-done.12.refs_13_
  40.6 0.5 collective-permute-start.11
  41.1 0.0 collective-permute-done.10.refs_10_
  41.1 0.1 collective-permute-start.8
  41.2 5.8 %collective-permute-done.1.refs_0_ = bf16[256,768]{1,0:T(8,128)(2,1)S(1)} collective-permute-done((bf16[256,768]{1,0:T(8,128)(2,1)S(1)}, bf16[256,768]{1,0:T(8,128)(2,1)S(1)}, u32[]{:S(2)}, u32[]{:S(2)}) %collective-permute-start.1) | collective-permute-done | bytes 393248 | tf_op jit(solution)/shard_map/ppermute | solution.py:377
  47.0 0.0 collective-permute-start.4
  47.0 0.0 collective-permute-done.3.refs_1_
  47.0 0.5 collective-permute-start.5
  47.5 0.0 collective-permute-done.7.refs_6_
  47.6 0.0 collective-permute-done.8.refs_7_
  47.6 0.0 collective-permute-done.11.refs_11_
  47.6 1.2 %collective-permute-done.4.refs_2_ = bf16[256,768]{1,0:T(8,128)(2,1)S(1)} collective-permute-done((bf16[256,768]{1,0:T(8,128)(2,1)S(1)}, bf16[256,768]{1,0:T(8,128)(2,1)S(1)}, u32[]{:S(2)}, u32[]{:S(2)}) %collective-permute-start.4) | collective-permute-done | bytes 393248 | tf_op jit(solution)/shard_map/ppermute | solution.py:385
  48.8 0.6 collective-permute-done.5.refs_3_
  49.3 0.0 all-to-all-done.1.g_ref
  49.3 21.2 %gradients.1 = (bf16[512,768]{1,0:T(8,128)(2,1)}, bf16[512,768]{1,0:T(8,128)(2,1)}, bf16[512,768]{1,0:T(8,128)(2,1)}, bf16[512,768]{1,0:T(8,128)(2,1)}, bf16[512...) custom-call(f32[512,8]{1,0:T(8,128)S(1)} %get-tuple-element.26.tgt_r, ...), custom_call_target="tpu_custom_call" | custom-call | flops 14495514624 | bytes 12582912 | tf_op jit(solution)/shard_map/gradients/pallas_call | solution.py:230
  70.6 0.2 collective-permute-start.15
  70.8 7.4 %all-to-all-start.2 = ((bf16[16,296,128]{2,1,0:T(8,128)(2,1)}), bf16[16,296,128]{2,1,0:T(8,128)(2,1)S(1)}, u32[]{:S(2)}, u32[]{:S(2)}) async-start(bf16[16,296,128]{2,1,0:T(8,128)(2,1)} %get-tuple-element.44), calls=%async_computation.2 | async-start | bytes 2424832 | tf_op jit(solution)/shard_map/all_to_all | solution.py:389
  78.1 0.0 collective-permute-start.14
  78.1 0.5 collective-permute-start.17
  78.6 0.0 collective-permute-done.15.refs_1_.refs_3_
  78.7 0.2 shard_map.76
  78.9 0.1 collective-permute-start.16
  79.0 3.2 %collective-permute-start.18 = (bf16[256,768]{1,0:T(8,128)(2,1)S(1)}, bf16[256,768]{1,0:T(8,128)(2,1)S(1)}, u32[]{:S(2)}, u32[]{:S(2)}) collective-permute-start(bf16[256,768]{1,0:T(8,128)(2,1)S(1)} %get-tuple-element.39), channel_id=1, source_target_pairs={{0,6},{2,0},{4,2},{6,4},{1,7},{3,1},{5,3},{7,5},{8,14},{10,8},{12,... | collective-permute-start | bytes 1179656 | tf_op jit(solution)/shard_map/ppermute | solution.py:381
  82.2 0.0 collective-permute-start.13
  82.2 0.0 collective-permute-done.14.refs_1_
  82.2 0.0 collective-permute-done.17.refs_4_.refs_3_
  82.2 1.0 shard_map.78
  83.2 0.1 collective-permute-start.20
  83.3 1.9 %collective-permute-start.21 = (bf16[256,768]{1,0:T(8,128)(2,1)}, bf16[256,768]{1,0:T(8,128)(2,1)S(1)}, u32[]{:S(2)}, u32[]{:S(2)}) collective-permute-start(bf16[256,768]{1,0:T(8,128)(2,1)} %get-tuple-element.42), channel_id=1, source_target_pairs={{0,2},{2,4},{4,6},{6,0},{1,3},{3,5},{5,7},{7,1},{8,10},{10,12},{12... | collective-permute-start | bytes 1179656 | tf_op jit(solution)/shard_map/ppermute | solution.py:377
  85.2 6.9 %collective-permute-done.16.refs_2_ = bf16[256,768]{1,0:T(8,128)(2,1)S(1)} collective-permute-done((bf16[256,768]{1,0:T(8,128)(2,1)S(1)}, bf16[256,768]{1,0:T(8,128)(2,1)S(1)}, u32[]{:S(2)}, u32[]{:S(2)}) %collective-permute-start.16) | collective-permute-done | bytes 393248 | tf_op jit(solution)/shard_map/ppermute | solution.py:377
  92.2 0.0 collective-permute-done.18.refs_5_
  92.2 1.0 shard_map.77
  93.2 0.0 collective-permute-start.19
  93.2 3.3 %collective-permute-start.22 = (bf16[256,768]{1,0:T(8,128)(2,1)}, bf16[256,768]{1,0:T(8,128)(2,1)}, u32[]{:S(2)}, u32[]{:S(2)}) collective-permute-start(bf16[256,768]{1,0:T(8,128)(2,1)} %get-tuple-element.43), channel_id=1, source_target_pairs={{0,6},{2,0},{4,2},{6,4},{1,7},{3,1},{5,3},{7,5},{8,14},{10,8},{12,... | collective-permute-start | bytes 1179656 | tf_op jit(solution)/shard_map/ppermute | solution.py:381
  96.4 0.0 all-to-all-done.2.y_ref
  96.4 0.3 reduced.1
  96.8 12.4 %all_to_all.32 = bf16[8,8,768]{2,1,0:T(8,128)(2,1)S(1)} all-to-all(bf16[8,8,768]{2,1,0:T(8,128)(2,1)S(1)} %bitcast.16), channel_id=1, replica_groups=mesh['xl'=2,'xh'=2,'y'=4,'z'=4,'c'=2] {'z','c'}, dimensions={0} | all-to-all | bytes 196608 | tf_op jit(solution)/shard_map/all_to_all | solution.py:389
  109.2 4.2 %weight_gradients.1 = (bf16[768,4608]{1,0:T(8,128)(2,1)}, bf16[6,768]{1,0:T(8,128)(2,1)}) custom-call(bf16[8,768]{1,0:T(8,128)(2,1)S(1)} %copy-done.4, bf16[64,768]{1,0:T(8,128)(2,1)S(1)} %bitcast.17), custom_call_target="tpu_custom_call" | custom-call | flops 452984832 | bytes 7077888 | tf_op jit(solution)/shard_map/weight_gradients/pallas_call | solution.py:307
  113.4 0.0 collective-permute-done.13.other_ref
  113.4 0.0 collective-permute-done.20.dl_ref
  113.5 0.0 collective-permute-done.21.uh_ref
  113.5 0.0 collective-permute-done.19.ul_ref
  113.5 0.0 collective-permute-done.22.dh_ref
  113.5 2.3 %document_sum.1 = bf16[512,768]{1,0:T(8,128)(2,1)} custom-call(bf16[512,768]{1,0:T(8,128)(2,1)S(1)} %copy-done.3, bf16[512,768]{1,0:T(8,128)(2,1)S(1)} %collective-permute-done.13.other_ref, bf16[256,768]{1,0:T(8,128)(2,1)S(1)} %collective-permute-done.19.ul_ref, bf16[256,768]{1,0:T(8,128)(2,1)S(1)} %collective-permute-done.20.dl_ref, ...), custom_call_target="tpu_custom_call" | custom-call | flops 1572864 | bytes 3932160 | tf_op jit(solution)/shard_map/document_sum/pallas_call | solution.py:365
  (21 shorter events, 0.0 us)
Async XLA Ops:
  0.6 10.9 %copy-start.5 = (bf16[512,768]{1,0:T(8,128)(2,1)S(1)}, bf16[512,768]{1,0:T(8,128)(2,1)}, u32[]{:S(2)}) copy-start(bf16[512,768]{1,0:T(8,128)(2,1)} %refs_12_.1) | copy-start | bytes 2359300
  6.2 12.0 %all-to-all-start = ((bf16[8,8,768]{2,1,0:T(8,128)(2,1)}), bf16[8,8,768]{2,1,0:T(8,128)(2,1)S(1)}, u32[]{:S(2)}, u32[]{:S(2)}) async-start(bf16[8,8,768]{2,1,0:T(8,128)(2,1)} %bitcast.18), calls=%async_computation | async-start | bytes 196608 | tf_op jit(solution)/shard_map/all_to_all | solution.py:389
  11.5 29.0 %collective-permute-start.12 = (bf16[512,768]{1,0:T(8,128)(2,1)S(1)}, bf16[512,768]{1,0:T(8,128)(2,1)}, u32[]{:S(2)}, u32[]{:S(2)}) collective-permute-start(bf16[512,768]{1,0:T(8,128)(2,1)S(1)} %copy-done.5), channel_id=1, source_target_pairs={{0,1},{1,0},{2,3},{3,2},{4,5},{5,4},{6,7},{7,6},{8,9},{9,8},{10,11... | collective-permute-start | bytes 2359304 | tf_op jit(solution)/shard_map/ppermute | solution.py:385
  12.0 15.4 %collective-permute-start.9 = (bf16[256,768]{1,0:T(8,128)(2,1)}, bf16[256,768]{1,0:T(8,128)(2,1)S(1)}, u32[]{:S(2)}, u32[]{:S(2)}) collective-permute-start(bf16[256,768]{1,0:T(8,128)(2,1)} %get-tuple-element.28), channel_id=1, source_target_pairs={{0,6},{2,0},{4,2},{6,4},{1,7},{3,1},{5,3},{7,5},{8,14},{10,8},{12,... | collective-permute-start | bytes 1179656 | tf_op jit(solution)/shard_map/ppermute | solution.py:381
  14.9 12.6 %collective-permute-start = (bf16[256,768]{1,0:T(8,128)(2,1)}, bf16[256,768]{1,0:T(8,128)(2,1)S(1)}, u32[]{:S(2)}, u32[]{:S(2)}) collective-permute-start(bf16[256,768]{1,0:T(8,128)(2,1)} %get-tuple-element.28), channel_id=1, source_target_pairs={{0,2},{2,4},{4,6},{6,0},{1,3},{3,5},{5,7},{7,1},{8,10},{10,12},{12... | collective-permute-start | bytes 1179656 | tf_op jit(solution)/shard_map/ppermute | solution.py:377
  14.9 17.8 %collective-permute-start.2 = (bf16[256,768]{1,0:T(8,128)(2,1)}, bf16[256,768]{1,0:T(8,128)(2,1)}, u32[]{:S(2)}, u32[]{:S(2)}) collective-permute-start(bf16[256,768]{1,0:T(8,128)(2,1)} %get-tuple-element.29), channel_id=1, source_target_pairs={{0,6},{2,0},{4,2},{6,4},{1,7},{3,1},{5,3},{7,5},{8,14},{10,8},{12,... | collective-permute-start | bytes 1179656 | tf_op jit(solution)/shard_map/ppermute | solution.py:381
  20.0 7.3 %copy-start.7 = (bf16[256,768]{1,0:T(8,128)(2,1)S(1)}, bf16[256,768]{1,0:T(8,128)(2,1)}, u32[]{:S(2)}) copy-start(bf16[256,768]{1,0:T(8,128)(2,1)} %get-tuple-element.29) | copy-start | bytes 1179652
  20.0 29.3 %all-to-all-start.1 = ((bf16[16,296,128]{2,1,0:T(8,128)(2,1)}), bf16[16,296,128]{2,1,0:T(8,128)(2,1)}, u32[]{:S(2)}, u32[]{:S(2)}) async-start(bf16[16,296,128]{2,1,0:T(8,128)(2,1)} %get-tuple-element.27), calls=%async_computation.1 | async-start | bytes 2424832 | tf_op jit(solution)/shard_map/all_to_all | solution.py:389
  27.3 13.3 %collective-permute-start.6 = (bf16[256,768]{1,0:T(8,128)(2,1)S(1)}, bf16[256,768]{1,0:T(8,128)(2,1)S(1)}, u32[]{:S(2)}, u32[]{:S(2)}) collective-permute-start(bf16[256,768]{1,0:T(8,128)(2,1)S(1)} %copy-done.7), channel_id=1, source_target_pairs={{0,2},{2,4},{4,6},{6,0},{1,3},{3,5},{5,7},{7,1},{8,10},{10,12},{12... | collective-permute-start | bytes 1179656 | tf_op jit(solution)/shard_map/ppermute | solution.py:377
  27.4 21.9 %copy-start.6 = (bf16[256,768]{1,0:T(8,128)(2,1)}, bf16[256,768]{1,0:T(8,128)(2,1)S(1)}, u32[]{:S(2)}) copy-start(bf16[256,768]{1,0:T(8,128)(2,1)S(1)} %collective-permute-done.9.refs_8_) | copy-start | bytes 1179652
  27.4 13.7 %collective-permute-start.10 = (bf16[256,768]{1,0:T(8,128)(2,1)S(1)}, bf16[256,768]{1,0:T(8,128)(2,1)S(1)}, u32[]{:S(2)}, u32[]{:S(2)}) collective-permute-start(bf16[256,768]{1,0:T(8,128)(2,1)S(1)} %collective-permute-done.9.refs_8_), channel_id=1, source_target_pairs={{0,1},{1,0},{2,3},{3,2},{4,5},{5,4},{6,7},{7,6},{8,9},{9,8},{10,11... | collective-permute-start | bytes 1179656 | tf_op jit(solution)/shard_map/ppermute | solution.py:385
  27.5 19.5 %collective-permute-start.1 = (bf16[256,768]{1,0:T(8,128)(2,1)S(1)}, bf16[256,768]{1,0:T(8,128)(2,1)S(1)}, u32[]{:S(2)}, u32[]{:S(2)}) collective-permute-start(bf16[256,768]{1,0:T(8,128)(2,1)S(1)} %collective-permute-done.refs_4_), channel_id=1, source_target_pairs={{0,2},{2,4},{4,6},{6,0},{1,3},{3,5},{5,7},{7,1},{8,10},{10,12},{12... | collective-permute-start | bytes 1179656 | tf_op jit(solution)/shard_map/ppermute | solution.py:377
  32.7 14.3 %collective-permute-start.3 = (bf16[256,768]{1,0:T(8,128)(2,1)}, bf16[256,768]{1,0:T(8,128)(2,1)S(1)}, u32[]{:S(2)}, u32[]{:S(2)}) collective-permute-start(bf16[256,768]{1,0:T(8,128)(2,1)} %collective-permute-done.2.refs_9_), channel_id=1, source_target_pairs={{0,6},{2,0},{4,2},{6,4},{1,7},{3,1},{5,3},{7,5},{8,14},{10,8},{12,... | collective-permute-start | bytes 1179656 | tf_op jit(solution)/shard_map/ppermute | solution.py:381
  40.6 7.0 %collective-permute-start.7 = (bf16[256,768]{1,0:T(8,128)(2,1)S(1)}, bf16[256,768]{1,0:T(8,128)(2,1)S(1)}, u32[]{:S(2)}, u32[]{:S(2)}) collective-permute-start(bf16[256,768]{1,0:T(8,128)(2,1)S(1)} %collective-permute-done.refs_4_), channel_id=1, source_target_pairs={{0,1},{1,0},{2,3},{3,2},{4,5},{5,4},{6,7},{7,6},{8,9},{9,8},{10,11... | collective-permute-start | bytes 1179656 | tf_op jit(solution)/shard_map/ppermute | solution.py:385
  40.6 7.0 %collective-permute-start.11 = (bf16[256,768]{1,0:T(8,128)(2,1)}, bf16[256,768]{1,0:T(8,128)(2,1)S(1)}, u32[]{:S(2)}, u32[]{:S(2)}) collective-permute-start(bf16[256,768]{1,0:T(8,128)(2,1)} %collective-permute-done.2.refs_9_), channel_id=1, source_target_pairs={{0,1},{1,0},{2,3},{3,2},{4,5},{5,4},{6,7},{7,6},{8,9},{9,8},{10,11... | collective-permute-start | bytes 1179656 | tf_op jit(solution)/shard_map/ppermute | solution.py:385
  41.1 7.7 %copy-start.8 = (bf16[256,768]{1,0:T(8,128)(2,1)}, bf16[256,768]{1,0:T(8,128)(2,1)S(1)}, u32[]{:S(2)}) copy-start(bf16[256,768]{1,0:T(8,128)(2,1)S(1)} %collective-permute-done.10.refs_10_) | copy-start | bytes 1179652
  41.1 6.5 %collective-permute-start.8 = (bf16[256,768]{1,0:T(8,128)(2,1)S(1)}, bf16[256,768]{1,0:T(8,128)(2,1)S(1)}, u32[]{:S(2)}, u32[]{:S(2)}) collective-permute-start(bf16[256,768]{1,0:T(8,128)(2,1)S(1)} %collective-permute-done.6.refs_5_), channel_id=1, source_target_pairs={{0,1},{1,0},{2,3},{3,2},{4,5},{5,4},{6,7},{7,6},{8,9},{9,8},{10,11... | collective-permute-start | bytes 1179656 | tf_op jit(solution)/shard_map/ppermute | solution.py:385
  47.0 1.7 %collective-permute-start.4 = (bf16[256,768]{1,0:T(8,128)(2,1)S(1)}, bf16[256,768]{1,0:T(8,128)(2,1)S(1)}, u32[]{:S(2)}, u32[]{:S(2)}) collective-permute-start(bf16[256,768]{1,0:T(8,128)(2,1)S(1)} %collective-permute-done.1.refs_0_), channel_id=1, source_target_pairs={{0,1},{1,0},{2,3},{3,2},{4,5},{5,4},{6,7},{7,6},{8,9},{9,8},{10,11... | collective-permute-start | bytes 1179656 | tf_op jit(solution)/shard_map/ppermute | solution.py:385
  47.0 2.3 %collective-permute-start.5 = (bf16[256,768]{1,0:T(8,128)(2,1)S(1)}, bf16[256,768]{1,0:T(8,128)(2,1)S(1)}, u32[]{:S(2)}, u32[]{:S(2)}) collective-permute-start(bf16[256,768]{1,0:T(8,128)(2,1)S(1)} %collective-permute-done.3.refs_1_), channel_id=1, source_target_pairs={{0,1},{1,0},{2,3},{3,2},{4,5},{5,4},{6,7},{7,6},{8,9},{9,8},{10,11... | collective-permute-start | bytes 1179656 | tf_op jit(solution)/shard_map/ppermute | solution.py:385
  47.6 1.2 %copy-start.10 = (bf16[256,768]{1,0:T(8,128)(2,1)}, bf16[256,768]{1,0:T(8,128)(2,1)S(1)}, u32[]{:S(2)}) copy-start(bf16[256,768]{1,0:T(8,128)(2,1)S(1)} %collective-permute-done.8.refs_7_) | copy-start | bytes 1179652
  47.6 1.2 %copy-start.9 = (bf16[256,768]{1,0:T(8,128)(2,1)}, bf16[256,768]{1,0:T(8,128)(2,1)S(1)}, u32[]{:S(2)}) copy-start(bf16[256,768]{1,0:T(8,128)(2,1)S(1)} %collective-permute-done.11.refs_11_) | copy-start | bytes 1179652
  70.6 8.1 %collective-permute-start.15 = (bf16[512,768]{1,0:T(8,128)(2,1)}, bf16[512,768]{1,0:T(8,128)(2,1)S(1)}, u32[]{:S(2)}, u32[]{:S(2)}) collective-permute-start(bf16[512,768]{1,0:T(8,128)(2,1)} %get-tuple-element.35), channel_id=1, source_target_pairs={{0,1},{1,0},{2,3},{3,2},{4,5},{5,4},{6,7},{7,6},{8,9},{9,8},{10,11... | collective-permute-start | bytes 2359304 | tf_op jit(solution)/shard_map/ppermute | solution.py:385
  70.8 7.9 %copy-start = (bf16[512,768]{1,0:T(8,128)(2,1)S(1)}, bf16[512,768]{1,0:T(8,128)(2,1)}, u32[]{:S(2)}) copy-start(bf16[512,768]{1,0:T(8,128)(2,1)} %get-tuple-element.34.refs_0_.refs_2_) | copy-start | bytes 2359300
  70.8 25.6 %all-to-all-start.2 = ((bf16[16,296,128]{2,1,0:T(8,128)(2,1)}), bf16[16,296,128]{2,1,0:T(8,128)(2,1)S(1)}, u32[]{:S(2)}, u32[]{:S(2)}) async-start(bf16[16,296,128]{2,1,0:T(8,128)(2,1)} %get-tuple-element.44), calls=%async_computation.2 | async-start | bytes 2424832 | tf_op jit(solution)/shard_map/all_to_all | solution.py:389
  78.1 4.1 %collective-permute-start.14 = (bf16[512,768]{1,0:T(8,128)(2,1)}, bf16[512,768]{1,0:T(8,128)(2,1)S(1)}, u32[]{:S(2)}, u32[]{:S(2)}) collective-permute-start(bf16[512,768]{1,0:T(8,128)(2,1)} %get-tuple-element.33), channel_id=1, source_target_pairs={{0,1},{1,0},{2,3},{3,2},{4,5},{5,4},{6,7},{7,6},{8,9},{9,8},{10,11... | collective-permute-start | bytes 2359304 | tf_op jit(solution)/shard_map/ppermute | solution.py:385
  78.1 4.1 %collective-permute-start.17 = (bf16[512,768]{1,0:T(8,128)(2,1)}, bf16[512,768]{1,0:T(8,128)(2,1)S(1)}, u32[]{:S(2)}, u32[]{:S(2)}) collective-permute-start(bf16[512,768]{1,0:T(8,128)(2,1)} %get-tuple-element.38), channel_id=1, source_target_pairs={{0,1},{1,0},{2,3},{3,2},{4,5},{5,4},{6,7},{7,6},{8,9},{9,8},{10,11... | collective-permute-start | bytes 2359304 | tf_op jit(solution)/shard_map/ppermute | solution.py:385
  78.7 3.6 %copy-start.1 = (bf16[512,768]{1,0:T(8,128)(2,1)S(1)}, bf16[512,768]{1,0:T(8,128)(2,1)}, u32[]{:S(2)}) copy-start(bf16[512,768]{1,0:T(8,128)(2,1)} %get-tuple-element.37.refs_3_.refs_2_) | copy-start | bytes 2359300
  78.7 3.6 %copy-start.2 = (bf16[512,768]{1,0:T(8,128)(2,1)S(1)}, bf16[512,768]{1,0:T(8,128)(2,1)}, u32[]{:S(2)}) copy-start(bf16[512,768]{1,0:T(8,128)(2,1)} %get-tuple-element.32.refs_0_) | copy-start | bytes 2359300
  78.9 13.3 %collective-permute-start.16 = (bf16[256,768]{1,0:T(8,128)(2,1)S(1)}, bf16[256,768]{1,0:T(8,128)(2,1)S(1)}, u32[]{:S(2)}, u32[]{:S(2)}) collective-permute-start(bf16[256,768]{1,0:T(8,128)(2,1)S(1)} %get-tuple-element.36), channel_id=1, source_target_pairs={{0,2},{2,4},{4,6},{6,0},{1,3},{3,5},{5,7},{7,1},{8,10},{10,12},{12... | collective-permute-start | bytes 1179656 | tf_op jit(solution)/shard_map/ppermute | solution.py:377
  79.0 13.2 %collective-permute-start.18 = (bf16[256,768]{1,0:T(8,128)(2,1)S(1)}, bf16[256,768]{1,0:T(8,128)(2,1)S(1)}, u32[]{:S(2)}, u32[]{:S(2)}) collective-permute-start(bf16[256,768]{1,0:T(8,128)(2,1)S(1)} %get-tuple-element.39), channel_id=1, source_target_pairs={{0,6},{2,0},{4,2},{6,4},{1,7},{3,1},{5,3},{7,5},{8,14},{10,8},{12,... | collective-permute-start | bytes 1179656 | tf_op jit(solution)/shard_map/ppermute | solution.py:381
  82.2 31.2 %collective-permute-start.13 = (bf16[512,768]{1,0:T(8,128)(2,1)}, bf16[512,768]{1,0:T(8,128)(2,1)S(1)}, u32[]{:S(2)}, u32[]{:S(2)}) collective-permute-start(bf16[512,768]{1,0:T(8,128)(2,1)} %get-tuple-element.31), channel_id=1, source_target_pairs={{0,1},{1,0},{2,3},{3,2},{4,5},{5,4},{6,7},{7,6},{8,9},{9,8},{10,11... | collective-permute-start | bytes 2359304 | tf_op jit(solution)/shard_map/ppermute | solution.py:385
  83.2 30.2 %collective-permute-start.20 = (bf16[256,768]{1,0:T(8,128)(2,1)}, bf16[256,768]{1,0:T(8,128)(2,1)S(1)}, u32[]{:S(2)}, u32[]{:S(2)}) collective-permute-start(bf16[256,768]{1,0:T(8,128)(2,1)} %get-tuple-element.41), channel_id=1, source_target_pairs={{0,6},{2,0},{4,2},{6,4},{1,7},{3,1},{5,3},{7,5},{8,14},{10,8},{12,... | collective-permute-start | bytes 1179656 | tf_op jit(solution)/shard_map/ppermute | solution.py:381
  83.3 30.2 %collective-permute-start.21 = (bf16[256,768]{1,0:T(8,128)(2,1)}, bf16[256,768]{1,0:T(8,128)(2,1)S(1)}, u32[]{:S(2)}, u32[]{:S(2)}) collective-permute-start(bf16[256,768]{1,0:T(8,128)(2,1)} %get-tuple-element.42), channel_id=1, source_target_pairs={{0,2},{2,4},{4,6},{6,0},{1,3},{3,5},{5,7},{7,1},{8,10},{10,12},{12... | collective-permute-start | bytes 1179656 | tf_op jit(solution)/shard_map/ppermute | solution.py:377
  93.2 16.0 %copy-start.4 = (bf16[8,768]{1,0:T(8,128)(2,1)S(1)}, bf16[8,768]{1,0:T(8,128)(2,1)}, u32[]{:S(2)}) copy-start(bf16[8,768]{1,0:T(8,128)(2,1)} %q_ref.3) | copy-start | bytes 36868
  93.2 20.3 %collective-permute-start.19 = (bf16[256,768]{1,0:T(8,128)(2,1)}, bf16[256,768]{1,0:T(8,128)(2,1)S(1)}, u32[]{:S(2)}, u32[]{:S(2)}) collective-permute-start(bf16[256,768]{1,0:T(8,128)(2,1)} %get-tuple-element.40), channel_id=1, source_target_pairs={{0,2},{2,4},{4,6},{6,0},{1,3},{3,5},{5,7},{7,1},{8,10},{10,12},{12... | collective-permute-start | bytes 1179656 | tf_op jit(solution)/shard_map/ppermute | solution.py:377
  93.2 20.3 %collective-permute-start.22 = (bf16[256,768]{1,0:T(8,128)(2,1)}, bf16[256,768]{1,0:T(8,128)(2,1)}, u32[]{:S(2)}, u32[]{:S(2)}) collective-permute-start(bf16[256,768]{1,0:T(8,128)(2,1)} %get-tuple-element.43), channel_id=1, source_target_pairs={{0,6},{2,0},{4,2},{6,4},{1,7},{3,1},{5,3},{7,5},{8,14},{10,8},{12,... | collective-permute-start | bytes 1179656 | tf_op jit(solution)/shard_map/ppermute | solution.py:381
  96.7 16.7 %copy-start.3 = (bf16[512,768]{1,0:T(8,128)(2,1)S(1)}, bf16[512,768]{1,0:T(8,128)(2,1)}, u32[]{:S(2)}) copy-start(bf16[512,768]{1,0:T(8,128)(2,1)} %get-tuple-element.30.mine_ref) | copy-start | bytes 2359300
